TPU v7x, 32 devices: a whole 2x2x4 slice. The times are simulated.
32 devices in a mesh: seq: 4 (over z), ctx: 8 (over y, x, core).
Axes of the slice: x: 2, y: 2, z: 4, core: 2. Of those that a mesh axis runs over, the one named last changes fastest.
Arguments:
- inputs: bfloat16 [2, 4, 512, 1536], P(None, 'seq', 'ctx'), may hold values from -6 to 6
- out_grad: bfloat16 [2, 4, 512, 1536], P(None, 'seq', 'ctx'), may hold values from -6 to 6
- pair_index: int32 [2, 8], replicated, may hold values from 0 to 7, each once within a row
- norm_gain: bfloat16 [1536], P(('seq', 'ctx')), may hold values from 0.5 to 1.5
- query_weight: bfloat16 [1536, 1536], P(('seq', 'ctx')), may hold values from -0.15625 to 0.15625
- key_weight: bfloat16 [1536, 1536], P(('seq', 'ctx')), may hold values from -0.15625 to 0.15625
- value_weight: bfloat16 [1536, 1536], P(('seq', 'ctx')), may hold values from -0.15625 to 0.15625
- score_kernel: float32 [16, 6, 11], replicated, may hold values from -1 to 1
- head_mixing: float32 [16, 2], replicated, may hold values from 0.3 to 1
- group_gain: bfloat16 [1536], P(('seq', 'ctx')), may hold values from 0.5 to 1.5
- output_weight: bfloat16 [1536, 1536], P(('seq', 'ctx')), may hold values from -0.15625 to 0.15625
- second_gain: bfloat16 [1536], P(('seq', 'ctx')), may hold values from 0.5 to 1.5
- gate_weight: bfloat16 [1536, 4096], P(('seq', 'ctx')), may hold values from -0.15625 to 0.15625
- up_weight: bfloat16 [1536, 4096], P(('seq', 'ctx')), may hold values from -0.15625 to 0.15625
- down_weight: bfloat16 [4096, 1536], P(('seq', 'ctx')), may hold values from -0.09375 to 0.09375
Outputs:
- layer_out: bfloat16 [2, 4, 512, 1536], P(None, 'seq', 'ctx')
- input_grad: bfloat16 [2, 4, 512, 1536], P(None, 'seq', 'ctx')
- norm_gain_grad: float32 [1536], P(('seq', 'ctx'))
- query_weight_grad: float32 [1536, 1536], P(('seq', 'ctx'))
- key_weight_grad: float32 [1536, 1536], P(('seq', 'ctx'))
- value_weight_grad: float32 [1536, 1536], P(('seq', 'ctx'))
- score_kernel_grad: float32 [16, 6, 11], replicated
- head_mixing_grad: float32 [16, 2], replicated
- group_gain_grad: float32 [1536], P(('seq', 'ctx'))
- output_weight_grad: float32 [1536, 1536], P(('seq', 'ctx'))
- second_gain_grad: float32 [1536], P(('seq', 'ctx'))
- gate_weight_grad: float32 [1536, 4096], P(('seq', 'ctx'))
- up_weight_grad: float32 [1536, 4096], P(('seq', 'ctx'))
- down_weight_grad: float32 [4096, 1536], P(('seq', 'ctx'))
Inputs may be any that keep to these rules, and one draw needn't show every extreme that they name: `pair_index`: each row names every number of 0 to 7 once.
All inputs are finite; a program needn't handle non-finite values.
Results may differ from a plain program's by a relative error of at most 0.025.
Values may be sent and summed in bfloat16 or wider, within the bound.
A program may use at most 320 MiB of HBM per device.

v0:
```python
import jax
import jax.numpy as jnp
from jax import lax
from jax.sharding import PartitionSpec as P

EPSILON = 1e-05
NEGATIVE = -1e30
PRECISE = lax.Precision.HIGHEST


def normalize(values):
    factor = lax.rsqrt(jnp.mean(values * values, axis=-1, keepdims=True) + EPSILON)
    return (values * factor, factor)


def normalize_back(normed, factor, gain, upstream):
    gain_grad = jnp.sum(upstream * normed, axis=0)
    scaled = upstream * gain
    return (
        factor * (scaled - normed * jnp.mean(scaled * normed, axis=-1, keepdims=True)),
        gain_grad,
    )


def add_rows(target, update, offset):
    current = lax.dynamic_slice_in_dim(target, offset, update.shape[0], 0)
    return lax.dynamic_update_slice_in_dim(target, current + update, offset, 0)


def masked_scores(query_ext, key_pad, offset, row_pos, layout):
    block_rows, halo_rows, key_reach, key_block, groups, score_scale = layout
    extent = key_block + 4 * key_reach
    key_slab = lax.dynamic_slice_in_dim(key_pad, offset, extent, 0)
    raw_scores = (
        jnp.einsum("nrhd,khd->nhrk", query_ext, key_slab, preferred_element_type=jnp.float32)
        * score_scale
    )
    key_pos = offset - 2 * key_reach + jnp.arange(extent, dtype=jnp.int32)
    keep_mask = (key_pos[None, None, :] <= row_pos[:, :, None]) & (key_pos >= 0)[None, None, :]
    return jnp.where(keep_mask[:, None], raw_scores, 0.0)


def convolve(zeroed, kernel, shift, extent, layout):
    block_rows, halo_rows, key_reach = (layout[0], layout[1], layout[2])
    result = jnp.zeros(zeroed.shape[:2] + (block_rows, extent), jnp.float32)
    for row_tap in range(halo_rows + 1):
        for key_tap in range(2 * key_reach + 1):
            column = shift + 3 * key_reach - key_tap
            result = (
                result
                + kernel[:, row_tap, key_tap][None, :, None, None]
                * zeroed[
                    :,
                    :,
                    halo_rows - row_tap : halo_rows - row_tap + block_rows,
                    column : column + extent,
                ]
            )
    return result


def attend_forward(query_ext, row_pos, key_pad, value_pad, kernel, layout):
    block_rows, halo_rows, key_reach, key_block, groups, score_scale = layout
    members = query_ext.shape[0]
    head_count = query_ext.shape[2]
    pair_width = value_pad.shape[1] // groups
    block_count = jnp.max(row_pos) // key_block + 1

    def advance(position, carried):
        running_max, running_sum, gathered = carried
        offset = position * key_block
        zeroed = masked_scores(query_ext, key_pad, offset, row_pos, layout)
        logits = convolve(zeroed, kernel, 0, key_block, layout)
        key_pos = offset + jnp.arange(key_block, dtype=jnp.int32)
        valid_mask = key_pos[None, None, :] <= row_pos[:, halo_rows:, None]
        logits = jnp.where(valid_mask[:, None], logits, NEGATIVE)
        new_max = jnp.maximum(running_max, jnp.max(logits, axis=-1))
        shrink = jnp.exp(running_max - new_max)
        weights = jnp.exp(logits - new_max[..., None])
        running_sum = running_sum * shrink + jnp.sum(weights, axis=-1)
        value_slab = lax.dynamic_slice_in_dim(
            value_pad, offset + 2 * key_reach, key_block, 0
        ).reshape(key_block, groups, pair_width)
        low_weights = weights.astype(jnp.bfloat16).reshape(
            members, groups, 2, block_rows, key_block
        )
        gathered = gathered * shrink.reshape(members, groups, 2, block_rows, 1) + jnp.einsum(
            "ngpik,kgc->ngpic", low_weights, value_slab, preferred_element_type=jnp.float32
        )
        return (new_max, running_sum, gathered)

    initial = (
        jnp.full((members, head_count, block_rows), NEGATIVE, jnp.float32),
        jnp.zeros((members, head_count, block_rows), jnp.float32),
        jnp.zeros((members, groups, 2, block_rows, pair_width), jnp.float32),
    )
    running_max, running_sum, gathered = lax.fori_loop(0, block_count, advance, initial)
    mixed_in = gathered / running_sum.reshape(members, groups, 2, block_rows, 1)
    return (mixed_in, running_max + jnp.log(running_sum))


def attend_backward(
    query_ext,
    row_pos,
    key_pad,
    value_pad,
    kernel,
    log_total,
    mixed_low,
    delta_rows,
    key_acc,
    value_acc,
    layout,
):
    block_rows, halo_rows, key_reach, key_block, groups, score_scale = layout
    members = query_ext.shape[0]
    ext_rows = query_ext.shape[1]
    head_count = query_ext.shape[2]
    model_width = value_pad.shape[1]
    pair_width = model_width // groups
    extent = key_block + 2 * key_reach
    block_count = jnp.max(row_pos) // key_block + 1

    def advance(position, carried):
        query_grad, key_acc, value_acc, kernel_grad = carried
        offset = position * key_block
        zeroed = masked_scores(query_ext, key_pad, offset, row_pos, layout)
        logits = convolve(zeroed, kernel, -key_reach, extent, layout)
        key_pos = offset - key_reach + jnp.arange(extent, dtype=jnp.int32)
        valid_mask = (key_pos[None, None, :] <= row_pos[:, halo_rows:, None]) & (key_pos >= 0)[
            None, None, :
        ]
        probability = jnp.where(valid_mask[:, None], jnp.exp(logits - log_total[..., None]), 0.0)
        value_slab = lax.dynamic_slice_in_dim(value_pad, offset + key_reach, extent, 0).reshape(
            extent, groups, pair_width
        )
        prob_grad = jnp.einsum(
            "ngpic,kgc->ngpik", mixed_low, value_slab, preferred_element_type=jnp.float32
        ).reshape(members, head_count, block_rows, extent)
        logit_grad = probability * (prob_grad - delta_rows[..., None])
        central = (
            probability[..., key_reach : key_reach + key_block]
            .astype(jnp.bfloat16)
            .reshape(members, groups, 2, block_rows, key_block)
        )
        value_part = jnp.einsum(
            "ngpik,ngpic->kgc", central, mixed_low, preferred_element_type=jnp.float32
        ).reshape(key_block, model_width)
        value_acc = add_rows(value_acc, value_part, offset)
        middle = logit_grad[..., key_reach : key_reach + key_block]
        tap_sums = []
        for row_tap in range(halo_rows + 1):
            for key_tap in range(2 * key_reach + 1):
                column = 3 * key_reach - key_tap
                tap_sums.append(
                    jnp.sum(
                        middle
                        * zeroed[
                            :,
                            :,
                            halo_rows - row_tap : halo_rows - row_tap + block_rows,
                            column : column + key_block,
                        ],
                        axis=(0, 2, 3),
                    )
                )
        kernel_grad = kernel_grad + jnp.stack(tap_sums, axis=1).reshape(
            head_count, halo_rows + 1, 2 * key_reach + 1
        )
        padded = jnp.pad(logit_grad, ((0, 0), (0, 0), (halo_rows, halo_rows), (0, 0)))
        score_grad = jnp.zeros((members, head_count, ext_rows, key_block), jnp.float32)
        for row_tap in range(halo_rows + 1):
            for key_tap in range(2 * key_reach + 1):
                score_grad = (
                    score_grad
                    + kernel[:, row_tap, key_tap][None, :, None, None]
                    * padded[:, :, row_tap : row_tap + ext_rows, key_tap : key_tap + key_block]
                )
        key_central = offset + jnp.arange(key_block, dtype=jnp.int32)
        keep_mask = (key_central[None, None, :] <= row_pos[:, :, None]) & (key_central >= 0)[
            None, None, :
        ]
        score_low = jnp.where(keep_mask[:, None], score_grad, 0.0).astype(jnp.bfloat16)
        key_slab = lax.dynamic_slice_in_dim(key_pad, offset + 2 * key_reach, key_block, 0)
        query_grad = (
            query_grad
            + jnp.einsum("nhrk,khd->nrhd", score_low, key_slab, preferred_element_type=jnp.float32)
            * score_scale
        )
        key_part = (
            jnp.einsum(
                "nhrk,nrhd->khd", score_low, query_ext, preferred_element_type=jnp.float32
            ).reshape(key_block, model_width)
            * score_scale
        )
        key_acc = add_rows(key_acc, key_part, offset)
        return (query_grad, key_acc, value_acc, kernel_grad)

    initial = (
        jnp.zeros(query_ext.shape, jnp.float32),
        key_acc,
        value_acc,
        jnp.zeros(kernel.shape, jnp.float32),
    )
    return lax.fori_loop(0, block_count, advance, initial)


def accumulate(previous, update):
    return (
        update
        if previous is None
        else tuple((left + right for left, right in zip(previous, update)))
    )


def on_device(
    inputs,
    out_grad,
    pair_index,
    norm_gain,
    query_weight,
    key_weight,
    value_weight,
    score_kernel,
    head_mixing,
    group_gain,
    output_weight,
    second_gain,
    gate_weight,
    up_weight,
    down_weight,
):
    micro_count = inputs.shape[0]
    local_rows = inputs.shape[2]
    block_rows = local_rows // 2
    model_width = inputs.shape[3]
    head_count = score_kernel.shape[0]
    head_dim = model_width // head_count
    groups = head_count // 2
    halo_rows = score_kernel.shape[1] - 1
    key_reach = (score_kernel.shape[2] - 1) // 2
    block_count = 2 * lax.axis_size("ctx")
    seq_length = block_count * block_rows
    key_block = min(512, seq_length)
    layout = (block_rows, halo_rows, key_reach, key_block, groups, head_dim ** (-0.5))
    extended = block_rows + halo_rows
    my_index = lax.axis_index("ctx")
    slot_ids = jnp.arange(block_count, dtype=jnp.int32)
    mix_table = head_mixing.reshape(groups, 2, 2)
    pad_width = ((2 * key_reach, 2 * key_reach), (0, 0))
    layer_rows = []
    input_rows = []
    feed_sums = None
    attention_sums = None
    kernel_total = jnp.zeros(score_kernel.shape, jnp.float32)
    mixing_total = jnp.zeros(head_mixing.shape, jnp.float32)
    for batch_index in range(micro_count):
        gain_first, query_full, key_full, value_full, gain_group, out_full = (
            lax.all_gather(norm_gain, ("seq", "ctx"), axis=0, tiled=True),
            lax.all_gather(query_weight, ("seq", "ctx"), axis=0, tiled=True),
            lax.all_gather(key_weight, ("seq", "ctx"), axis=0, tiled=True),
            lax.all_gather(value_weight, ("seq", "ctx"), axis=0, tiled=True),
            lax.all_gather(group_gain, ("seq", "ctx"), axis=0, tiled=True),
            lax.all_gather(output_weight, ("seq", "ctx"), axis=0, tiled=True),
        )
        tokens = inputs[batch_index, 0].astype(jnp.float32)
        normed_first, factor_first = normalize(tokens)
        hidden = (normed_first * gain_first.astype(jnp.float32)).astype(jnp.bfloat16)
        query_proj = jnp.dot(hidden, query_full, preferred_element_type=jnp.float32).astype(
            jnp.bfloat16
        )
        key_proj = jnp.dot(hidden, key_full, preferred_element_type=jnp.float32).astype(
            jnp.bfloat16
        )
        value_proj = jnp.dot(hidden, value_full, preferred_element_type=jnp.float32).astype(
            jnp.bfloat16
        )
        tail_rows = jnp.concatenate(
            [query_proj[block_rows - halo_rows : block_rows], query_proj[local_rows - halo_rows :]],
            axis=0,
        )
        key_dealt, value_dealt, tail_dealt = (
            lax.all_gather(key_proj, "ctx", axis=0, tiled=True),
            lax.all_gather(value_proj, "ctx", axis=0, tiled=True),
            lax.all_gather(tail_rows, "ctx", axis=0, tiled=True),
        )
        pairs_row = pair_index[batch_index]
        owner_pair = pairs_row[slot_ids // 2]
        block_of_slot = jnp.where(slot_ids % 2 == 0, owner_pair, block_count - 1 - owner_pair)
        slot_of_block = jnp.argsort(block_of_slot)
        my_pair = pairs_row[my_index]
        my_blocks = jnp.stack([my_pair, block_count - 1 - my_pair])
        key_pad = jnp.pad(
            key_dealt.reshape(block_count, block_rows, model_width)[slot_of_block].reshape(
                seq_length, model_width
            ),
            pad_width,
        ).reshape(-1, head_count, head_dim)
        value_pad = jnp.pad(
            value_dealt.reshape(block_count, block_rows, model_width)[slot_of_block].reshape(
                seq_length, model_width
            ),
            pad_width,
        )
        tail_blocks = tail_dealt.reshape(block_count, halo_rows, model_width)[slot_of_block]
        previous = jnp.concatenate(
            [jnp.zeros((1, halo_rows, model_width), jnp.bfloat16), tail_blocks[:-1]], axis=0
        )
        query_ext = jnp.concatenate(
            [previous[my_blocks], query_proj.reshape(2, block_rows, model_width)], axis=1
        ).reshape(2, extended, head_count, head_dim)
        row_pos = (
            my_blocks[:, None] * block_rows
            - halo_rows
            + jnp.arange(extended, dtype=jnp.int32)[None, :]
        )
        mixed_in, log_total = attend_forward(
            query_ext, row_pos, key_pad, value_pad, score_kernel, layout
        )
        mixed_six = mixed_in.reshape(2, groups, 2, block_rows, 2, head_dim)
        heads_out = jnp.einsum(
            "gqp,ngpiqd->nigqd", mix_table, mixed_six, precision=PRECISE
        ).reshape(local_rows, head_count, head_dim)
        group_normed, group_factor = normalize(heads_out)
        normed_low = (
            group_normed.reshape(local_rows, model_width) * gain_group.astype(jnp.float32)
        ).astype(jnp.bfloat16)
        residual = tokens + jnp.dot(normed_low, out_full, preferred_element_type=jnp.float32)
        gain_second, gate_full, up_full, down_full = (
            lax.all_gather(second_gain, ("seq", "ctx"), axis=0, tiled=True),
            lax.all_gather(gate_weight, ("seq", "ctx"), axis=0, tiled=True),
            lax.all_gather(up_weight, ("seq", "ctx"), axis=0, tiled=True),
            lax.all_gather(down_weight, ("seq", "ctx"), axis=0, tiled=True),
        )
        normed_second, factor_second = normalize(residual)
        second_hidden = (normed_second * gain_second.astype(jnp.float32)).astype(jnp.bfloat16)
        gate_proj = jnp.dot(second_hidden, gate_full, preferred_element_type=jnp.float32)
        up_proj = jnp.dot(second_hidden, up_full, preferred_element_type=jnp.float32)
        activated = (jax.nn.silu(gate_proj) * up_proj).astype(jnp.bfloat16)
        layer_rows.append(
            (residual + jnp.dot(activated, down_full, preferred_element_type=jnp.float32)).astype(
                jnp.bfloat16
            )
        )
        gain_second, gate_full, up_full, down_full = (
            lax.all_gather(second_gain, ("seq", "ctx"), axis=0, tiled=True),
            lax.all_gather(gate_weight, ("seq", "ctx"), axis=0, tiled=True),
            lax.all_gather(up_weight, ("seq", "ctx"), axis=0, tiled=True),
            lax.all_gather(down_weight, ("seq", "ctx"), axis=0, tiled=True),
        )
        grad_rows = out_grad[batch_index, 0]
        hid_grad = jnp.dot(grad_rows, down_full.T, preferred_element_type=jnp.float32)
        down_grad = jnp.dot(activated.T, grad_rows, preferred_element_type=jnp.float32)
        sigmoid_gate = jax.nn.sigmoid(gate_proj)
        up_low = (hid_grad * gate_proj * sigmoid_gate).astype(jnp.bfloat16)
        gate_low = (
            hid_grad * up_proj * sigmoid_gate * (1.0 + gate_proj * (1.0 - sigmoid_gate))
        ).astype(jnp.bfloat16)
        second_grad = jnp.dot(gate_low, gate_full.T, preferred_element_type=jnp.float32) + jnp.dot(
            up_low, up_full.T, preferred_element_type=jnp.float32
        )
        gate_grad = jnp.dot(second_hidden.T, gate_low, preferred_element_type=jnp.float32)
        up_grad = jnp.dot(second_hidden.T, up_low, preferred_element_type=jnp.float32)
        residual_part, gain_second_grad = normalize_back(
            normed_second, factor_second, gain_second.astype(jnp.float32), second_grad
        )
        residual_grad = grad_rows.astype(jnp.float32) + residual_part
        feed_shards = (
            lax.psum_scatter(gain_second_grad, ("seq", "ctx"), scatter_dimension=0, tiled=True),
            lax.psum_scatter(gate_grad, ("seq", "ctx"), scatter_dimension=0, tiled=True),
            lax.psum_scatter(up_grad, ("seq", "ctx"), scatter_dimension=0, tiled=True),
            lax.psum_scatter(down_grad, ("seq", "ctx"), scatter_dimension=0, tiled=True),
        )
        feed_sums = accumulate(feed_sums, feed_shards)
        gain_first, query_full, key_full, value_full, gain_group, out_full = (
            lax.all_gather(norm_gain, ("seq", "ctx"), axis=0, tiled=True),
            lax.all_gather(query_weight, ("seq", "ctx"), axis=0, tiled=True),
            lax.all_gather(key_weight, ("seq", "ctx"), axis=0, tiled=True),
            lax.all_gather(value_weight, ("seq", "ctx"), axis=0, tiled=True),
            lax.all_gather(group_gain, ("seq", "ctx"), axis=0, tiled=True),
            lax.all_gather(output_weight, ("seq", "ctx"), axis=0, tiled=True),
        )
        attended_low = residual_grad.astype(jnp.bfloat16)
        out_weight_grad = jnp.dot(normed_low.T, attended_low, preferred_element_type=jnp.float32)
        normed_grad = jnp.dot(attended_low, out_full.T, preferred_element_type=jnp.float32)
        heads_grad, gain_group_grad = normalize_back(
            group_normed,
            group_factor,
            gain_group.astype(jnp.float32).reshape(head_count, head_dim),
            normed_grad.reshape(local_rows, head_count, head_dim),
        )
        heads_five = heads_grad.reshape(2, block_rows, groups, 2, head_dim)
        mixing_total = mixing_total + jnp.einsum(
            "nigqd,ngpiqd->gqp", heads_five, mixed_six, precision=PRECISE
        ).reshape(head_count, 2)
        mixed_grad = jnp.einsum(
            "gqp,nigqd->ngpiqd", mix_table, heads_five, precision=PRECISE
        ).reshape(2, groups, 2, block_rows, 2 * head_dim)
        mixed_low = mixed_grad.astype(jnp.bfloat16)
        delta_rows = jnp.sum(mixed_low.astype(jnp.float32) * mixed_in, axis=-1).reshape(
            2, head_count, block_rows
        )
        key_acc = jnp.zeros((seq_length, model_width), jnp.float32)
        value_acc = jnp.zeros((seq_length, model_width), jnp.float32)
        query_grad, key_acc, value_acc, kernel_part = attend_backward(
            query_ext,
            row_pos,
            key_pad,
            value_pad,
            score_kernel,
            log_total,
            mixed_low,
            delta_rows,
            key_acc,
            value_acc,
            layout,
        )
        kernel_total = kernel_total + kernel_part
        halo_grad = query_grad[:, :halo_rows].reshape(2, halo_rows, model_width)
        own_grad = query_grad[:, halo_rows:].reshape(2, block_rows, model_width)
        target_slot = slot_of_block[jnp.maximum(my_blocks - 1, 0)]
        routing = ((slot_ids[None, :] == target_slot[:, None]) & (my_blocks > 0)[:, None]).astype(
            jnp.float32
        )
        tail_grad = jnp.einsum("ws,wrc->src", routing, halo_grad, precision=PRECISE).reshape(
            block_count * halo_rows, model_width
        )
        key_back = key_acc.reshape(block_count, block_rows, model_width)[block_of_slot].reshape(
            seq_length, model_width
        )
        value_back = value_acc.reshape(block_count, block_rows, model_width)[block_of_slot].reshape(
            seq_length, model_width
        )
        key_mine, value_mine, tail_mine = (
            lax.psum_scatter(
                key_back.astype(jnp.bfloat16), "ctx", scatter_dimension=0, tiled=True
            ).astype(jnp.float32),
            lax.psum_scatter(
                value_back.astype(jnp.bfloat16), "ctx", scatter_dimension=0, tiled=True
            ).astype(jnp.float32),
            lax.psum_scatter(
                tail_grad.astype(jnp.bfloat16), "ctx", scatter_dimension=0, tiled=True
            ).astype(jnp.float32),
        )
        tail_mine = tail_mine.reshape(2, halo_rows, model_width)
        query_total = jnp.concatenate(
            [
                own_grad[:, : block_rows - halo_rows],
                own_grad[:, block_rows - halo_rows :] + tail_mine,
            ],
            axis=1,
        ).reshape(local_rows, model_width)
        query_low = query_total.astype(jnp.bfloat16)
        key_low = key_mine.astype(jnp.bfloat16)
        value_low = value_mine.astype(jnp.bfloat16)
        query_w_grad = jnp.dot(hidden.T, query_low, preferred_element_type=jnp.float32)
        key_w_grad = jnp.dot(hidden.T, key_low, preferred_element_type=jnp.float32)
        value_w_grad = jnp.dot(hidden.T, value_low, preferred_element_type=jnp.float32)
        hidden_grad = (
            jnp.dot(query_low, query_full.T, preferred_element_type=jnp.float32)
            + jnp.dot(key_low, key_full.T, preferred_element_type=jnp.float32)
            + jnp.dot(value_low, value_full.T, preferred_element_type=jnp.float32)
        )
        token_part, gain_first_grad = normalize_back(
            normed_first, factor_first, gain_first.astype(jnp.float32), hidden_grad
        )
        input_rows.append((residual_grad + token_part).astype(jnp.bfloat16))
        attention_shards = (
            lax.psum_scatter(gain_first_grad, ("seq", "ctx"), scatter_dimension=0, tiled=True),
            lax.psum_scatter(query_w_grad, ("seq", "ctx"), scatter_dimension=0, tiled=True),
            lax.psum_scatter(key_w_grad, ("seq", "ctx"), scatter_dimension=0, tiled=True),
            lax.psum_scatter(value_w_grad, ("seq", "ctx"), scatter_dimension=0, tiled=True),
            lax.psum_scatter(
                gain_group_grad.reshape(model_width),
                ("seq", "ctx"),
                scatter_dimension=0,
                tiled=True,
            ),
            lax.psum_scatter(out_weight_grad, ("seq", "ctx"), scatter_dimension=0, tiled=True),
        )
        attention_sums = accumulate(attention_sums, attention_shards)
    kernel_sum, mixing_sum = lax.psum((kernel_total, mixing_total), ("seq", "ctx"))
    layer_out = jnp.stack(layer_rows)[:, None]
    input_grad = jnp.stack(input_rows)[:, None]
    return (
        layer_out,
        input_grad,
        attention_sums[0],
        attention_sums[1],
        attention_sums[2],
        attention_sums[3],
        kernel_sum,
        mixing_sum,
        attention_sums[4],
        attention_sums[5],
        feed_sums[0],
        feed_sums[1],
        feed_sums[2],
        feed_sums[3],
    )


def solution(mesh):
    placed = (
        P(None, "seq", "ctx", None),
        P(None, "seq", "ctx", None),
        P(),
        P(("seq", "ctx")),
        P(("seq", "ctx"), None),
        P(("seq", "ctx"), None),
        P(("seq", "ctx"), None),
        P(),
        P(),
        P(("seq", "ctx")),
        P(("seq", "ctx"), None),
        P(("seq", "ctx")),
        P(("seq", "ctx"), None),
        P(("seq", "ctx"), None),
        P(("seq", "ctx"), None),
    )
    return jax.shard_map(
        on_device,
        mesh=mesh,
        in_specs=placed,
        out_specs=(
            P(None, "seq", "ctx", None),
            P(None, "seq", "ctx", None),
            P(("seq", "ctx")),
            P(("seq", "ctx"), None),
            P(("seq", "ctx"), None),
            P(("seq", "ctx"), None),
            P(),
            P(),
            P(("seq", "ctx")),
            P(("seq", "ctx"), None),
            P(("seq", "ctx")),
            P(("seq", "ctx"), None),
            P(("seq", "ctx"), None),
            P(("seq", "ctx"), None),
        ),
        check_vma=False,
    )
```

profile of v0, /device:TPU:9, one launch (start us, length us, event | category | flops | bytes accessed | tf_op | source)
XLA Modules:
  0.0 2958.3 jit_solution(10205337969670304350)
XLA Ops:
  12.0 40.5 %all-reduce.17 = (bf16[1536]{0:T(1024)(128)(2,1)S(1)}, bf16[1536]{0:T(1024)(128)(2,1)S(1)}, bf16[1536]{0:T(1024)(128)(2,1)S(1)}) all-reduce(bf16[1536]{0:T(1024)(128)(2,1)S(1)} %dynamic-update-slice, bf16[1536]{0:T(1024)(128)(2,1)S(1)} %dynamic-update-slice.1, ...), channel_id=1, replica_groups=mesh['seq'=4,'ctx'=8] {'seq','ctx'}, use_global_device_ids=true, to_apply=%add.8 | all-reduce | flops 4608 | bytes 18432
  53.8 22.8 all-gather.14.cloned.1.call-done
  80.8 61.2 %all-gather.20.cloned.1.call-done = bf16[1536,1536]{1,0:T(8,128)(2,1)} async-done(((bf16[48,1536]{1,0:T(8,128)(2,1)}), bf16[1536,1536]{1,0:T(8,128)(2,1)}) %all-gather.20.cloned.1.call-update) | async-done | bytes 4718608 | tf_op jit(solution)/shard_map/all_gather | solution.py:262
  184.0 23.5 all-gather.18.cloned.1.call-done
  214.8 10.0 all-gather.1
  226.3 9.4 all-gather
  241.7 22.6 all-gather.34.cloned.1.call-done
  274.9 57.3 %while.71 = (s32[]{:T(128)}, f32[2,16,32]{2,0,1:T(2,128)S(1)}, f32[2,16,32]{2,0,1:T(2,128)S(1)}, f32[2,8,2,32,192]{4,3,2,0,1:T(8,128)}, s32[]{:T(128)}, /*index=...) while((s32[]{:T(128)}, f32[2,16,32]{2,0,1:T(2,128)S(1)}, ...), condition=%wide.region_15.16_spmd, body=%wide.region_12.15_spmd.sunk | while | flops 395336896 | bytes 161904976 | solution.py:97
  280.5 45.0 %fusion.1015 = (f32[2,16,32]{2,0,1:T(2,128)S(1)}, f32[2,16,32,512]{3,2,0,1:T(8,128)}) fusion(f32[2,16,37,532]{3,2,0,1:T(8,128)S(1)} %bitcast_select_fusion.9, f32[16]{0:T(128)S(1)} %get-tuple-element.2304, f32[16]{0:T(128)S(1)} %get-tuple-element.2305, f32[16]{0:T(128)S(1)} %get-tuple-element.2306, f32[16]{0:T(128)S(1)} %get-tuple-element.2307, ...), kind=kLoop, calls=%fused_computation.1815.clone.1 | loop fusion | flops 69729280 | bytes 140550272 | tf_op jit(solution)/shard_map/while/body/reduce_max | solution.py:77
  356.6 57.7 %while.70 = (s32[]{:T(128)}, f32[2,16,32]{2,0,1:T(2,128)S(1)}, f32[2,16,32]{2,0,1:T(2,128)S(1)}, f32[2,8,2,32,192]{4,3,2,0,1:T(8,128)}, s32[]{:T(128)}, /*index=...) while((s32[]{:T(128)}, f32[2,16,32]{2,0,1:T(2,128)S(1)}, ...), condition=%wide.region_6.7_spmd, body=%wide.region_3.6_spmd.sunk | while | flops 395336896 | bytes 161904976 | solution.py:97
  362.6 45.0 %fusion.1008 = (f32[2,16,32]{2,0,1:T(2,128)S(1)}, f32[2,16,32,512]{3,2,0,1:T(8,128)}) fusion(f32[2,16,37,532]{3,2,0,1:T(8,128)S(1)} %bitcast_select_fusion.8, f32[16]{0:T(128)S(1)} %get-tuple-element.2222, f32[16]{0:T(128)S(1)} %get-tuple-element.2223, f32[16]{0:T(128)S(1)} %get-tuple-element.2224, f32[16]{0:T(128)S(1)} %get-tuple-element.2225, ...), kind=kLoop, calls=%fused_computation.1814.clone.1 | loop fusion | flops 69729280 | bytes 140550272 | tf_op jit(solution)/shard_map/while/body/reduce_max | solution.py:77
  433.3 50.9 %all-gather.26.cloned.1.call-done = bf16[1536,4096]{1,0:T(8,128)(2,1)} async-done(((bf16[48,4096]{1,0:T(8,128)(2,1)}), bf16[1536,4096]{1,0:T(8,128)(2,1)}) %all-gather.26.cloned.1.call-update) | async-done | bytes 12582928 | tf_op jit(solution)/shard_map/all_gather | solution.py:331
  491.1 90.1 %all-gather.28.cloned.1.call-done = bf16[1536,4096]{1,0:T(8,128)(2,1)} async-done(((bf16[48,4096]{1,0:T(8,128)(2,1)}), bf16[1536,4096]{1,0:T(8,128)(2,1)}) %all-gather.28.cloned.1.call-update) | async-done | bytes 12582928 | tf_op jit(solution)/shard_map/all_gather | solution.py:332
  589.0 89.3 %all-gather.30.cloned.1.call-done = bf16[4096,1536]{1,0:T(8,128)(2,1)} async-done(((bf16[128,1536]{1,0:T(8,128)(2,1)}), bf16[4096,1536]{1,0:T(8,128)(2,1)}) %all-gather.30.cloned.1.call-update) | async-done | bytes 12582928 | tf_op jit(solution)/shard_map/all_gather | solution.py:333
  678.3 9.9 multiply_convert_fusion.6
  688.2 8.9 fusion.862
  725.6 8.7 fusion.864
  734.4 9.3 multiply_reduce_fusion.4
  770.5 306.8 %while.73 = (s32[]{:T(128)}, f32[2,37,16,96]{3,1,0,2:T(8,128)}, f32[512,1536]{0,1:T(8,128)}, f32[512,1536]{0,1:T(8,128)}, f32[16,6,11]{2,1,0:T(8,128)S(1)}, /*in...) while((s32[]{:T(128)}, f32[2,37,16,96]{3,1,0,2:T(8,128)}, ...), condition=%wide.region_163.164_spmd.clone, body=%wide.region_96.163_spmd.clone.sunk | while | flops 987300992 | bytes 401819392 | solution.py:205
  784.5 49.0 %fusion.1050 = (f32[2,16,32,522]{3,2,0,1:T(8,128)}, bf16[2,16,32,522]{3,2,0,1:T(8,128)(2,1)}) fusion(f32[2,8,2,32,522]{4,3,0,2,1:T(8,128)} %copy.611, f32[2,16,32]{2,0,1:T(2,128)} %bitcast.1502, f32[2,16,32]{2,0,1:T(2,128)} %get-tuple-element.2832, f32[2,16,37,532]{3,2,0,1:T(8,128)S(1)} %bitcast_select_fusion.11, f32[16]{0:T(128)S(1)} %get-tuple-element.2542, ...), kind=kLoop, calls=%fused_computation.1346.clone.1 | loop fusion | flops 72695808 | bytes 146506496 | tf_op jit(solution)/shard_map/while/body/mul | solution.py:140
  834.3 122.2 %select_convert_fusion.5 = bf16[2,16,37,512]{3,2,0,1:T(8,128)(2,1)} fusion(f32[2,16,32,522]{3,2,0,1:T(8,128)} %get-tuple-element.2608, f32[16]{0:T(128)S(1)} %get-tuple-element.2542, f32[16]{0:T(128)S(1)} %get-tuple-element.2543, f32[16]{0:T(128)S(1)} %get-tuple-element.2544, f32[16]{0:T(128)S(1)} %get-tuple-element.2545, ...), kind=kLoop, calls=%fused_computation.1347.clone.1 | loop fusion | flops 80625664 | bytes 3392640 | tf_op jit(solution)/shard_map/while/body/convert_element_type | solution.py:183
  975.3 10.2 fusion.1054
  1088.2 315.0 %while.72 = (s32[]{:T(128)}, f32[2,37,16,96]{3,1,0,2:T(8,128)}, f32[512,1536]{0,1:T(8,128)}, f32[512,1536]{0,1:T(8,128)}, f32[16,6,11]{2,1,0:T(8,128)S(1)}, /*in...) while((s32[]{:T(128)}, f32[2,37,16,96]{3,1,0,2:T(8,128)}, ...), condition=%wide.region_88.89_spmd.clone, body=%wide.region_21.88_spmd.clone.sunk | while | flops 987300992 | bytes 401819392 | solution.py:205
  1102.3 49.4 %fusion.1029 = (f32[2,16,32,522]{3,2,0,1:T(8,128)}, bf16[2,16,32,522]{3,2,0,1:T(8,128)(2,1)}) fusion(f32[2,8,2,32,522]{4,3,0,2,1:T(8,128)} %copy.542, f32[2,16,32]{2,0,1:T(2,128)} %bitcast.1414, f32[2,16,32]{2,0,1:T(2,128)} %get-tuple-element.2904, f32[2,16,37,532]{3,2,0,1:T(8,128)S(1)} %bitcast_select_fusion.10, f32[16]{0:T(128)S(1)} %get-tuple-element.2391, ...), kind=kLoop, calls=%fused_computation.784.clone.1 | loop fusion | flops 72695808 | bytes 146506496 | tf_op jit(solution)/shard_map/while/body/mul | solution.py:140
  1152.5 124.7 %select_convert_fusion.4 = bf16[2,16,37,512]{3,2,0,1:T(8,128)(2,1)} fusion(f32[2,16,32,522]{3,2,0,1:T(8,128)} %get-tuple-element.2457, f32[16]{0:T(128)S(1)} %get-tuple-element.2391, f32[16]{0:T(128)S(1)} %get-tuple-element.2392, f32[16]{0:T(128)S(1)} %get-tuple-element.2393, f32[16]{0:T(128)S(1)} %get-tuple-element.2394, ...), kind=kLoop, calls=%fused_computation.785.clone.1 | loop fusion | flops 80625664 | bytes 3392640 | tf_op jit(solution)/shard_map/while/body/convert_element_type | solution.py:183
  1296.0 10.2 fusion.1033
  1438.2 20.5 all-reduce.21.cloned.1.call-done
  1467.8 33.2 %reduce-scatter.12.cloned.1.call-done = bf16[64,1536]{1,0:T(8,128)(2,1)} async-done(((bf16[512,1536]{1,0:T(8,128)(2,1)}), bf16[64,1536]{1,0:T(8,128)(2,1)}) %reduce-scatter.12.cloned.1.call-update) | async-done | bytes 196624 | tf_op jit(solution)/shard_map/reduce_scatter | solution.py:435
  1507.1 35.9 %reduce-scatter.16.cloned.1.call-done = bf16[64,1536]{1,0:T(8,128)(2,1)} async-done(((bf16[512,1536]{1,0:T(8,128)(2,1)}), bf16[64,1536]{1,0:T(8,128)(2,1)}) %reduce-scatter.16.cloned.1.call-update) | async-done | bytes 196624 | tf_op jit(solution)/shard_map/reduce_scatter | solution.py:435
  1543.0 8.9 convolution_add_fusion.5
  1552.0 33.0 %reduce-scatter.14.cloned.1.call-done = bf16[64,1536]{1,0:T(8,128)(2,1)} async-done(((bf16[512,1536]{1,0:T(8,128)(2,1)}), bf16[64,1536]{1,0:T(8,128)(2,1)}) %reduce-scatter.14.cloned.1.call-update) | async-done | bytes 196624 | tf_op jit(solution)/shard_map/reduce_scatter | solution.py:438
  1591.0 35.9 %reduce-scatter.18.cloned.1.call-done = bf16[64,1536]{1,0:T(8,128)(2,1)} async-done(((bf16[512,1536]{1,0:T(8,128)(2,1)}), bf16[64,1536]{1,0:T(8,128)(2,1)}) %reduce-scatter.18.cloned.1.call-update) | async-done | bytes 196624 | tf_op jit(solution)/shard_map/reduce_scatter | solution.py:438
  1626.9 8.9 convolution_add_fusion.4
  1637.0 11.0 fusion.866
  1647.9 18.9 convolution_add_fusion.1
  1667.9 10.7 fusion.867
  1678.6 16.5 convolution_add_fusion
  1696.3 10.5 fusion.792
  1706.8 17.7 convolution_add_fusion.2
  1725.8 10.7 fusion.730
  1736.6 11.1 fusion.732
  1772.6 40.5 %all-reduce.16 = (f32[1536]{0:T(1024)S(1)}, f32[16,6,11]{0,1,2:T(8,128)}, f32[16,2]{0,1:T(2,128)}, f32[1536]{0:T(1024)S(1)}, f32[1536]{0:T(1024)S(1)}) all-reduce(f32[1536]{0:T(1024)S(1)} %add.3205, f32[16,6,11]{0,1,2:T(8,128)S(1)} %add.3196, f32[16,2]{0,1:T(2,128)S(1)} %add.3198, ...), channel_id=18, replica_groups=mesh['seq'=4,'ctx'=8] {'seq','ctx'}, use_global_device_ids=true, to_apply=%region_169.170.clone | all-reduce | flops 5696 | bytes 45568
  1815.9 92.9 %reduce-scatter.20.cloned.1.call-done = f32[48,1536]{1,0:T(8,128)} async-done(((f32[1536,1536]{1,0:T(8,128)}), f32[48,1536]{1,0:T(8,128)}) %reduce-scatter.20.cloned.1.call-update) | async-done | bytes 294928 | tf_op jit(solution)/shard_map/reduce_scatter | solution.py:470
  1908.8 142.1 %reduce-scatter.22.cloned.1.call-done = f32[48,1536]{1,0:T(8,128)} async-done(((f32[1536,1536]{1,0:T(8,128)}), f32[48,1536]{1,0:T(8,128)}) %reduce-scatter.22.cloned.1.call-update) | async-done | bytes 294928 | tf_op jit(solution)/shard_map/reduce_scatter | solution.py:471
  2050.9 140.8 %reduce-scatter.24.cloned.1.call-done = f32[48,1536]{1,0:T(8,128)} async-done(((f32[1536,1536]{1,0:T(8,128)}), f32[48,1536]{1,0:T(8,128)}) %reduce-scatter.24.cloned.1.call-update) | async-done | bytes 294928 | tf_op jit(solution)/shard_map/reduce_scatter | solution.py:472
  2191.7 254.7 %reduce-scatter.28.cloned.1.call-done = f32[48,4096]{1,0:T(8,128)} async-done(((f32[1536,4096]{1,0:T(8,128)}), f32[48,4096]{1,0:T(8,128)}) %reduce-scatter.28.cloned.1.call-update) | async-done | bytes 786448 | tf_op jit(solution)/shard_map/reduce_scatter | solution.py:370
  2446.3 252.0 %reduce-scatter.30.cloned.1.call-done = f32[48,4096]{1,0:T(8,128)} async-done(((f32[1536,4096]{1,0:T(8,128)}), f32[48,4096]{1,0:T(8,128)}) %reduce-scatter.30.cloned.1.call-update) | async-done | bytes 786448 | tf_op jit(solution)/shard_map/reduce_scatter | solution.py:371
  2698.3 253.2 %reduce-scatter.32.cloned.1.call-done = f32[128,1536]{1,0:T(8,128)} async-done(((f32[4096,1536]{1,0:T(8,128)}), f32[128,1536]{1,0:T(8,128)}) %reduce-scatter.32.cloned.1.call-update) | async-done | bytes 786448 | tf_op jit(solution)/shard_map/reduce_scatter | solution.py:372
  (812 shorter events, 550.3 us)
Async XLA Ops:
  7.2 69.4 %all-gather.14.cloned.1.call-start = ((), (), s32[]{:S(2)}) async-start(), calls=%async_computation.11 | async-start | bytes 4866048 | tf_op jit(solution)/shard_map/all_gather | solution.py:261
  7.9 134.0 %all-gather.20.cloned.1.call-start = ((), (), s32[]{:S(2)}) async-start(), calls=%async_computation.14 | async-start | bytes 4866048 | tf_op jit(solution)/shard_map/all_gather | solution.py:262
  8.7 198.8 %all-gather.18.cloned.1.call-start = ((), (), s32[]{:S(2)}) async-start(), calls=%async_computation.13 | async-start | bytes 4866048 | tf_op jit(solution)/shard_map/all_gather | solution.py:260
  9.4 229.5 %all-gather.32.cloned.1.call-start = ((), (), s32[]{:S(2)}) async-start(), calls=%async_computation.20 | async-start | bytes 1769472 | tf_op jit(solution)/shard_map/all_gather | solution.py:283
  52.5 158.5 %copy-start.72 = (f32[1536]{0:T(1024)}, f32[1536]{0:T(1024)S(1)}, u32[]{:S(2)}) copy-start(f32[1536]{0:T(1024)S(1)} %convert_element_type.268) | copy-start | bytes 18436
  53.7 153.7 %copy-start.108 = (f32[64]{0:T(128)}, f32[64]{0:T(128)S(1)}, u32[]{:S(2)}) copy-start(f32[64]{0:T(128)S(1)} %add_rsqrt_fusion.3) | copy-start | bytes 772
  53.7 88.2 %copy-start.26 = (bf16[2,1,64,1536]{3,2,1,0:T(8,128)(2,1)S(1)}, bf16[2,1,64,1536]{3,2,1,0:T(8,128)(2,1)}, u32[]{:S(2)}) copy-start(bf16[2,1,64,1536]{3,2,1,0:T(8,128)(2,1)} %param.23) | copy-start | bytes 1179652
  80.7 183.6 %all-gather.34.cloned.1.call-start = ((), (), s32[]{:S(2)}) async-start(), calls=%async_computation.21 | async-start | bytes 1769472 | tf_op jit(solution)/shard_map/all_gather | solution.py:284
  146.0 196.9 %all-gather.16.cloned.1.call-start = ((), (), s32[]{:S(2)}) async-start(), calls=%async_computation.12 | async-start | bytes 1769472 | tf_op jit(solution)/shard_map/all_gather | solution.py:283
  146.0 65.0 %copy-start.105 = (f32[64]{0:T(128)}, f32[64]{0:T(128)S(1)}, u32[]{:S(2)}) copy-start(f32[64]{0:T(128)S(1)} %add_rsqrt_fusion.5) | copy-start | bytes 772
  150.1 20.4 copy-start.124
  150.1 26.3 copy-start.107
  150.1 195.7 %all-gather.22.cloned.1.call-start = ((), (), s32[]{:S(2)}) async-start(), calls=%async_computation.15 | async-start | bytes 1769472 | tf_op jit(solution)/shard_map/all_gather | solution.py:284
  154.3 272.6 %all-gather.24.cloned.1.call-start = ((), (), s32[]{:S(2)}) async-start(), calls=%async_computation.16 | async-start | bytes 4866048 | tf_op jit(solution)/shard_map/all_gather | solution.py:264
  155.0 329.1 %all-gather.26.cloned.1.call-start = ((), (), s32[]{:S(2)}) async-start(), calls=%async_computation.17 | async-start | bytes 12976128 | tf_op jit(solution)/shard_map/all_gather | solution.py:331
  155.8 425.4 %all-gather.28.cloned.1.call-start = ((), (), s32[]{:S(2)}) async-start(), calls=%async_computation.18 | async-start | bytes 12976128 | tf_op jit(solution)/shard_map/all_gather | solution.py:332
  156.4 521.9 %all-gather.30.cloned.1.call-start = ((), (), s32[]{:S(2)}) async-start(), calls=%async_computation.19 | async-start | bytes 12976128 | tf_op jit(solution)/shard_map/all_gather | solution.py:333
  157.1 1301.7 %all-reduce.21.cloned.1.call-start = ((), (), s32[]{:S(2)}) async-start(), calls=%async_computation.33 | async-start | bytes 983040
  171.2 39.5 %copy-start.83 = (f32[8,2,2]{1,0,2:T(8,128)}, f32[8,2,2]{1,0,2:T(8,128)S(1)}, u32[]{:S(2)}) copy-start(f32[8,2,2]{1,0,2:T(8,128)S(1)} %reshape.1212) | copy-start | bytes 388
  177.1 30.4 %copy-start.120 = (s32[16]{0:T(128)}, s32[16]{0:T(128)S(1)}, u32[]{:S(2)}) copy-start(s32[16]{0:T(128)S(1)} %gather_fusion.5) | copy-start | bytes 196
  180.3 55.5 %copy-start.119 = (s32[1024]{0:T(1024)}, s32[1024]{0:T(1024)S(1)}, u32[]{:S(2)}) copy-start(s32[1024]{0:T(1024)S(1)} %pad_clamp_fusion.7) | copy-start | bytes 12292
  430.5 266.6 %copy-start.34 = (f32[64,1536]{1,0:T(8,128)}, f32[64,1536]{1,0:T(8,128)S(1)}, u32[]{:S(2)}) copy-start(f32[64,1536]{1,0:T(8,128)S(1)} %get-tuple-element.1504) | copy-start | bytes 1179652
  431.8 265.3 %copy-start.31 = (f32[64,1536]{1,0:T(8,128)}, f32[64,1536]{1,0:T(8,128)S(1)}, u32[]{:S(2)}) copy-start(f32[64,1536]{1,0:T(8,128)S(1)} %get-tuple-element.1506) | copy-start | bytes 1179652
  433.3 147.9 %copy-start.48 = (bf16[64,1536]{1,0:T(8,128)(2,1)}, bf16[64,1536]{1,0:T(8,128)(2,1)S(1)}, u32[]{:S(2)}) copy-start(bf16[64,1536]{1,0:T(8,128)(2,1)S(1)} %multiply_convert_fusion.12) | copy-start | bytes 589828
  678.3 18.8 slice-start.3
  678.3 18.8 slice-start.4
  702.5 16.0 slice-start
  702.5 16.0 slice-start.1
  1406.5 94.6 %reduce-scatter.12.cloned.1.call-start = ((), (), s32[]{:S(2)}) async-start(), calls=%async_computation.22 | async-start | bytes 1769472 | tf_op jit(solution)/shard_map/reduce_scatter | solution.py:435
  1413.0 130.0 %reduce-scatter.16.cloned.1.call-start = ((), (), s32[]{:S(2)}) async-start(), calls=%async_computation.24 | async-start | bytes 1769472 | tf_op jit(solution)/shard_map/reduce_scatter | solution.py:435
  1418.2 166.8 %reduce-scatter.14.cloned.1.call-start = ((), (), s32[]{:S(2)}) async-start(), calls=%async_computation.23 | async-start | bytes 1769472 | tf_op jit(solution)/shard_map/reduce_scatter | solution.py:438
  1423.3 203.6 %reduce-scatter.18.cloned.1.call-start = ((), (), s32[]{:S(2)}) async-start(), calls=%async_computation.25 | async-start | bytes 1769472 | tf_op jit(solution)/shard_map/reduce_scatter | solution.py:438
  1428.4 387.5 %reduce-scatter.26.cloned.1.call-start = ((), (), s32[]{:S(2)}) async-start(), calls=%async_computation.29 | async-start | bytes 9732096 | tf_op jit(solution)/shard_map/reduce_scatter | solution.py:479
  1435.0 473.8 %reduce-scatter.20.cloned.1.call-start = ((), (), s32[]{:S(2)}) async-start(), calls=%async_computation.26 | async-start | bytes 9732096 | tf_op jit(solution)/shard_map/reduce_scatter | solution.py:470
  1437.6 23.2 copy-start.28
  1437.6 23.2 copy-start.73
  1437.6 23.2 copy-start.106
  1467.4 583.5 %reduce-scatter.22.cloned.1.call-start = ((), (), s32[]{:S(2)}) async-start(), calls=%async_computation.27 | async-start | bytes 9732096 | tf_op jit(solution)/shard_map/reduce_scatter | solution.py:471
  1552.0 639.7 %reduce-scatter.24.cloned.1.call-start = ((), (), s32[]{:S(2)}) async-start(), calls=%async_computation.28 | async-start | bytes 9732096 | tf_op jit(solution)/shard_map/reduce_scatter | solution.py:472
  1635.8 12.1 copy-start.39
  1635.9 810.5 %reduce-scatter.28.cloned.1.call-start = ((), (), s32[]{:S(2)}) async-start(), calls=%async_computation.30 | async-start | bytes 25952256 | tf_op jit(solution)/shard_map/reduce_scatter | solution.py:370
  1666.9 1031.5 %reduce-scatter.30.cloned.1.call-start = ((), (), s32[]{:S(2)}) async-start(), calls=%async_computation.31 | async-start | bytes 25952256 | tf_op jit(solution)/shard_map/reduce_scatter | solution.py:371
  1695.1 1256.4 %reduce-scatter.32.cloned.1.call-start = ((), (), s32[]{:S(2)}) async-start(), calls=%async_computation.32 | async-start | bytes 25952256 | tf_op jit(solution)/shard_map/reduce_scatter | solution.py:372
  1724.5 12.1 copy-start.93
  1748.1 15.0 slice-start.12
  1748.1 18.1 slice-start.10
  1770.9 43.9 %copy-start.55 = (f32[64,1536]{1,0:T(8,128)S(1)}, f32[64,1536]{1,0:T(8,128)}, u32[]{:S(2)}) copy-start(f32[64,1536]{1,0:T(8,128)} %copy-done.53) | copy-start | bytes 1179652
  1770.9 43.9 %copy-start.58 = (f32[64,1536]{1,0:T(8,128)S(1)}, f32[64,1536]{1,0:T(8,128)}, u32[]{:S(2)}) copy-start(f32[64,1536]{1,0:T(8,128)} %copy-done.56) | copy-start | bytes 1179652
  (116 other events, 545.4 us)
Sparse Core Ops, SparseCore 0:
  10.9 65.6 all-gather.13
  79.5 62.4 all-gather.19
  144.9 62.5 all-gather.17
  209.8 26.0 all-gather.31
  238.2 26.0 all-gather.33
  266.6 25.6 all-gather.15
  294.8 25.6 all-gather.21
  323.4 64.0 all-gather.23
  390.4 93.7 all-gather.25
  486.9 94.2 all-gather.27
  584.0 94.2 all-gather.29
  1406.6 52.1 all-reduce.20
  1462.4 38.6 reduce-scatter.11
  1504.6 38.4 reduce-scatter.15
  1546.5 38.4 reduce-scatter.13
  1588.5 38.4 reduce-scatter.17
  1634.2 133.5 reduce-scatter.25
  1774.2 134.5 reduce-scatter.19
  1916.3 134.5 reduce-scatter.21
  2057.2 134.4 reduce-scatter.23
  2199.8 246.4 reduce-scatter.27
  2453.3 244.9 reduce-scatter.29
  2706.5 245.0 reduce-scatter.31
where the time goes:
time: 2970 us; the launch traced here: 2960 us
  waiting for transfers between devices  1660 us (56%)
  other arithmetic  608 us (20%)
  matrix products  320 us (11%)
  local copies, waits for them, and re-layouts  233 us (8%)
  blocking collectives  100 us (3%)
    reduce_scatter x1, waiting for transfers between devices, on_device(): lax.psum_scatter(gate_grad, ('seq', 'ctx'), scatter_dimension=0, tiled=True)  255 us
    reduce_scatter x1, waiting for transfers between devices, on_device(): lax.psum_scatter(down_grad, ('seq', 'ctx'), scatter_dimension=0, tiled=True)  253 us
    reduce_scatter x1, waiting for transfers between devices, on_device(): lax.psum_scatter(up_grad, ('seq', 'ctx'), scatter_dimension=0, tiled=True)  252 us
    convert_element_type x2, other arithmetic, advance(): jnp.where(keep_mask[:, None], score_grad, 0.0).astype(jnp.bfloat16)  247 us
    reduce_scatter x1, waiting for transfers between devices, on_device(): lax.psum_scatter(key_w_grad, ('seq', 'ctx'), scatter_dimension=0, tiled=T...  142 us
    reduce_scatter x1, waiting for transfers between devices, on_device(): lax.psum_scatter(value_w_grad, ('seq', 'ctx'), scatter_dimension=0, tiled...  141 us
    reduce_sum x14, other arithmetic, advance(): jnp.sum(middle * zeroed[:, :, halo_rows - row_tap:halo_rows - row_tap + b...  112 us
    another operation x134, local copies, waits for them, and re-layouts, advance(): jnp.stack(tap_sums, axis=1)  98.7 us
  transfers between devices with their start and end apart: 23, of which 18 were waited for; matrix products, arithmetic and copies ran while one was open for 15% of the time, Pallas kernels for 0%

commit v1 on v0

--- a/solution.py
+++ b/solution.py
@@ -1,10 +1,346 @@
+import functools
+
 import jax
 import jax.numpy as jnp
 from jax import lax
+from jax.experimental import pallas as pl
+from jax.experimental.pallas import tpu as pltpu
 from jax.sharding import PartitionSpec as P
 
 EPSILON = 1e-05
 NEGATIVE = -1e30
+F32 = jnp.float32
+BF16 = jnp.bfloat16
+TILE = 128
+
+
+def nt(left, right):
+    return lax.dot_general(left, right, (((1,), (1,)), ((), ())), preferred_element_type=F32)
+
+
+def tn(left, right):
+    return lax.dot_general(left, right, (((0,), (0,)), ((), ())), preferred_element_type=F32)
+
+
+def nn(left, right):
+    return lax.dot_general(left, right, (((1,), (0,)), ((), ())), preferred_element_type=F32)
+
+
+def natural_rows(blk_ref, m, blk, seq):
+    return [pl.multiple_of(blk_ref[m, b] * blk, blk) for b in range(seq // blk)]
+
+
+def head_lanes(width):
+    return lax.broadcasted_iota(jnp.int32, (1, width), 1) < width // 2
+
+
+def load_heads(blk_ref, m, blk, seq, q_ref, k_ref, v_ref, qm, kf, ks, vn):
+    width = q_ref.shape[1]
+    first = head_lanes(width)
+    kf[0:8, :] = jnp.zeros((8, width), F32)
+    kf[seq : seq + TILE + 8, :] = jnp.zeros((TILE + 8, width), F32)
+    for b, row in enumerate(natural_rows(blk_ref, m, blk, seq)):
+        here = pl.ds(blk * b, blk)
+        q = q_ref[pl.ds(row, blk), :].astype(F32)
+        qm[0, here, :] = jnp.where(first, q, 0.0).astype(BF16)
+        qm[1, here, :] = jnp.where(first, 0.0, q).astype(BF16)
+        kf[pl.ds(blk * b + 5, blk), :] = k_ref[pl.ds(row, blk), :].astype(F32)
+        vn[here, :] = v_ref[pl.ds(row, blk), :]
+    ks[...] = kf[0 : seq + TILE, :].astype(BF16)
+
+
+def scores(qm, ks, h, rb, upto, scale):
+    rows = pl.ds(TILE * rb, TILE)
+    raw = nt(qm[h, rows, :], ks[0 : TILE * upto, :]) * scale
+    key = lax.broadcasted_iota(jnp.int32, raw.shape, 1) - 5
+    row = lax.broadcasted_iota(jnp.int32, raw.shape, 0) + TILE * rb
+    return jnp.where((key >= 0) & (key <= row), raw, 0.0)
+
+
+def head_factor(values, first, dim):
+    squares = values * values
+    own = jnp.sum(jnp.where(first, squares, 0.0), axis=1, keepdims=True)
+    other = jnp.sum(jnp.where(first, 0.0, squares), axis=1, keepdims=True)
+    return jnp.where(
+        first, lax.rsqrt(own / dim + EPSILON), lax.rsqrt(other / dim + EPSILON)
+    )
+
+
+def forward_kernel(
+    seq, blk, rows_tap, keys_tap, scale,
+    blk_ref, ker_ref, mix_ref, gain_ref, q_ref, k_ref, v_ref,
+    z_ref, y_ref, p_ref,
+    qm, kf, ks, vn, shi, slo, thi, tlo, run, logit,
+):
+    m = pl.program_id(0)
+    width = q_ref.shape[1]
+    first = head_lanes(width)
+    tiles = seq // TILE
+
+    @pl.when(m == 0)
+    def _():
+        shi[...] = jnp.zeros(shi.shape, BF16)
+        slo[...] = jnp.zeros(slo.shape, BF16)
+        away = lax.broadcasted_iota(jnp.int32, (2 * TILE, TILE), 0) - lax.broadcasted_iota(
+            jnp.int32, (2 * TILE, TILE), 1
+        )
+        for h in range(2):
+            for a in range(rows_tap):
+                band = jnp.zeros((2 * TILE, TILE), F32)
+                for t in range(keys_tap):
+                    band = jnp.where(away == keys_tap - 1 - t, ker_ref[h, a, t], band)
+                high = band.astype(BF16)
+                thi[h, :, TILE * a : TILE * (a + 1)] = high
+                tlo[h, :, TILE * a : TILE * (a + 1)] = (band - high.astype(F32)).astype(BF16)
+
+    load_heads(blk_ref, m, blk, seq, q_ref, k_ref, v_ref, qm, kf, ks, vn)
+    for h in range(2):
+        for rb in range(tiles):
+            upto = min(rb + 2, tiles + 1)
+            zeroed = scores(qm, ks, h, rb, upto, scale)
+            high = zeroed.astype(BF16)
+            shi[pl.ds(16 + TILE * rb, TILE), 0 : TILE * upto] = high
+            slo[pl.ds(16 + TILE * rb, TILE), 0 : TILE * upto] = (zeroed - high.astype(F32)).astype(BF16)
+        for b in range(tiles):
+            count = seq - TILE * b
+            rows = pl.ds(TILE * b, count + 16)
+            lanes = pl.ds(TILE * b, 2 * TILE)
+            high, low = shi[rows, lanes], slo[rows, lanes]
+            run[0 : count + 16, :] = nn(high, thi[h]) + nn(low, thi[h]) + nn(high, tlo[h])
+            total = run[16 : 16 + count, 0:TILE]
+            for a in range(1, rows_tap):
+                total = total + run[pl.ds(16 - a, count), TILE * a : TILE * (a + 1)]
+            logit[pl.ds(TILE * b, count), TILE * b : TILE * (b + 1)] = total
+        for rb in range(tiles):
+            rows = pl.ds(TILE * rb, TILE)
+            wide = TILE * (rb + 1)
+            value = logit[rows, 0:wide]
+            key = lax.broadcasted_iota(jnp.int32, value.shape, 1)
+            row = lax.broadcasted_iota(jnp.int32, value.shape, 0) + TILE * rb
+            value = jnp.where(key <= row, value, NEGATIVE)
+            weight = jnp.exp(value - jnp.max(value, axis=1, keepdims=True))
+            weight = weight / jnp.sum(weight, axis=1, keepdims=True)
+            lowered = weight.astype(BF16)
+            p_ref[0, h, rows, 0:wide] = lowered
+            y_ref[0, h, rows, :] = nn(lowered, vn[0:wide, :])
+    out = mix_ref[0:1, :] * y_ref[0, 0] + mix_ref[1:2, :] * y_ref[0, 1]
+    normed = out * head_factor(out, first, width // 2)
+    final = (normed * gain_ref[...]).astype(BF16)
+    for b, row in enumerate(natural_rows(blk_ref, m, blk, seq)):
+        z_ref[pl.ds(row, blk), :] = final[blk * b : blk * (b + 1), :]
+
+
+def backward_kernel(
+    seq, blk, rows_tap, keys_tap, scale,
+    blk_ref, ker_ref, mix_ref, gain_ref, q_ref, k_ref, v_ref, zg_ref, y_ref, p_ref,
+    ql_ref, kl_ref, vl_ref, gg_ref, hm_ref, kg_ref,
+    qm, kf, ks, vn, sb, up, zn, yl, cg, cs, eb, qa, ka, acc,
+):
+    m = pl.program_id(0)
+    width = q_ref.shape[1]
+    first = head_lanes(width)
+    tiles = seq // TILE
+    wide_u = 3 * TILE
+    span = keys_tap - 1
+    lanes_all = rows_tap * TILE
+
+    @pl.when(m == 0)
+    def _():
+        gg_ref[...] = jnp.zeros(gg_ref.shape, F32)
+        hm_ref[...] = jnp.zeros(hm_ref.shape, F32)
+        acc[...] = jnp.zeros(acc.shape, F32)
+        cg[...] = jnp.zeros(cg.shape, F32)
+        cs[...] = jnp.zeros(cs.shape, BF16)
+        eb[...] = jnp.zeros(eb.shape, BF16)
+        sb[...] = jnp.zeros(sb.shape, BF16)
+        away = lax.broadcasted_iota(jnp.int32, (wide_u, 2 * TILE), 0) - lax.broadcasted_iota(
+            jnp.int32, (wide_u, 2 * TILE), 1
+        )
+        for h in range(2):
+            for a in range(rows_tap):
+                band = jnp.zeros((wide_u, 2 * TILE), F32)
+                for t in range(keys_tap):
+                    band = jnp.where(away == TILE - span + t, ker_ref[h, a, t], band)
+                up[h, wide_u * a : wide_u * (a + 1), :] = band.astype(BF16)
+
+    load_heads(blk_ref, m, blk, seq, q_ref, k_ref, v_ref, qm, kf, ks, vn)
+    places = natural_rows(blk_ref, m, blk, seq)
+    for b, row in enumerate(places):
+        zn[pl.ds(blk * b, blk), :] = zg_ref[pl.ds(row, blk), :].astype(F32)
+    dim = width // 2
+    y0, y1 = y_ref[0, 0], y_ref[0, 1]
+    out = mix_ref[0:1, :] * y0 + mix_ref[1:2, :] * y1
+    factor = head_factor(out, first, dim)
+    normed = out * factor
+    upstream = zn[...]
+    gg_ref[...] += jnp.sum(upstream * normed, axis=0, keepdims=True)
+    scaled = upstream * gain_ref[...]
+    both = scaled * normed
+    own = jnp.sum(jnp.where(first, both, 0.0), axis=1, keepdims=True) / dim
+    other = jnp.sum(jnp.where(first, 0.0, both), axis=1, keepdims=True) / dim
+    out_grad = factor * (scaled - normed * jnp.where(first, own, other))
+    hm_ref[0:1, :] += jnp.sum(out_grad * y0, axis=0, keepdims=True)
+    hm_ref[1:2, :] += jnp.sum(out_grad * y1, axis=0, keepdims=True)
+    yl[0] = (mix_ref[0:1, :] * out_grad).astype(BF16)
+    yl[1] = (mix_ref[1:2, :] * out_grad).astype(BF16)
+
+    for b in range(tiles):
+        rows = pl.ds(TILE * b, seq - TILE * b)
+        lanes = pl.ds(TILE * b, TILE)
+        part = tn(p_ref[0, 0, rows, lanes], yl[0, rows, :]) + tn(p_ref[0, 1, rows, lanes], yl[1, rows, :])
+        part = part.astype(BF16)
+        for i in range(TILE // blk):
+            vl_ref[pl.ds(places[b * (TILE // blk) + i], blk), :] = part[blk * i : blk * (i + 1), :]
+
+    ka[...] = jnp.zeros(ka.shape, F32)
+    for h in range(2):
+        for rb in range(tiles):
+            rows = pl.ds(TILE * rb, TILE)
+            upto = min(rb + 2, tiles + 1)
+            sb[rows, 0 : TILE * upto] = scores(qm, ks, h, rb, upto, scale).astype(BF16)
+            wide = TILE * (rb + 1)
+            prob = p_ref[0, h, rows, 0:wide].astype(F32)
+            grad = nt(yl[h, rows, :], vn[0:wide, :])
+            both = prob * grad
+            cg[rows, 0:wide] = both - prob * jnp.sum(both, axis=1, keepdims=True)
+        for b in range(tiles):
+            start = max(0, TILE * b - 16)
+            count = seq - start
+            for a in range(rows_tap):
+                cs[pl.ds(start, count), pl.ds(lanes_all * b + TILE * a, TILE)] = cg[
+                    pl.ds(start + a, count), TILE * b : TILE * (b + 1)
+                ].astype(BF16)
+            acc[h] += tn(
+                sb[pl.ds(start, count), pl.ds(TILE * b, 2 * TILE)],
+                cs[pl.ds(start, count), pl.ds(lanes_all * b, lanes_all)],
+            )
+        for b in range(0, tiles + 1, 2):
+            start = max(0, TILE * b - 16)
+            count = seq - start
+            columns = min(2, tiles + 1 - b)
+            left, right = [], []
+            for a in range(rows_tap):
+                for piece in range(columns + 1):
+                    block = b - 1 + piece
+                    if 0 <= block < tiles:
+                        left.append(cs[pl.ds(start, count), pl.ds(lanes_all * block + TILE * a, TILE)])
+                        right.append(
+                            up[h, pl.ds(wide_u * a + TILE * piece, TILE), 0 : TILE * columns]
+                        )
+            grad = nn(jnp.concatenate(left, axis=1), jnp.concatenate(right, axis=0))
+            key = lax.broadcasted_iota(jnp.int32, grad.shape, 1) + TILE * b - 5
+            row = lax.broadcasted_iota(jnp.int32, grad.shape, 0) + start
+            low = jnp.where((key >= 0) & (key <= row), grad, 0.0).astype(BF16)
+            eb[pl.ds(start, count), pl.ds(TILE * b, TILE * columns)] = low
+            ka[pl.ds(TILE * b, TILE * columns), :] += tn(low, qm[h, pl.ds(start, count), :])
+        for rb in range(tiles):
+            rows = pl.ds(TILE * rb, TILE)
+            upto = min(rb + 2, tiles + 1)
+            part = nn(eb[rows, 0 : TILE * upto], ks[0 : TILE * upto, :]) * scale
+            if h == 0:
+                qa[rows, :] = part
+            else:
+                qa[rows, :] = jnp.where(first, qa[rows, :], part)
+    for b, row in enumerate(places):
+        ql_ref[pl.ds(row, blk), :] = qa[pl.ds(blk * b, blk), :].astype(BF16)
+        kl_ref[pl.ds(row, blk), :] = (ka[pl.ds(blk * b + 5, blk), :] * scale).astype(BF16)
+
+    @pl.when(m == pl.num_programs(0) - 1)
+    def _():
+        away = lax.broadcasted_iota(jnp.int32, (2 * TILE, TILE), 0) - lax.broadcasted_iota(
+            jnp.int32, (2 * TILE, TILE), 1
+        )
+        for h in range(2):
+            for a in range(rows_tap):
+                table = acc[h, :, TILE * a : TILE * (a + 1)]
+                for t in range(keys_tap):
+                    at = a * keys_tap + t
+                    kg_ref[h, at : at + 1, :] = jnp.sum(
+                        jnp.where(away == span - t, table, 0.0), axis=0, keepdims=True
+                    )
+
+
+def whole(shape):
+    return pl.BlockSpec(shape, lambda m: (0,) * len(shape))
+
+
+def pair_forward(blk_table, ker, mix, gain, q, k, v, micro, seq, blk, scale):
+    width = q.shape[1]
+    rows_tap, keys_tap = ker.shape[1:]
+    smem = pl.BlockSpec(memory_space=pltpu.SMEM)
+    per = lambda shape: pl.BlockSpec((1,) + shape, lambda m: (m,) + (0,) * len(shape))
+    return pl.pallas_call(
+        functools.partial(forward_kernel, seq, blk, rows_tap, keys_tap, scale),
+        name="pair_forward",
+        grid=(micro,),
+        out_shape=(
+            jax.ShapeDtypeStruct(q.shape, BF16),
+            jax.ShapeDtypeStruct((micro, 2, seq, width), F32),
+            jax.ShapeDtypeStruct((micro, 2, seq, seq), BF16),
+        ),
+        in_specs=[smem, smem, whole(mix.shape), whole(gain.shape)] + [whole(q.shape)] * 3,
+        out_specs=(whole(q.shape), per((2, seq, width)), per((2, seq, seq))),
+        scratch_shapes=[
+            pltpu.VMEM((2, seq, width), BF16),
+            pltpu.VMEM((seq + TILE + 8, width), F32),
+            pltpu.VMEM((seq + TILE, width), BF16),
+            pltpu.VMEM((seq, width), BF16),
+            pltpu.VMEM((seq + 16, seq + TILE), BF16),
+            pltpu.VMEM((seq + 16, seq + TILE), BF16),
+            pltpu.VMEM((2, 2 * TILE, rows_tap * TILE), BF16),
+            pltpu.VMEM((2, 2 * TILE, rows_tap * TILE), BF16),
+            pltpu.VMEM((seq + 16, rows_tap * TILE), F32),
+            pltpu.VMEM((seq, seq), F32),
+        ],
+        compiler_params=pltpu.CompilerParams(vmem_limit_bytes=56 << 20),
+        cost_estimate=pl.CostEstimate(flops=20 * 10**9, transcendentals=10**6, bytes_accessed=8 << 20),
+    )(blk_table, ker, mix, gain, q, k, v)
+
+
+def pair_backward(blk_table, ker, mix, gain, q, k, v, zg, y, p, seq, blk, scale):
+    width = q.shape[1]
+    micro = y.shape[0]
+    rows_tap, keys_tap = ker.shape[1:]
+    tiles = seq // TILE
+    smem = pl.BlockSpec(memory_space=pltpu.SMEM)
+    per = lambda shape: pl.BlockSpec((1,) + shape, lambda m: (m,) + (0,) * len(shape))
+    low = jax.ShapeDtypeStruct(q.shape, BF16)
+    taps = -(-rows_tap * keys_tap // 8) * 8
+    return pl.pallas_call(
+        functools.partial(backward_kernel, seq, blk, rows_tap, keys_tap, scale),
+        name="pair_backward",
+        grid=(micro,),
+        out_shape=(
+            low, low, low,
+            jax.ShapeDtypeStruct((1, width), F32),
+            jax.ShapeDtypeStruct((2, width), F32),
+            jax.ShapeDtypeStruct((2, taps, TILE), F32),
+        ),
+        in_specs=[smem, smem, whole(mix.shape), whole(gain.shape)]
+        + [whole(q.shape)] * 4
+        + [per((2, seq, width)), per((2, seq, seq))],
+        out_specs=(whole(q.shape),) * 3 + (whole((1, width)), whole((2, width)), whole((2, taps, TILE))),
+        scratch_shapes=[
+            pltpu.VMEM((2, seq, width), BF16),
+            pltpu.VMEM((seq + TILE + 8, width), F32),
+            pltpu.VMEM((seq + TILE, width), BF16),
+            pltpu.VMEM((seq, width), BF16),
+            pltpu.VMEM((seq, seq + TILE), BF16),
+            pltpu.VMEM((2, rows_tap * 3 * TILE, 2 * TILE), BF16),
+            pltpu.VMEM((seq, width), F32),
+            pltpu.VMEM((2, seq, width), BF16),
+            pltpu.VMEM((seq + 8, seq), F32),
+            pltpu.VMEM((seq, tiles * rows_tap * TILE), BF16),
+            pltpu.VMEM((seq, seq + TILE), BF16),
+            pltpu.VMEM((seq, width), F32),
+            pltpu.VMEM((seq + TILE, width), F32),
+            pltpu.VMEM((2, 2 * TILE, rows_tap * TILE), F32),
+        ],
+        compiler_params=pltpu.CompilerParams(vmem_limit_bytes=56 << 20),
+        cost_estimate=pl.CostEstimate(flops=30 * 10**9, transcendentals=10**5, bytes_accessed=12 << 20),
+    )(blk_table, ker, mix, gain, q, k, v, zg, y, p)
+
+
 PRECISE = lax.Precision.HIGHEST
 
 
@@ -205,6 +541,18 @@
     return lax.fori_loop(0, block_count, advance, initial)
 
 
+def reorder(selection, rows):
+    return jnp.dot(
+        selection.astype(rows.dtype), rows, precision=PRECISE, preferred_element_type=jnp.float32
+    ).astype(rows.dtype)
+
+
+def pick(table, places):
+    return jnp.stack(
+        [lax.dynamic_index_in_dim(table, places[i], 0, keepdims=False) for i in range(2)]
+    )
+
+
 def accumulate(previous, update):
     return (
         update
@@ -213,7 +561,7 @@
     )
 
 
-def on_device(
+def general_device(
     inputs,
     out_grad,
     pair_index,
@@ -285,29 +633,34 @@
             lax.all_gather(tail_rows, "ctx", axis=0, tiled=True),
         )
         pairs_row = pair_index[batch_index]
-        owner_pair = pairs_row[slot_ids // 2]
+        owner_pair = jnp.repeat(pairs_row, 2)
         block_of_slot = jnp.where(slot_ids % 2 == 0, owner_pair, block_count - 1 - owner_pair)
-        slot_of_block = jnp.argsort(block_of_slot)
-        my_pair = pairs_row[my_index]
+        to_natural = (block_of_slot[None, :] == slot_ids[:, None]).astype(jnp.float32)
+        slot_of_block = jnp.sum(
+            jnp.where(block_of_slot[None, :] == slot_ids[:, None], slot_ids[None, :], 0), axis=1
+        )
+        my_pair = lax.dynamic_index_in_dim(pairs_row, my_index, 0, keepdims=False)
         my_blocks = jnp.stack([my_pair, block_count - 1 - my_pair])
         key_pad = jnp.pad(
-            key_dealt.reshape(block_count, block_rows, model_width)[slot_of_block].reshape(
+            reorder(to_natural, key_dealt.reshape(block_count, -1)).reshape(
                 seq_length, model_width
             ),
             pad_width,
         ).reshape(-1, head_count, head_dim)
         value_pad = jnp.pad(
-            value_dealt.reshape(block_count, block_rows, model_width)[slot_of_block].reshape(
+            reorder(to_natural, value_dealt.reshape(block_count, -1)).reshape(
                 seq_length, model_width
             ),
             pad_width,
         )
-        tail_blocks = tail_dealt.reshape(block_count, halo_rows, model_width)[slot_of_block]
+        tail_blocks = reorder(to_natural, tail_dealt.reshape(block_count, -1)).reshape(
+            block_count, halo_rows, model_width
+        )
         previous = jnp.concatenate(
             [jnp.zeros((1, halo_rows, model_width), jnp.bfloat16), tail_blocks[:-1]], axis=0
         )
         query_ext = jnp.concatenate(
-            [previous[my_blocks], query_proj.reshape(2, block_rows, model_width)], axis=1
+            [pick(previous, my_blocks), query_proj.reshape(2, block_rows, model_width)], axis=1
         ).reshape(2, extended, head_count, head_dim)
         row_pos = (
             my_blocks[:, None] * block_rows
@@ -418,17 +771,17 @@
         kernel_total = kernel_total + kernel_part
         halo_grad = query_grad[:, :halo_rows].reshape(2, halo_rows, model_width)
         own_grad = query_grad[:, halo_rows:].reshape(2, block_rows, model_width)
-        target_slot = slot_of_block[jnp.maximum(my_blocks - 1, 0)]
+        target_slot = pick(slot_of_block, jnp.maximum(my_blocks - 1, 0))
         routing = ((slot_ids[None, :] == target_slot[:, None]) & (my_blocks > 0)[:, None]).astype(
             jnp.float32
         )
         tail_grad = jnp.einsum("ws,wrc->src", routing, halo_grad, precision=PRECISE).reshape(
             block_count * halo_rows, model_width
         )
-        key_back = key_acc.reshape(block_count, block_rows, model_width)[block_of_slot].reshape(
+        key_back = reorder(to_natural.T, key_acc.reshape(block_count, -1)).reshape(
             seq_length, model_width
         )
-        value_back = value_acc.reshape(block_count, block_rows, model_width)[block_of_slot].reshape(
+        value_back = reorder(to_natural.T, value_acc.reshape(block_count, -1)).reshape(
             seq_length, model_width
         )
         key_mine, value_mine, tail_mine = (
@@ -497,6 +850,210 @@
         feed_sums[1],
         feed_sums[2],
         feed_sums[3],
+    )
+
+
+def shared_sum(values, groups):
+    moved = lax.all_to_all(values.astype(BF16), "ctx", 0, 0, tiled=True)
+    parts = moved.reshape(groups, -1, values.shape[1]).astype(F32)
+    return jnp.sum(parts, axis=0)
+
+
+def on_device(
+    inputs,
+    out_grad,
+    pair_index,
+    norm_gain,
+    query_weight,
+    key_weight,
+    value_weight,
+    score_kernel,
+    head_mixing,
+    group_gain,
+    output_weight,
+    second_gain,
+    gate_weight,
+    up_weight,
+    down_weight,
+):
+    groups, planes = lax.axis_size("ctx"), lax.axis_size("seq")
+    heads, width = score_kernel.shape[0], inputs.shape[3]
+    if heads != 2 * groups or (groups * inputs.shape[2]) % TILE:
+        return general_device(
+            inputs, out_grad, pair_index, norm_gain, query_weight, key_weight, value_weight,
+            score_kernel, head_mixing, group_gain, output_weight, second_gain, gate_weight,
+            up_weight, down_weight,
+        )
+    micro, local = inputs.shape[0], inputs.shape[2]
+    blk, seq = local // 2, local * groups
+    blocks = seq // blk
+    pair = width // groups
+    owned = width // (groups * planes)
+    hidden = gate_weight.shape[1]
+    chunk = hidden // (groups * planes)
+    me = lax.axis_index("ctx")
+    tokens_low = inputs.reshape(micro * local, width)
+    grads_low = out_grad.reshape(micro * local, width)
+
+    gains = lax.all_gather(
+        jnp.stack([norm_gain, group_gain, second_gain]), ("seq", "ctx"), axis=1, tiled=True
+    ).astype(F32)
+    gain_first, gain_group, gain_second = gains[0], gains[1], gains[2]
+
+    def split_columns(weight):
+        return jnp.transpose(weight.reshape(owned, groups, pair), (1, 0, 2))
+
+    def split_hidden(weight):
+        return jnp.transpose(weight.reshape(owned, planes, groups, chunk), (2, 0, 1, 3)).reshape(
+            groups, owned, planes * chunk
+        )
+
+    all_tokens = lax.all_gather(tokens_low, "ctx", axis=0, tiled=True)
+    qkv_mine = lax.all_to_all(
+        jnp.concatenate(
+            [split_columns(query_weight), split_columns(key_weight), split_columns(value_weight)],
+            axis=2,
+        ),
+        "ctx", 0, 0, tiled=True,
+    ).reshape(groups * owned, 3 * pair)
+    qkv = lax.all_gather(qkv_mine, "seq", axis=0, tiled=True)
+    feed_mine = lax.all_to_all(
+        jnp.concatenate([split_hidden(gate_weight), split_hidden(up_weight)], axis=2),
+        "ctx", 0, 0, tiled=True,
+    ).reshape(groups * owned, 2 * planes * chunk)
+    out_full = lax.all_gather(output_weight, ("seq", "ctx"), axis=0, tiled=True)
+    feed = lax.all_gather(feed_mine, "seq", axis=0, tiled=True)
+    down = lax.all_gather(down_weight, "seq", axis=0, tiled=True)
+    all_grads = lax.all_gather(grads_low, "ctx", axis=0, tiled=True)
+
+    slots = jnp.arange(blocks, dtype=jnp.int32)
+    owner = jnp.repeat(pair_index, 2, axis=1)
+    block_of_slot = jnp.where(slots % 2 == 0, owner, blocks - 1 - owner)
+    place = (
+        (slots // 2)[None] * (2 * micro)
+        + 2 * jnp.arange(micro, dtype=jnp.int32)[:, None]
+        + (slots % 2)[None]
+    )
+    blk_table = jnp.sum(
+        jnp.where(block_of_slot[:, None, :] == slots[None, :, None], place[:, None, :], 0), axis=2
+    ).astype(jnp.int32)
+    ker = lax.dynamic_slice_in_dim(score_kernel, 2 * me, 2, 0)
+    mix = jnp.repeat(lax.dynamic_slice_in_dim(head_mixing, 2 * me, 2, 0), pair // 2, axis=0).T
+    gain_pair = lax.dynamic_slice_in_dim(gain_group, pair * me, pair, 0)[None]
+    scale = (width // heads) ** (-0.5)
+
+    normed_all, _ = normalize(all_tokens.astype(F32))
+    hidden_all = (normed_all * gain_first).astype(BF16)
+    q, k, v = (
+        jnp.dot(hidden_all, qkv[:, pair * i : pair * (i + 1)], preferred_element_type=F32).astype(BF16)
+        for i in range(3)
+    )
+    mixed, y, prob = pair_forward(blk_table, ker, mix, gain_pair, q, k, v, micro, seq, blk, scale)
+    mixed_tok = jnp.transpose(
+        lax.all_to_all(mixed, "ctx", 0, 0, tiled=True).reshape(groups, -1, pair), (1, 0, 2)
+    ).reshape(-1, width)
+    tokens = tokens_low.astype(F32)
+    residual = tokens + jnp.dot(mixed_tok, out_full, preferred_element_type=F32)
+    normed_second, factor_second = normalize(residual)
+    second_low = (normed_second * gain_second).astype(BF16)
+    second_all = lax.all_gather(second_low, "ctx", axis=0, tiled=True)
+
+    half = planes * chunk
+    both = jnp.dot(second_all, feed, preferred_element_type=F32)
+    gate, up = both[:, :half], both[:, half:]
+    hid_grad = lax.dot_general(all_grads, down, (((1,), (1,)), ((), ())), preferred_element_type=F32)
+    sigmoid = jax.nn.sigmoid(gate)
+    active = (gate * sigmoid * up).astype(BF16)
+    up_low = (hid_grad * gate * sigmoid).astype(BF16)
+    gate_low = (hid_grad * up * sigmoid * (1.0 + gate * (1.0 - sigmoid))).astype(BF16)
+    lows = jnp.concatenate([gate_low, up_low], axis=1)
+    second_part = lax.dot_general(lows, feed, (((1,), (1,)), ((), ())), preferred_element_type=F32)
+    second_grad = shared_sum(second_part, groups)
+    feed_grad = lax.dot_general(second_all, lows, (((0,), (0,)), ((), ())), preferred_element_type=F32)
+    down_grad = lax.dot_general(active, all_grads, (((0,), (0,)), ((), ())), preferred_element_type=F32)
+    layer_part = jnp.dot(active, down, preferred_element_type=F32)
+    layer_out = (residual + shared_sum(layer_part, groups)).astype(BF16)
+
+    residual_part, gain_second_grad = normalize_back(
+        normed_second, factor_second, gain_second, second_grad
+    )
+    residual_grad = grads_low.astype(F32) + residual_part
+    attended_low = residual_grad.astype(BF16)
+    mixed_grad = lax.dot_general(
+        attended_low, out_full, (((1,), (1,)), ((), ())), preferred_element_type=F32
+    ).astype(BF16)
+    mixed_grad = lax.all_to_all(
+        jnp.transpose(mixed_grad.reshape(-1, groups, pair), (1, 0, 2)), "ctx", 0, 0, tiled=True
+    ).reshape(-1, pair)
+    all_attended = lax.all_gather(attended_low, "ctx", axis=0, tiled=True)
+    mixed_rows = lax.all_to_all(
+        jnp.transpose(
+            mixed_tok.reshape(-1, planes, groups, owned), (2, 0, 1, 3)
+        ).reshape(groups, -1, planes * owned),
+        "ctx", 0, 0, tiled=True,
+    ).reshape(-1, planes * owned)
+    out_w_grad = lax.dot_general(
+        mixed_rows, all_attended, (((0,), (0,)), ((), ())), preferred_element_type=F32
+    )
+    q_low, k_low, v_low, group_part, mix_part, ker_part = pair_backward(
+        blk_table, ker, mix, gain_pair, q, k, v, mixed_grad, y, prob, seq, blk, scale
+    )
+    qkv_low = jnp.concatenate([q_low, k_low, v_low], axis=1)
+    hidden_part = lax.dot_general(qkv_low, qkv, (((1,), (1,)), ((), ())), preferred_element_type=F32)
+    hidden_grad = shared_sum(hidden_part, groups)
+    qkv_grad = lax.dot_general(hidden_all, qkv_low, (((0,), (0,)), ((), ())), preferred_element_type=F32)
+    normed_first, factor_first = normalize(tokens)
+    token_part, gain_first_grad = normalize_back(normed_first, factor_first, gain_first, hidden_grad)
+    input_grad = (residual_grad + token_part).astype(BF16)
+
+    def over_planes(value):
+        return lax.psum_scatter(value.astype(BF16), "seq", scatter_dimension=0, tiled=True)
+
+    down_out = over_planes(down_grad).astype(F32)
+    out_w_out = over_planes(out_w_grad).astype(F32)
+    feed_back = lax.all_to_all(over_planes(feed_grad), "ctx", 0, 0, tiled=True)
+    feed_back = jnp.transpose(
+        feed_back.reshape(groups, owned, 2, planes, chunk), (2, 1, 3, 0, 4)
+    ).reshape(2, owned, hidden).astype(F32)
+    qkv_back = lax.all_to_all(over_planes(qkv_grad), "ctx", 0, 0, tiled=True)
+    qkv_back = jnp.transpose(qkv_back.reshape(groups, owned, 3, pair), (2, 1, 0, 3)).reshape(
+        3, owned, width
+    ).astype(F32)
+
+    taps = score_kernel.shape[1] * score_kernel.shape[2]
+    ker_mine = jnp.sum(ker_part, axis=2)[:, :taps]
+    mix_mine = jnp.sum(mix_part.reshape(2, 2, pair // 2), axis=2).T
+    group_all = lax.dynamic_update_slice(jnp.zeros((width,), F32), group_part[0], (pair * me,))
+    ker_all = lax.dynamic_update_slice(jnp.zeros((heads, taps), F32), ker_mine, (2 * me, 0))
+    mix_all = lax.dynamic_update_slice(jnp.zeros((heads, 2), F32), mix_mine, (2 * me, 0))
+    sums = lax.psum(
+        jnp.concatenate(
+            [gain_first_grad, gain_second_grad, group_all, ker_all.reshape(-1), mix_all.reshape(-1)]
+        ),
+        ("seq", "ctx"),
+    )
+    at = (lax.axis_index("seq") * groups + me) * owned
+    gain_outs = [
+        lax.dynamic_slice_in_dim(sums[width * i : width * (i + 1)], at, owned, 0) for i in range(3)
+    ]
+    ker_out = sums[3 * width : 3 * width + heads * taps].reshape(score_kernel.shape)
+    mix_out = sums[3 * width + heads * taps :].reshape(heads, 2)
+    shape = inputs.shape
+    return (
+        layer_out.reshape(shape),
+        input_grad.reshape(shape),
+        gain_outs[0],
+        qkv_back[0],
+        qkv_back[1],
+        qkv_back[2],
+        ker_out,
+        mix_out,
+        gain_outs[2],
+        out_w_out,
+        gain_outs[1],
+        feed_back[0],
+        feed_back[1],
+        down_out,
     )
 
 

time: 2970 us -> 616 us (0.21)
  waiting for transfers between devices: 1660 us -> 235 us
  other arithmetic: 608 us -> 21.3 us
  matrix products: 320 us -> 66.8 us
  local copies, waits for them, and re-layouts: 233 us -> 34.8 us
  blocking collectives: 100 us -> 153 us
  starting transfers between devices: 1.34 us -> 46.1 us
  Pallas kernels: 0 us -> 38.4 us
    reduce_scatter x11 -> x4, waiting for transfers between devices: 1270 us -> 0.01 us  [over_planes(): lax.psum_scatter(value.astype(BF16), 'seq', scatter_dimension=0, tiled=True)]
    dot_general x62 -> x14, matrix products: 320 us -> 66.8 us  [the longest x1 8.31 us: on_device(): both = jnp.dot(second_all, feed, preferred_element_type=F32)]
    convert_element_type x13 -> x6, other arithmetic: 259 us -> 7.91 us  [the longest x1 2.42 us: on_device(): input_grad = (residual_grad + token_part).astype(BF16)]
    all_gather x11 -> x8, waiting for transfers between devices: 360 us -> 199 us  [the longest x1 55.3 us: on_device(): feed = lax.all_gather(feed_mine, 'seq', axis=0, tiled=True)]
    another operation x148 -> x0, local copies, waits for them, and re-layouts: 111 us -> none  [the longest x134 98.7 us: advance(): jnp.stack(tap_sums, axis=1)]
    reduce_sum x17 -> x8, other arithmetic: 114 us -> 8.67 us  [the longest x3 6.13 us: shared_sum(): return jnp.sum(parts, axis=0)]
    mul x5 -> x1, other arithmetic: 102 us -> 0.01 us  [on_device(): 2 * jnp.arange(micro, dtype=jnp.int32)[:, None]]
    reduce_max x2 -> x0, other arithmetic: 90 us -> none  [advance(): new_max = jnp.maximum(running_max, jnp.max(logits, axis=-1))]
  transfers between devices with their start and end apart: 23 -> 19, of which waited for: 18 -> 10; matrix products, arithmetic and copies ran while one was open for 15% -> 18% of each run, Pallas kernels for 0% -> 6%
where the time goes in v1:
time: 616 us; the launch traced here: 610 us
  waiting for transfers between devices  235 us (38%)
  blocking collectives  153 us (25%)
  matrix products  66.8 us (11%)
  starting transfers between devices  46.1 us (7%)
  Pallas kernels  38.4 us (6%)
  local copies, waits for them, and re-layouts  34.8 us (6%)
  other arithmetic  21.3 us (3%)
  between operations  15 us (2%)
    all_gather x1, waiting for transfers between devices, on_device(): feed = lax.all_gather(feed_mine, 'seq', axis=0, tiled=True)  55.3 us
    all_gather x1, blocking collectives, on_device(): lax.all_gather(jnp.stack([norm_gain, group_gain, second_gain]), ('seq', '...  45.4 us
    psum x1, blocking collectives, on_device(): lax.psum(jnp.concatenate([gain_first_grad, gain_second_grad, group_all, k...  40.2 us
    all_to_all x1, blocking collectives, shared_sum(): moved = lax.all_to_all(values.astype(BF16), 'ctx', 0, 0, tiled=True)  39.3 us
    all_gather x1, waiting for transfers between devices, on_device(): second_all = lax.all_gather(second_low, 'ctx', axis=0, tiled=True)  36.2 us
    all_gather x1, waiting for transfers between devices, on_device(): all_grads = lax.all_gather(grads_low, 'ctx', axis=0, tiled=True)  34.8 us
    all_gather x1, waiting for transfers between devices, on_device(): out_full = lax.all_gather(output_weight, ('seq', 'ctx'), axis=0, tiled=True)  32.8 us
    all_to_all x2, waiting for transfers between devices, shared_sum(): moved = lax.all_to_all(values.astype(BF16), 'ctx', 0, 0, tiled=True)  29.5 us
  transfers between devices with their start and end apart: 19, of which 10 were waited for; matrix products, arithmetic and copies ran while one was open for 18% of the time, Pallas kernels for 6%

profile of v1, /device:TPU:9, one launch (start us, length us, event | category | flops | bytes accessed | tf_op | source)
XLA Modules:
  0.0 610.3 jit_solution(15965488646290526335)
XLA Ops:
  11.6 14.0 %all_to_all.74 = bf16[8,48,576]{2,1,0:T(8,128)(2,1)} all-to-all(bf16[8,48,576]{2,1,0:T(8,128)(2,1)S(1)} %pad_maximum_fusion.5), channel_id=1, replica_groups=mesh['seq'=4,'ctx'=8] {'ctx'}, dimensions={0} | all-to-all | bytes 884736 | tf_op jit(solution)/shard_map/all_to_all | solution.py:912
  28.3 5.8 all-to-all-start.2
  34.2 45.4 %all-gather = bf16[32,48,3]{1,2,0:T(4,128)(2,1)S(1)} all-gather(bf16[1,48,3]{1,2,0:T(4,128)(2,1)S(1)} %maximum_bitcast_fusion), channel_id=1, replica_groups=mesh['seq'=4,'ctx'=8] {'seq','ctx'}, dimensions={0}, use_global_device_ids=true | all-gather | bytes 9504 | tf_op jit(solution)/shard_map/all_gather | solution.py:898
  84.1 2.7 fusion
  86.8 11.1 %all-gather.12.cloned.1.call-done = bf16[1536,576]{1,0:T(8,128)(2,1)} async-done(((bf16[384,576]{1,0:T(8,128)(2,1)}), bf16[1536,576]{1,0:T(8,128)(2,1)}) %all-gather.12.cloned.1.call-update) | async-done | bytes 1769488 | tf_op jit(solution)/shard_map/all_gather | solution.py:919
  97.9 3.1 convolution_convert_fusion.10.q_ref
  101.0 1.9 convolution_convert_fusion.8.v_ref
  102.9 2.0 convolution_convert_fusion.9.k_ref
  105.0 14.1 %pair_forward.1 = (bf16[1024,192]{1,0:T(8,128)(2,1)}, f32[2,2,512,192]{3,2,1,0:T(8,128)}, bf16[2,2,512,512]{3,2,1,0:T(8,128)(2,1)}) custom-call(s32[2,16]{1,0:T(2,128)} %select_reduce_fusion.blk_ref, f32[2,6,11]{2,1,0:T(8,128)} %copy.202.ker_ref, f32[2,192]{1,0:T(2,128)} %bitcast.139, f32[1,192]{1,0:T(1,128)} %constant_dynamic-slice_fusion.gain_ref, ...), custom_call_target="tpu_custom_call" | custom-call | flops 20000000000 | bytes 8388608 | tf_op jit(solution)/shard_map/pair_forward/pallas_call | solution.py:272
  119.0 1.3 copy.178
  120.3 14.1 %all_to_all.75 = bf16[8,128,192]{1,2,0:T(8,128)(2,1)S(1)} all-to-all(bf16[8,128,192]{1,2,0:T(8,128)(2,1)S(1)} %copy.178), channel_id=1, replica_groups=mesh['seq'=4,'ctx'=8] {'ctx'}, dimensions={0} | all-to-all | bytes 786432 | tf_op jit(solution)/shard_map/all_to_all | solution.py:953
  134.5 32.8 %all-gather.14.cloned.1.call-done = bf16[1536,1536]{1,0:T(8,128)(2,1)} async-done(((bf16[48,1536]{1,0:T(8,128)(2,1)}), bf16[1536,1536]{1,0:T(8,128)(2,1)}) %all-gather.14.cloned.1.call-update) | async-done | bytes 4718608 | tf_op jit(solution)/shard_map/all_gather | solution.py:924
  167.3 3.2 multiply_reduce_fusion.2
  173.0 55.3 %all-gather.18.cloned.1.call-done = bf16[1536,1024]{1,0:T(8,128)(2,1)} async-done(((bf16[384,1024]{1,0:T(8,128)(2,1)}), bf16[1536,1024]{1,0:T(8,128)(2,1)}) %all-gather.18.cloned.1.call-update) | async-done | bytes 3145744 | tf_op jit(solution)/shard_map/all_gather | solution.py:925
  228.4 36.2 %all-gather.16.cloned.1.call-done = bf16[1024,1536]{1,0:T(8,128)(2,1)} async-done(((bf16[128,1536]{1,0:T(8,128)(2,1)}), bf16[1024,1536]{1,0:T(8,128)(2,1)}) %all-gather.16.cloned.1.call-update) | async-done | bytes 3145744 | tf_op jit(solution)/shard_map/all_gather | solution.py:959
  264.5 8.3 %fusion.31 = f32[1024,1024]{0,1:T(8,128)} fusion(bf16[1024,1536]{1,0:T(8,128)(2,1)} %all-gather.16.cloned.1.call-done, bf16[1536,1024]{1,0:T(8,128)(2,1)} %all-gather.18.cloned.1.call-done), kind=kOutput, calls=%fused_computation.92 | convolution fusion | flops 3221225472 | bytes 10485760 | tf_op jit(solution)/shard_map/dot_general | solution.py:962
  272.8 28.6 %all-gather.20.cloned.1.call-done = bf16[512,1536]{1,0:T(8,128)(2,1)} async-done(((bf16[128,1536]{1,0:T(8,128)(2,1)}), bf16[512,1536]{1,0:T(8,128)(2,1)}) %all-gather.20.cloned.1.call-update) | async-done | bytes 1572880 | tf_op jit(solution)/shard_map/all_gather | solution.py:926
  301.4 34.8 %all-gather.22.cloned.1.call-done = bf16[1024,1536]{1,0:T(8,128)(2,1)} async-done(((bf16[128,1536]{1,0:T(8,128)(2,1)}), bf16[1024,1536]{1,0:T(8,128)(2,1)}) %all-gather.22.cloned.1.call-update) | async-done | bytes 3145744 | tf_op jit(solution)/shard_map/all_gather | solution.py:927
  336.2 7.6 %multiply_convert_fusion.1 = (bf16[1024,512]{0,1:T(8,128)(2,1)}, bf16[1024,512]{0,1:T(8,128)(2,1)}, bf16[1024,512]{0,1:T(8,128)(2,1)S(1)}) fusion(f32[1024,1024]{0,1:T(8,128)} %fusion.31, bf16[1024,1536]{1,0:T(8,128)(2,1)} %all-gather.22.cloned.1.call-done, bf16[512,1536]{1,0:T(8,128)(2,1)} %all-gather.20.cloned.1.call-done), kind=kOutput, calls=%fused_computation.19 | convolution fusion | flops 1619001344 | bytes 12058624 | tf_op jit(solution)/shard_map/dot_general | solution.py:964
  343.7 3.0 convolution_convert_fusion.5
  346.8 7.6 %convolution_convert_fusion.2 = bf16[1536,1024]{1,0:T(8,128)(2,1)} fusion(bf16[1024,1536]{1,0:T(8,128)(2,1)} %all-gather.16.cloned.1.call-done, bf16[1024,512]{0,1:T(8,128)(2,1)} %get-tuple-element.137, bf16[1024,512]{0,1:T(8,128)(2,1)} %get-tuple-element.136), kind=kOutput, calls=%fused_computation.10 | convolution fusion | flops 3226992640 | bytes 8388608 | tf_op jit(solution)/shard_map/dot_general | solution.py:972
  355.7 5.7 convolution_convert_fusion.3
  361.4 39.3 %all_to_all.76 = bf16[8,128,1536]{2,1,0:T(8,128)(2,1)S(1)} all-to-all(bf16[8,128,1536]{2,1,0:T(8,128)(2,1)S(1)} %bitcast.121), channel_id=1, replica_groups=mesh['seq'=4,'ctx'=8] {'ctx'}, dimensions={0} | all-to-all | bytes 6291456 | tf_op jit(solution)/shard_map/all_to_all | solution.py:857
  403.0 4.1 convolution_convert_fusion.7
  408.1 4.7 all-to-all-start.5
  412.8 5.3 convolution_convert_fusion.1
  418.8 6.9 %all-to-all-start.3 = ((bf16[8,128,1536]{2,1,0:T(8,128)(2,1)}), bf16[8,128,1536]{2,1,0:T(8,128)(2,1)}, u32[]{:S(2)}, u32[]{:S(2)}) async-start(bf16[8,128,1536]{2,1,0:T(8,128)(2,1)} %bitcast.120), calls=%async_computation.3 | async-start | bytes 6291456 | tf_op jit(solution)/shard_map/all_to_all | solution.py:857
  426.7 24.3 %pair_backward.1 = (bf16[1024,192]{1,0:T(8,128)(2,1)}, bf16[1024,192]{1,0:T(8,128)(2,1)}, bf16[1024,192]{1,0:T(8,128)(2,1)}, f32[1,192]{1,0:T(1,128)}, f32[2,192]{1,0:T(2,128)}, /*index=5*/f32[2,72,128]{2,1,0:T(8,128)}) custom-call(s32[2,16]{1,0:T(2,128)} %select_reduce_fusion.blk_ref, f32[2,6,11]{2,1,0:T(8,128)} %copy.202.ker_ref, f32[2,192]{1,0:T(2,128)} %bitcast.140, ...), custom_call_target="tpu_custom_call" | custom-call | flops 30000001024 | bytes 12582912 | tf_op jit(solution)/shard_map/pair_backward/pallas_call | solution.py:309
  451.0 5.5 convolution_convert_fusion
  456.6 7.7 %all-to-all-done.3 = bf16[8,128,1536]{2,1,0:T(8,128)(2,1)} async-done(((bf16[8,128,1536]{2,1,0:T(8,128)(2,1)}), bf16[8,128,1536]{2,1,0:T(8,128)(2,1)}, u32[]{:S(2)}, u32[]{:S(2)}) %all-to-all-start.3) | async-done | bytes 3145760 | tf_op jit(solution)/shard_map/all_to_all | solution.py:857
  464.3 8.1 %all-to-all-start.6 = ((bf16[8,128,1536]{2,1,0:T(8,128)(2,1)}), bf16[8,128,1536]{2,1,0:T(8,128)(2,1)}, u32[]{:S(2)}, u32[]{:S(2)}) async-start(bf16[8,128,1536]{2,1,0:T(8,128)(2,1)} %bitcast.119), calls=%async_computation.6 | async-start | bytes 6291456 | tf_op jit(solution)/shard_map/all_to_all | solution.py:857
  472.6 5.9 convolution_convert_fusion.4
  478.5 3.9 copy.200
  484.0 3.3 convert_reduce_fusion.2
  489.2 2.0 convert_element_type.143
  491.1 21.8 %all-to-all-done.6 = bf16[8,128,1536]{2,1,0:T(8,128)(2,1)} async-done(((bf16[8,128,1536]{2,1,0:T(8,128)(2,1)}), bf16[8,128,1536]{2,1,0:T(8,128)(2,1)}, u32[]{:S(2)}, u32[]{:S(2)}) %all-to-all-start.6) | async-done | bytes 3145760 | tf_op jit(solution)/shard_map/all_to_all | solution.py:857
  512.9 6.7 %all-to-all-start.8 = ((bf16[8,128,192]{1,2,0:T(8,128)(2,1)}), bf16[8,128,192]{1,2,0:T(8,128)(2,1)S(1)}, u32[]{:S(2)}, u32[]{:S(2)}) async-start(bf16[8,128,192]{1,2,0:T(8,128)(2,1)} %bitcast.38), calls=%async_computation.8 | async-start | bytes 786432 | tf_op jit(solution)/shard_map/all_to_all | solution.py:989
  519.5 2.4 convert_reduce_fusion
  523.4 1.3 div.37
  524.6 1.4 concatenate.19
  526.0 40.2 %psum.7 = f32[5696]{0:T(1024)} all-reduce(f32[5696]{0:T(1024)} %concatenate.19), channel_id=1, replica_groups=mesh['seq'=4,'ctx'=8] {'seq','ctx'}, use_global_device_ids=true, to_apply=%region_13.14 | all-reduce | flops 5696 | bytes 45568 | tf_op jit(solution)/shard_map/psum | solution.py:1029
  566.3 5.3 all-to-all-start.9
  571.6 3.5 convolution_convert_fusion.6
  575.1 2.4 fusion.11
  577.5 3.1 all-to-all-done.9
  580.6 7.3 %all-to-all-start.7 = ((bf16[8,48,576]{2,1,0:T(8,128)(2,1)}), bf16[8,48,576]{2,1,0:T(8,128)(2,1)S(1)}, u32[]{:S(2)}, u32[]{:S(2)}) async-start(bf16[8,48,576]{2,1,0:T(8,128)(2,1)} %bitcast.132), calls=%async_computation.7 | async-start | bytes 983040 | tf_op jit(solution)/shard_map/all_to_all | solution.py:1018
  591.5 1.9 reshape.344
  601.5 1.6 convert_element_type.137
  (174 shorter events, 36.7 us)
Async XLA Ops:
  7.2 72.6 %copy-start = (f32[16,6,11]{0,1,2:T(8,128)S(1)}, f32[16,6,11]{0,1,2:T(8,128)}, u32[]{:S(2)}) copy-start(f32[16,6,11]{0,1,2:T(8,128)} %param.22) | copy-start | bytes 12676
  7.2 19.2 %copy-start.6 = (bf16[48,4096]{1,0:T(8,128)(2,1)S(1)}, bf16[48,4096]{1,0:T(8,128)(2,1)}, u32[]{:S(2)}) copy-start(bf16[48,4096]{1,0:T(8,128)(2,1)} %param.27) | copy-start | bytes 1179652
  7.2 76.9 %all-gather.10.cloned.1.call-start = ((), (), s32[]{:S(2)}) async-start(), calls=%async_computation.14 | async-start | bytes 3538944 | tf_op jit(solution)/shard_map/all_gather | solution.py:911
  7.9 90.0 %all-gather.12.cloned.1.call-start = ((), (), s32[]{:S(2)}) async-start(), calls=%async_computation.15 | async-start | bytes 2457600 | tf_op jit(solution)/shard_map/all_gather | solution.py:919
  11.3 15.6 %copy-start.7 = (bf16[48,4096]{1,0:T(8,128)(2,1)S(1)}, bf16[48,4096]{1,0:T(8,128)(2,1)}, u32[]{:S(2)}) copy-start(bf16[48,4096]{1,0:T(8,128)(2,1)} %param.28) | copy-start | bytes 1179652
  25.7 141.6 %all-gather.14.cloned.1.call-start = ((), (), s32[]{:S(2)}) async-start(), calls=%async_computation.16 | async-start | bytes 4866048 | tf_op jit(solution)/shard_map/all_gather | solution.py:924
  26.7 7.4 %copy-start.21 = (bf16[48]{0:T(256)(128)(2,1)S(1)}, bf16[48]{0:T(256)(128)(2,1)}, u32[]{:S(2)}) copy-start(bf16[48]{0:T(256)(128)(2,1)} %param.26) | copy-start | bytes 292
  26.7 7.4 %copy-start.22 = (bf16[48]{0:T(256)(128)(2,1)S(1)}, bf16[48]{0:T(256)(128)(2,1)}, u32[]{:S(2)}) copy-start(bf16[48]{0:T(256)(128)(2,1)} %param.24) | copy-start | bytes 292
  26.7 7.4 %copy-start.23 = (bf16[48]{0:T(256)(128)(2,1)S(1)}, bf16[48]{0:T(256)(128)(2,1)}, u32[]{:S(2)}) copy-start(bf16[48]{0:T(256)(128)(2,1)} %param.18) | copy-start | bytes 292
  26.7 53.0 %copy-start.19 = (f32[16,2]{0,1:T(2,128)S(1)}, f32[16,2]{0,1:T(2,128)}, u32[]{:S(2)}) copy-start(f32[16,2]{0,1:T(2,128)} %param.23) | copy-start | bytes 388
  26.9 54.5 %copy-start.18 = (s32[2,8]{1,0:T(2,128)S(1)}, s32[2,8]{1,0:T(2,128)}, u32[]{:S(2)}) copy-start(s32[2,8]{1,0:T(2,128)} %param.17) | copy-start | bytes 196
  28.3 54.6 %all-to-all-start.2 = ((bf16[8,48,1024]{2,1,0:T(8,128)(2,1)}), bf16[8,48,1024]{2,1,0:T(8,128)(2,1)S(1)}, u32[]{:S(2)}, u32[]{:S(2)}) async-start(bf16[8,48,1024]{2,1,0:T(8,128)(2,1)} %pad_maximum_fusion.4), calls=%async_computation.2 | async-start | bytes 1572864 | tf_op jit(solution)/shard_map/all_to_all | solution.py:920
  34.1 194.2 %all-gather.18.cloned.1.call-start = ((), (), s32[]{:S(2)}) async-start(), calls=%async_computation.18 | async-start | bytes 3932160 | tf_op jit(solution)/shard_map/all_gather | solution.py:925
  83.8 180.7 %all-gather.16.cloned.1.call-start = ((), (), s32[]{:S(2)}) async-start(), calls=%async_computation.17 | async-start | bytes 3538944 | tf_op jit(solution)/shard_map/all_gather | solution.py:959
  84.1 13.9 %copy-start.4 = (bf16[1024,1536]{1,0:T(8,128)(2,1)S(1)}, bf16[1024,1536]{1,0:T(8,128)(2,1)}, u32[]{:S(2)}) copy-start(bf16[1024,1536]{1,0:T(8,128)(2,1)} %all-gather.10.cloned.1.call-done) | copy-start | bytes 9437188
  86.8 16.1 %copy-start.14 = (f32[1024]{0:T(1024)}, f32[1024]{0:T(1024)S(1)}, u32[]{:S(2)}) copy-start(f32[1024]{0:T(1024)S(1)} %add_rsqrt_fusion) | copy-start | bytes 12292
  97.9 3.1 copy-start.25
  105.0 62.3 %copy-start.2 = (bf16[2,1,64,1536]{3,2,1,0:T(8,128)(2,1)S(1)}, bf16[2,1,64,1536]{3,2,1,0:T(8,128)(2,1)}, u32[]{:S(2)}) copy-start(bf16[2,1,64,1536]{3,2,1,0:T(8,128)(2,1)} %param.15) | copy-start | bytes 1179652
  170.5 231.5 %copy-start.11 = (f32[128]{0:T(128)}, f32[128]{0:T(128)S(1)}, u32[]{:S(2)}) copy-start(f32[128]{0:T(128)S(1)} %add_rsqrt_fusion.2) | copy-start | bytes 1540
  171.4 130.0 %all-gather.20.cloned.1.call-start = ((), (), s32[]{:S(2)}) async-start(), calls=%async_computation.19 | async-start | bytes 1966080 | tf_op jit(solution)/shard_map/all_gather | solution.py:926
  172.0 164.2 %all-gather.22.cloned.1.call-start = ((), (), s32[]{:S(2)}) async-start(), calls=%async_computation.20 | async-start | bytes 3538944 | tf_op jit(solution)/shard_map/all_gather | solution.py:927
  172.7 316.4 %reduce-scatter.11.cloned.1.call-start = ((), (), s32[]{:S(2)}) async-start(), calls=%async_computation.24 | async-start | bytes 1966080 | tf_op jit(solution)/shard_map/reduce_scatter | solution.py:1010
  336.2 7.6 %copy-start.24 = (bf16[1024,1536]{1,0:T(8,128)(2,1)S(1)}, bf16[1024,1536]{1,0:T(8,128)(2,1)}, u32[]{:S(2)}) copy-start(bf16[1024,1536]{1,0:T(8,128)(2,1)} %all-gather.22.cloned.1.call-done) | copy-start | bytes 9437188
  343.7 3.0 copy-start.27
  346.8 219.5 %reduce-scatter.9.cloned.1.call-start = ((), (), s32[]{:S(2)}) async-start(), calls=%async_computation.23 | async-start | bytes 3932160 | tf_op jit(solution)/shard_map/reduce_scatter | solution.py:1010
  354.4 1.2 copy-start.29
  354.5 217.1 %all-gather.24.cloned.1.call-start = ((), (), s32[]{:S(2)}) async-start(), calls=%async_computation.21 | async-start | bytes 3538944 | tf_op jit(solution)/shard_map/all_gather | solution.py:988
  400.7 1.3 copy-start.3
  402.0 1.0 copy-start.16
  408.1 10.8 %all-to-all-start.5 = ((bf16[8,128,192]{1,2,0:T(8,128)(2,1)}), bf16[8,128,192]{1,2,0:T(8,128)(2,1)S(1)}, u32[]{:S(2)}, u32[]{:S(2)}) async-start(bf16[8,128,192]{1,2,0:T(8,128)(2,1)} %bitcast.24), calls=%async_computation.5 | async-start | bytes 786432 | tf_op jit(solution)/shard_map/all_to_all | solution.py:985
  418.8 45.4 %all-to-all-start.3 = ((bf16[8,128,1536]{2,1,0:T(8,128)(2,1)}), bf16[8,128,1536]{2,1,0:T(8,128)(2,1)}, u32[]{:S(2)}, u32[]{:S(2)}) async-start(bf16[8,128,1536]{2,1,0:T(8,128)(2,1)} %bitcast.120), calls=%async_computation.3 | async-start | bytes 6291456 | tf_op jit(solution)/shard_map/all_to_all | solution.py:857
  426.7 24.3 %copy-start.26 = (bf16[1536,576]{1,0:T(8,128)(2,1)S(1)}, bf16[1536,576]{1,0:T(8,128)(2,1)}, u32[]{:S(2)}) copy-start(bf16[1536,576]{1,0:T(8,128)(2,1)} %all-gather.12.cloned.1.call-done) | copy-start | bytes 5308420
  464.3 8.3 %copy-start.15 = (f32[1024]{0:T(1024)S(1)}, f32[1024]{0:T(1024)}, u32[]{:S(2)}) copy-start(f32[1024]{0:T(1024)} %copy-done.14) | copy-start | bytes 12292
  464.3 8.3 %copy-start.28 = (bf16[1024,192]{1,0:T(8,128)(2,1)S(1)}, bf16[1024,192]{1,0:T(8,128)(2,1)}, u32[]{:S(2)}) copy-start(bf16[1024,192]{1,0:T(8,128)(2,1)} %get-tuple-element.26) | copy-start | bytes 1179652
  464.3 48.6 %all-to-all-start.6 = ((bf16[8,128,1536]{2,1,0:T(8,128)(2,1)}), bf16[8,128,1536]{2,1,0:T(8,128)(2,1)}, u32[]{:S(2)}, u32[]{:S(2)}) async-start(bf16[8,128,1536]{2,1,0:T(8,128)(2,1)} %bitcast.119), calls=%async_computation.6 | async-start | bytes 6291456 | tf_op jit(solution)/shard_map/all_to_all | solution.py:857
  472.4 105.1 %reduce-scatter.13.cloned.1.call-start = ((), (), s32[]{:S(2)}) async-start(), calls=%async_computation.25 | async-start | bytes 2457600 | tf_op jit(solution)/shard_map/reduce_scatter | solution.py:1010
  482.4 4.9 copy-start.9
  482.4 5.7 copy-start.17
  482.4 6.6 %copy-start.20 = (f32[1,192]{1,0:T(1,128)S(1)}, f32[1,192]{1,0:T(1,128)}, u32[]{:S(2)}) copy-start(f32[1,192]{1,0:T(1,128)} %get-tuple-element.29) | copy-start | bytes 2308
  482.6 30.3 %copy-start.12 = (f32[2,64]{1,0:T(2,128)}, f32[2,64]{1,0:T(2,128)S(1)}, u32[]{:S(2)}) copy-start(f32[2,64]{1,0:T(2,128)S(1)} %add_rsqrt_fusion.1) | copy-start | bytes 1540
  489.1 23.7 %copy-start.10 = (f32[1536]{0:T(1024)}, f32[1536]{0:T(1024)S(1)}, u32[]{:S(2)}) copy-start(f32[1536]{0:T(1024)S(1)} %dynamic_update_slice.9) | copy-start | bytes 18436
  512.9 53.4 %all-to-all-start.8 = ((bf16[8,128,192]{1,2,0:T(8,128)(2,1)}), bf16[8,128,192]{1,2,0:T(8,128)(2,1)S(1)}, u32[]{:S(2)}, u32[]{:S(2)}) async-start(bf16[8,128,192]{1,2,0:T(8,128)(2,1)} %bitcast.38), calls=%async_computation.8 | async-start | bytes 786432 | tf_op jit(solution)/shard_map/all_to_all | solution.py:989
  519.5 2.4 copy-start.13
  566.3 14.4 %all-to-all-start.9 = ((bf16[8,48,1024]{2,1,0:T(8,128)(2,1)}), bf16[8,48,1024]{2,1,0:T(8,128)(2,1)}, u32[]{:S(2)}, u32[]{:S(2)}) async-start(bf16[8,48,1024]{2,1,0:T(8,128)(2,1)} %bitcast.128), calls=%async_computation.11 | async-start | bytes 1572864 | tf_op jit(solution)/shard_map/all_to_all | solution.py:1014
  571.6 30.0 %reduce-scatter.7.cloned.1.call-start = ((), (), s32[]{:S(2)}) async-start(), calls=%async_computation.22 | async-start | bytes 737280 | tf_op jit(solution)/shard_map/reduce_scatter | solution.py:1010
  575.0 12.9 %copy-start.8 = (f32[5696]{0:T(1024)S(1)}, f32[5696]{0:T(1024)}, u32[]{:S(2)}) copy-start(f32[5696]{0:T(1024)} %psum.7) | copy-start | bytes 68356
  580.6 15.9 %all-to-all-start.7 = ((bf16[8,48,576]{2,1,0:T(8,128)(2,1)}), bf16[8,48,576]{2,1,0:T(8,128)(2,1)S(1)}, u32[]{:S(2)}, u32[]{:S(2)}) async-start(bf16[8,48,576]{2,1,0:T(8,128)(2,1)} %bitcast.132), calls=%async_computation.7 | async-start | bytes 983040 | tf_op jit(solution)/shard_map/all_to_all | solution.py:1018
  597.3 5.9 copy-start.1
  (1 other events, 0.9 us)
Sparse Core Ops, SparseCore 0:
  9.9 43.9 all-gather.9
  55.5 42.3 all-gather.11
  100.8 66.3 all-gather.13
  169.3 59.0 all-gather.17
  230.7 33.8 all-gather.15
  265.9 35.4 all-gather.19
  303.3 32.8 all-gather.21
  346.9 32.9 reduce-scatter.10
  382.2 60.6 reduce-scatter.8
  445.2 43.4 all-gather.23
  491.1 48.6 reduce-scatter.12
  575.2 18.2 reduce-scatter.6

commit v2 on v1

--- a/solution.py
+++ b/solution.py
@@ -34,18 +34,18 @@
     return lax.broadcasted_iota(jnp.int32, (1, width), 1) < width // 2
 
 
-def load_heads(blk_ref, m, blk, seq, q_ref, k_ref, v_ref, qm, kf, ks, vn):
-    width = q_ref.shape[1]
+def load_heads(blk_ref, m, blk, seq, qkv_ref, qm, kf, ks, vn):
+    width = vn.shape[1]
     first = head_lanes(width)
     kf[0:8, :] = jnp.zeros((8, width), F32)
     kf[seq : seq + TILE + 8, :] = jnp.zeros((TILE + 8, width), F32)
     for b, row in enumerate(natural_rows(blk_ref, m, blk, seq)):
         here = pl.ds(blk * b, blk)
-        q = q_ref[pl.ds(row, blk), :].astype(F32)
+        q = qkv_ref[pl.ds(row, blk), 0:width].astype(F32)
         qm[0, here, :] = jnp.where(first, q, 0.0).astype(BF16)
         qm[1, here, :] = jnp.where(first, 0.0, q).astype(BF16)
-        kf[pl.ds(blk * b + 5, blk), :] = k_ref[pl.ds(row, blk), :].astype(F32)
-        vn[here, :] = v_ref[pl.ds(row, blk), :]
+        kf[pl.ds(blk * b + 5, blk), :] = qkv_ref[pl.ds(row, blk), width : 2 * width].astype(F32)
+        vn[here, :] = qkv_ref[pl.ds(row, blk), 2 * width : 3 * width]
     ks[...] = kf[0 : seq + TILE, :].astype(BF16)
 
 
@@ -68,12 +68,12 @@
 
 def forward_kernel(
     seq, blk, rows_tap, keys_tap, scale,
-    blk_ref, ker_ref, mix_ref, gain_ref, q_ref, k_ref, v_ref,
+    blk_ref, ker_ref, mix_ref, gain_ref, qkv_ref,
     z_ref, y_ref, p_ref,
     qm, kf, ks, vn, shi, slo, thi, tlo, run, logit,
 ):
     m = pl.program_id(0)
-    width = q_ref.shape[1]
+    width = vn.shape[1]
     first = head_lanes(width)
     tiles = seq // TILE
 
@@ -93,7 +93,7 @@
                 thi[h, :, TILE * a : TILE * (a + 1)] = high
                 tlo[h, :, TILE * a : TILE * (a + 1)] = (band - high.astype(F32)).astype(BF16)
 
-    load_heads(blk_ref, m, blk, seq, q_ref, k_ref, v_ref, qm, kf, ks, vn)
+    load_heads(blk_ref, m, blk, seq, qkv_ref, qm, kf, ks, vn)
     for h in range(2):
         for rb in range(tiles):
             upto = min(rb + 2, tiles + 1)
@@ -132,12 +132,12 @@
 
 def backward_kernel(
     seq, blk, rows_tap, keys_tap, scale,
-    blk_ref, ker_ref, mix_ref, gain_ref, q_ref, k_ref, v_ref, zg_ref, y_ref, p_ref,
-    ql_ref, kl_ref, vl_ref, gg_ref, hm_ref, kg_ref,
+    blk_ref, ker_ref, mix_ref, gain_ref, qkv_ref, zg_ref, y_ref, p_ref,
+    low_ref, gg_ref, hm_ref, kg_ref,
     qm, kf, ks, vn, sb, up, zn, yl, cg, cs, eb, qa, ka, acc,
 ):
     m = pl.program_id(0)
-    width = q_ref.shape[1]
+    width = vn.shape[1]
     first = head_lanes(width)
     tiles = seq // TILE
     wide_u = 3 * TILE
@@ -163,7 +163,7 @@
                     band = jnp.where(away == TILE - span + t, ker_ref[h, a, t], band)
                 up[h, wide_u * a : wide_u * (a + 1), :] = band.astype(BF16)
 
-    load_heads(blk_ref, m, blk, seq, q_ref, k_ref, v_ref, qm, kf, ks, vn)
+    load_heads(blk_ref, m, blk, seq, qkv_ref, qm, kf, ks, vn)
     places = natural_rows(blk_ref, m, blk, seq)
     for b, row in enumerate(places):
         zn[pl.ds(blk * b, blk), :] = zg_ref[pl.ds(row, blk), :].astype(F32)
@@ -190,7 +190,7 @@
         part = tn(p_ref[0, 0, rows, lanes], yl[0, rows, :]) + tn(p_ref[0, 1, rows, lanes], yl[1, rows, :])
         part = part.astype(BF16)
         for i in range(TILE // blk):
-            vl_ref[pl.ds(places[b * (TILE // blk) + i], blk), :] = part[blk * i : blk * (i + 1), :]
+            low_ref[pl.ds(places[b * (TILE // blk) + i], blk), 2 * width : 3 * width] = part[blk * i : blk * (i + 1), :]
 
     ka[...] = jnp.zeros(ka.shape, F32)
     for h in range(2):
@@ -242,8 +242,8 @@
             else:
                 qa[rows, :] = jnp.where(first, qa[rows, :], part)
     for b, row in enumerate(places):
-        ql_ref[pl.ds(row, blk), :] = qa[pl.ds(blk * b, blk), :].astype(BF16)
-        kl_ref[pl.ds(row, blk), :] = (ka[pl.ds(blk * b + 5, blk), :] * scale).astype(BF16)
+        low_ref[pl.ds(row, blk), 0:width] = qa[pl.ds(blk * b, blk), :].astype(BF16)
+        low_ref[pl.ds(row, blk), width : 2 * width] = (ka[pl.ds(blk * b + 5, blk), :] * scale).astype(BF16)
 
     @pl.when(m == pl.num_programs(0) - 1)
     def _():
@@ -264,8 +264,9 @@
     return pl.BlockSpec(shape, lambda m: (0,) * len(shape))
 
 
-def pair_forward(blk_table, ker, mix, gain, q, k, v, micro, seq, blk, scale):
-    width = q.shape[1]
+def pair_forward(blk_table, ker, mix, gain, qkv, micro, seq, blk, scale):
+    width = qkv.shape[1] // 3
+    mixed = (qkv.shape[0], width)
     rows_tap, keys_tap = ker.shape[1:]
     smem = pl.BlockSpec(memory_space=pltpu.SMEM)
     per = lambda shape: pl.BlockSpec((1,) + shape, lambda m: (m,) + (0,) * len(shape))
@@ -274,12 +275,12 @@
         name="pair_forward",
         grid=(micro,),
         out_shape=(
-            jax.ShapeDtypeStruct(q.shape, BF16),
+            jax.ShapeDtypeStruct(mixed, BF16),
             jax.ShapeDtypeStruct((micro, 2, seq, width), F32),
             jax.ShapeDtypeStruct((micro, 2, seq, seq), BF16),
         ),
-        in_specs=[smem, smem, whole(mix.shape), whole(gain.shape)] + [whole(q.shape)] * 3,
-        out_specs=(whole(q.shape), per((2, seq, width)), per((2, seq, seq))),
+        in_specs=[smem, smem, whole(mix.shape), whole(gain.shape), whole(qkv.shape)],
+        out_specs=(whole(mixed), per((2, seq, width)), per((2, seq, seq))),
         scratch_shapes=[
             pltpu.VMEM((2, seq, width), BF16),
             pltpu.VMEM((seq + TILE + 8, width), F32),
@@ -294,32 +295,30 @@
         ],
         compiler_params=pltpu.CompilerParams(vmem_limit_bytes=56 << 20),
         cost_estimate=pl.CostEstimate(flops=20 * 10**9, transcendentals=10**6, bytes_accessed=8 << 20),
-    )(blk_table, ker, mix, gain, q, k, v)
-
-
-def pair_backward(blk_table, ker, mix, gain, q, k, v, zg, y, p, seq, blk, scale):
-    width = q.shape[1]
+    )(blk_table, ker, mix, gain, qkv)
+
+
+def pair_backward(blk_table, ker, mix, gain, qkv, zg, y, p, seq, blk, scale):
+    width = qkv.shape[1] // 3
     micro = y.shape[0]
     rows_tap, keys_tap = ker.shape[1:]
     tiles = seq // TILE
     smem = pl.BlockSpec(memory_space=pltpu.SMEM)
     per = lambda shape: pl.BlockSpec((1,) + shape, lambda m: (m,) + (0,) * len(shape))
-    low = jax.ShapeDtypeStruct(q.shape, BF16)
     taps = -(-rows_tap * keys_tap // 8) * 8
     return pl.pallas_call(
         functools.partial(backward_kernel, seq, blk, rows_tap, keys_tap, scale),
         name="pair_backward",
         grid=(micro,),
         out_shape=(
-            low, low, low,
+            jax.ShapeDtypeStruct(qkv.shape, BF16),
             jax.ShapeDtypeStruct((1, width), F32),
             jax.ShapeDtypeStruct((2, width), F32),
             jax.ShapeDtypeStruct((2, taps, TILE), F32),
         ),
-        in_specs=[smem, smem, whole(mix.shape), whole(gain.shape)]
-        + [whole(q.shape)] * 4
+        in_specs=[smem, smem, whole(mix.shape), whole(gain.shape), whole(qkv.shape), whole(zg.shape)]
         + [per((2, seq, width)), per((2, seq, seq))],
-        out_specs=(whole(q.shape),) * 3 + (whole((1, width)), whole((2, width)), whole((2, taps, TILE))),
+        out_specs=(whole(qkv.shape), whole((1, width)), whole((2, width)), whole((2, taps, TILE))),
         scratch_shapes=[
             pltpu.VMEM((2, seq, width), BF16),
             pltpu.VMEM((seq + TILE + 8, width), F32),
@@ -338,7 +337,555 @@
         ],
         compiler_params=pltpu.CompilerParams(vmem_limit_bytes=56 << 20),
         cost_estimate=pl.CostEstimate(flops=30 * 10**9, transcendentals=10**5, bytes_accessed=12 << 20),
-    )(blk_table, ker, mix, gain, q, k, v, zg, y, p)
+    )(blk_table, ker, mix, gain, qkv, zg, y, p)
+
+
+MESH = pl.DeviceIdType.MESH
+CHIPS = (6, 2, 4)
+
+
+def peer(offset):
+    mine = lax.axis_index("ctx")
+    y = (mine // 4 + offset // 4) % 2
+    x = ((mine // 2) % 2 + (offset // 2) % 2) % 2
+    core = (mine % 2 + offset % 2) % 2
+    return y * 4 + x * 2 + core
+
+
+def greet(places):
+    barrier = pltpu.get_barrier_semaphore()
+    for place in places:
+        pl.semaphore_signal(barrier, inc=1, device_id=place, device_id_type=MESH)
+    pl.semaphore_wait(barrier, len(places))
+
+
+def remote(source, target, send, receive, place):
+    return pltpu.make_async_remote_copy(
+        src_ref=source, dst_ref=target, send_sem=send, recv_sem=receive,
+        device_id=place, device_id_type=MESH,
+    )
+
+
+def exchange_start(plane, mine, source, target, sends, receives):
+    copies = [
+        remote(source.at[peer(d)], target.at[mine], sends.at[d], receives.at[d], (plane, peer(d)))
+        for d in (6, 7, 2, 3, 4, 5, 1)
+    ]
+    for copy in copies:
+        copy.start()
+    return copies
+
+
+def spread_start(plane, mine, source, target, sends, receives):
+    copies = {
+        d: remote(source, target.at[mine], sends.at[d], receives.at[d], (plane, peer(d)))
+        for d in CHIPS + (1,)
+    }
+    for copy in copies.values():
+        copy.start()
+    return copies
+
+
+def spread_pass(plane, copies, d, target, sends, receives):
+    copies[d].wait_recv()
+    block = peer(d)
+    copy = remote(target.at[block], target.at[block], sends.at[d + 1], receives.at[d + 1], (plane, peer(1)))
+    copy.start()
+    copies[d + 1] = copy
+
+
+def spread_finish(copies):
+    for d in (1, 3, 5, 7):
+        copies[d].wait_recv()
+    for copy in copies.values():
+        copy.wait_send()
+
+
+def spread(plane, mine, target, sends, receives):
+    copies = spread_start(plane, mine, target.at[mine], target, sends, receives)
+    for d in (2, 4, 6):
+        spread_pass(plane, copies, d, target, sends, receives)
+    spread_finish(copies)
+
+
+def gather_sum_start(plane, part, near, sends, receives):
+    copies = {}
+    for d in CHIPS + (0,):
+        copies[d] = remote(
+            part.at[peer(d + 1)], near.at[d // 2], sends.at[d], receives.at[d], (plane, peer(1))
+        )
+        copies[d].start()
+    return copies
+
+
+def gather_sum_pass(plane, copies, part, near, stage, far, sends, receives):
+    for d in CHIPS:
+        copies[d].wait_recv()
+        stage[d // 2] = (part[peer(d)].astype(F32) + near[d // 2].astype(F32)).astype(BF16)
+        copy = remote(
+            stage.at[d // 2], far.at[d // 2], sends.at[d + 1], receives.at[d + 1], (plane, peer(d))
+        )
+        copy.start()
+        copies[d + 1] = copy
+    copies[0].wait_recv()
+
+
+def gather_sum_finish(copies):
+    for d in (3, 5, 7):
+        copies[d].wait_recv()
+    for copy in copies.values():
+        copy.wait_send()
+
+
+def gather_sum_total(mine, part, near, far):
+    total = part[mine].astype(F32) + near[0].astype(F32)
+    for i in (1, 2, 3):
+        total = total + far[i].astype(F32)
+    return total
+
+
+class Line:
+    def __init__(self, sources, targets, planes, sends, receives):
+        self.sources, self.targets, self.planes = sources, targets, planes
+        self.sends, self.receives = sends, receives
+        self.plane, self.mine = lax.axis_index("seq"), lax.axis_index("ctx")
+
+    def copy(self, i, up, step):
+        block = jnp.clip(self.plane - step if up else self.plane + step, 0, self.planes - 1)
+        next_plane = jnp.clip(self.plane + 1 if up else self.plane - 1, 0, self.planes - 1)
+        at = (i, int(up), step)
+        target = self.targets[i].at[block]
+        source = target if step else self.sources[i]
+        return remote(source, target, self.sends.at[at], self.receives.at[at], (next_plane, self.mine))
+
+    def arrived(self, i, up, step):
+        block = jnp.clip(self.plane - 1 - step if up else self.plane + 1 + step, 0, self.planes - 1)
+        at = (i, int(up), step)
+        target = self.targets[i].at[block]
+        from_plane = jnp.clip(self.plane - 1 if up else self.plane + 1, 0, self.planes - 1)
+        return remote(target, target, self.sends.at[at], self.receives.at[at], (from_plane, self.mine))
+
+    def step(self, step):
+        for up in (True, False):
+            have = self.plane >= step if up else self.plane + step < self.planes
+            more = self.plane + 1 < self.planes if up else self.plane > 0
+            for i in range(len(self.targets)):
+                if step:
+                    @pl.when(have)
+                    def _(i=i, up=up):
+                        self.arrived(i, up, step - 1).wait_recv()
+
+                if step < self.planes - 1:
+                    @pl.when(have & more)
+                    def _(i=i, up=up):
+                        self.copy(i, up, step).start()
+
+    def finish(self):
+        for step in range(self.planes - 1):
+            for up in (True, False):
+                have = self.plane >= step if up else self.plane + step < self.planes
+                more = self.plane + 1 < self.planes if up else self.plane > 0
+                for i in range(len(self.targets)):
+                    @pl.when(have & more)
+                    def _(i=i, up=up, step=step):
+                        self.copy(i, up, step).wait_send()
+
+
+def plane_peers(plane, offsets):
+    return [(plane, peer(d)) for d in offsets]
+
+
+def other_planes(plane, mine, planes):
+    return [((plane + d) % planes, mine) for d in range(1, planes)]
+
+
+class Relay:
+    def __init__(self, target, planes, sends, receives):
+        self.target, self.planes, self.sends, self.receives = target, planes, sends, receives
+        self.plane, self.mine = lax.axis_index("seq"), lax.axis_index("ctx")
+        origin = self.mine // 2
+        self.source = self.plane == origin
+        self.above, self.below = self.plane > origin, self.plane < origin
+        self.up = (self.source | self.above) & (self.plane + 1 < planes)
+        self.down = (self.source | self.below) & (self.plane > 0)
+
+    def copy(self, i, up):
+        place = jnp.clip(self.plane + 1 if up else self.plane - 1, 0, self.planes - 1)
+        at = (int(up), i)
+        block = self.target.at[i]
+        return remote(block, block, self.sends.at[at], self.receives.at[at], (place, self.mine))
+
+    def start(self, i):
+        for up, go in ((True, self.up), (False, self.down)):
+            @pl.when(self.source & go)
+            def _():
+                self.copy(i, up).start()
+
+    def hand_on(self, i):
+        for up, got, go in ((True, self.above, self.up), (False, self.below, self.down)):
+            @pl.when(got)
+            def _():
+                self.copy(i, up).wait_recv()
+
+            @pl.when(got & go)
+            def _():
+                self.copy(i, up).start()
+
+    def finish(self, i):
+        for up, go in ((True, self.up), (False, self.down)):
+            @pl.when(go)
+            def _():
+                self.copy(i, up).wait_send()
+
+
+def enter_kernel(
+    planes, feed, qkv, out_w, gains, tokens, grads,
+    feed_out, qkv_out, out_w_out, gains_out, tokens_out, grads_out,
+    deal_sends, deal_receives, row_sends, row_receives, sends, receives,
+    line_sends, line_receives, relay_sends, relay_receives, local,
+):
+    plane, mine = lax.axis_index("seq"), lax.axis_index("ctx")
+    keep = [
+        pltpu.make_async_copy(qkv.at[mine], qkv_out.at[plane, mine], local.at[0]),
+        pltpu.make_async_copy(gains, gains_out.at[plane, mine], local.at[1]),
+        pltpu.make_async_copy(feed.at[mine], feed_out.at[mine], local.at[2]),
+        pltpu.make_async_copy(tokens, tokens_out.at[mine], local.at[3]),
+        pltpu.make_async_copy(grads, grads_out.at[mine], local.at[4]),
+    ]
+    for copy in keep:
+        copy.start()
+    greet(plane_peers(plane, range(1, 8)) + other_planes(plane, mine, planes))
+    qkv_copies = exchange_start(plane, mine, qkv, qkv_out.at[plane], deal_sends.at[0], deal_receives.at[0])
+    gain_copies = [
+        remote(gains, gains_out.at[plane, mine], deal_sends.at[1, d], deal_receives.at[1, d], (plane, peer(d)))
+        for d in (6, 7, 2, 3, 4, 5, 1)
+    ]
+    for copy in gain_copies:
+        copy.start()
+    owner = 2 * plane + mine // 4
+    here = owner == mine
+    slot = mine % 4
+    send_rows = remote(out_w, out_w_out.at[slot], row_sends, row_receives.at[slot], (plane, owner))
+    keep_rows = pltpu.make_async_copy(out_w, out_w_out.at[slot], local.at[5])
+
+    @pl.when(here)
+    def _():
+        keep_rows.start()
+
+    @pl.when(jnp.logical_not(here))
+    def _():
+        send_rows.start()
+
+    copies = spread_start(plane, mine, tokens, tokens_out, sends.at[0], receives.at[0])
+    keep[0].wait()
+    for copy in qkv_copies:
+        copy.wait_recv()
+    keep[1].wait()
+    for copy in gain_copies:
+        copy.wait_recv()
+    line = Line(
+        [qkv_out.at[plane], gains_out.at[plane]], [qkv_out, gains_out], planes, line_sends, line_receives
+    )
+    line.step(0)
+    relay = Relay(out_w_out, planes, relay_sends, relay_receives)
+
+    @pl.when(here)
+    def _():
+        keep_rows.wait()
+
+    for r in range(4):
+        @pl.when(relay.source & (4 * (mine % 2) + r != mine))
+        def _():
+            remote(out_w, out_w_out.at[r], row_sends, row_receives.at[r], (plane, owner)).wait_recv()
+
+        relay.start(r)
+    for d in (2, 4, 6):
+        spread_pass(plane, copies, d, tokens_out, sends.at[0], receives.at[0])
+    more = spread_start(plane, mine, grads, grads_out, sends.at[1], receives.at[1])
+    line.step(1)
+    deals = exchange_start(plane, mine, feed, feed_out, deal_sends.at[2], deal_receives.at[2])
+    spread_pass(plane, more, 2, grads_out, sends.at[1], receives.at[1])
+    spread_pass(plane, more, 4, grads_out, sends.at[1], receives.at[1])
+    for step in range(2, planes):
+        line.step(step)
+        if step == 2:
+            relay.hand_on(0)
+            spread_pass(plane, more, 6, grads_out, sends.at[1], receives.at[1])
+    for i in range(1, 4):
+        relay.hand_on(i)
+    for i in range(4):
+        relay.finish(i)
+    spread_finish(copies)
+    spread_finish(more)
+    for copy in qkv_copies + gain_copies:
+        copy.wait_send()
+    for copy in deals:
+        copy.wait()
+
+    @pl.when(jnp.logical_not(here))
+    def _():
+        send_rows.wait_send()
+
+    for copy in keep[2:]:
+        copy.wait()
+    line.finish()
+
+
+def inverse_root(values):
+    return lax.rsqrt(jnp.mean(values * values, axis=1, keepdims=True) + EPSILON)
+
+
+def second_kernel(
+    planes, part, tokens, gain, feed, residual, spread_out, feed_out,
+    near, stage, far, rs_sends, rs_receives, sends, receives, line_sends, line_receives, local,
+):
+    plane, mine = lax.axis_index("seq"), lax.axis_index("ctx")
+    keep = pltpu.make_async_copy(feed, feed_out.at[plane], local)
+    keep.start()
+    greet(plane_peers(plane, (1, 2, 4, 6)) + other_planes(plane, mine, planes))
+    copies = gather_sum_start(plane, part, near, rs_sends, rs_receives)
+    line = Line([feed], [feed_out], planes, line_sends, line_receives)
+    line.step(0)
+    gather_sum_pass(plane, copies, part, near, stage, far, rs_sends, rs_receives)
+    gather_sum_finish(copies)
+    line.step(1)
+    value = tokens[...].astype(F32) + gather_sum_total(mine, part, near, far)
+    residual[...] = value
+    spread_out[mine] = (value * inverse_root(value) * gain[...]).astype(BF16)
+    spread(plane, mine, spread_out, sends, receives)
+    for step in range(2, planes):
+        line.step(step)
+    keep.wait()
+    line.finish()
+
+
+def back_through_norm(upstream, values, gain):
+    factor = inverse_root(values)
+    normed = values * factor
+    scaled = upstream * gain
+    grad = factor * (scaled - normed * jnp.mean(scaled * normed, axis=1, keepdims=True))
+    return grad, jnp.sum(upstream * normed, axis=0, keepdims=True)
+
+
+def back_kernel(part, residual, grads, gain, residual_grad, gain_grad, spread_out, near, stage, far, rs_sends, rs_receives, sends, receives):
+    plane, mine = lax.axis_index("seq"), lax.axis_index("ctx")
+    greet(plane_peers(plane, (1, 2, 4, 6)))
+    copies = gather_sum_start(plane, part, near, rs_sends, rs_receives)
+    gather_sum_pass(plane, copies, part, near, stage, far, rs_sends, rs_receives)
+    gather_sum_finish(copies)
+    grad, gain_part = back_through_norm(gather_sum_total(mine, part, near, far), residual[...], gain[...])
+    grad = grad + grads[...].astype(F32)
+    gain_grad[...] = gain_part
+    residual_grad[...] = grad
+    spread_out[mine] = grad.astype(BF16)
+    spread(plane, mine, spread_out, sends, receives)
+
+
+class Fold:
+    def __init__(self, own, stage, landed, planes, sends, receives):
+        self.own, self.stage, self.landed, self.planes = own, stage, landed, planes
+        self.sends, self.receives = sends, receives
+        self.plane, self.mine = lax.axis_index("seq"), lax.axis_index("ctx")
+
+    def copy(self, j, up):
+        place = jnp.clip(self.plane + 1 if up else self.plane - 1, 0, self.planes - 1)
+        at = (int(up), j)
+        return remote(self.stage.at[at], self.landed.at[at], self.sends.at[at], self.receives.at[at], (place, self.mine))
+
+    def advance(self, j, up):
+        active = self.plane < j if up else self.plane > j
+        inner = self.plane > 0 if up else self.plane < self.planes - 1
+
+        @pl.when(active & inner)
+        def _():
+            self.copy(j, up).wait_recv()
+            self.stage[int(up), j] = (
+                self.own[j].astype(F32) + self.landed[int(up), j].astype(F32)
+            ).astype(BF16)
+
+        @pl.when(active & jnp.logical_not(inner))
+        def _():
+            self.stage[int(up), j] = self.own[j]
+
+        @pl.when(active)
+        def _():
+            self.copy(j, up).start()
+
+    def round(self, i):
+        self.advance(self.planes - 1 - i, True)
+        self.advance(i, False)
+
+    def total(self, out):
+        for j in range(self.planes):
+            @pl.when(self.plane == j)
+            def _():
+                value = self.own[j].astype(F32)
+                if j > 0:
+                    self.copy(j, True).wait_recv()
+                    value = value + self.landed[1, j].astype(F32)
+                if j < self.planes - 1:
+                    self.copy(j, False).wait_recv()
+                    value = value + self.landed[0, j].astype(F32)
+                rows = out.shape[1]
+                for p in range(out.shape[0]):
+                    out[p] = value[rows * p : rows * (p + 1), :].astype(BF16)
+
+    def finish(self):
+        for j in range(self.planes):
+            for up in (True, False):
+                @pl.when(self.plane < j if up else self.plane > j)
+                def _():
+                    self.copy(j, up).wait_send()
+
+
+def leave_kernel(
+    planes, part, layer_part, residual, residual_grad, tokens, gain, small, qkv_grad, feed_grad, out_w_grad,
+    input_grad, layer_out, small_out, qkv_out, feed_out, out_w_out,
+    near, stage, far, layer_near, layer_stage, layer_far, small_plane, small_all,
+    fold_stage, fold_landed, qkv_sum, row_stage, row_landed, row_sum,
+    rs_sends, rs_receives, small_sends, small_receives, fold_sends, fold_receives, row_fold_sends, row_fold_receives,
+    deal_sends, deal_receives, row_sends, row_receives, local,
+):
+    plane, mine = lax.axis_index("seq"), lax.axis_index("ctx")
+    keep_feed = pltpu.make_async_copy(feed_grad.at[mine], feed_out.at[mine], local.at[0])
+    keep_feed.start()
+    greet([((plane + dz) % planes, peer(d)) for dz in range(planes) for d in range(8) if dz or d])
+    fold = Fold(qkv_grad, fold_stage, fold_landed, planes, fold_sends, fold_receives)
+    row_fold = Fold(out_w_grad, row_stage, row_landed, planes, row_fold_sends, row_fold_receives)
+    copies = gather_sum_start(plane, part, near, rs_sends.at[0], rs_receives.at[0])
+
+    ends = (plane == 0) | (plane == planes - 1)
+
+    @pl.when(ends)
+    def _():
+        for i in range(planes - 1):
+            fold.round(i)
+            row_fold.round(i)
+
+    layer_copies = gather_sum_start(plane, layer_part, layer_near, rs_sends.at[1], rs_receives.at[1])
+    gather_sum_pass(plane, copies, part, near, stage, far, rs_sends.at[0], rs_receives.at[0])
+
+    @pl.when(jnp.logical_not(ends))
+    def _():
+        for i in range(2):
+            fold.round(i)
+            row_fold.round(i)
+
+    rows = exchange_start(plane, mine, feed_grad, feed_out, deal_sends.at[0], deal_receives.at[0])
+    gather_sum_pass(plane, layer_copies, layer_part, layer_near, layer_stage, layer_far, rs_sends.at[1], rs_receives.at[1])
+
+    @pl.when(jnp.logical_not(ends))
+    def _():
+        for i in range(2, planes - 1):
+            fold.round(i)
+            row_fold.round(i)
+
+    gather_sum_finish(copies)
+    grad, gain_part = back_through_norm(
+        gather_sum_total(mine, part, near, far), tokens[...].astype(F32), gain[...]
+    )
+    small_plane[mine] = small[...]
+    small_plane[mine, 0:1, :] = gain_part
+    near_copies = [
+        remote(small_plane.at[mine], small_plane.at[mine], small_sends.at[0, d], small_receives.at[0, d], (plane, peer(d)))
+        for d in range(1, 8)
+    ]
+    for copy in near_copies:
+        copy.start()
+    input_grad[...] = (residual_grad[...] + grad).astype(BF16)
+    for copy in near_copies:
+        copy.wait()
+    total = small_plane[0]
+    for i in range(1, 8):
+        total = total + small_plane[i]
+    small_all[plane] = total
+    far_copies = [
+        remote(small_all.at[plane], small_all.at[plane], small_sends.at[1, d], small_receives.at[1, d], ((plane + d) % planes, mine))
+        for d in range(1, planes)
+    ]
+    for copy in far_copies:
+        copy.start()
+    row_fold.total(row_sum)
+    owner_plane, owner = mine // 2, 4 * (mine % 2) + plane
+    here = (owner_plane == plane) & (owner == mine)
+    send_rows = remote(row_sum.at[0], out_w_out, row_sends, row_receives, (owner_plane, owner))
+    keep_rows = pltpu.make_async_copy(row_sum.at[0], out_w_out, local.at[1])
+
+    @pl.when(here)
+    def _():
+        keep_rows.start()
+
+    @pl.when(jnp.logical_not(here))
+    def _():
+        send_rows.start()
+
+    fold.total(qkv_sum)
+    keep_qkv = pltpu.make_async_copy(qkv_sum.at[mine], qkv_out.at[mine], local.at[2])
+    keep_qkv.start()
+    rows += exchange_start(plane, mine, qkv_sum, qkv_out, deal_sends.at[1], deal_receives.at[1])
+    gather_sum_finish(layer_copies)
+    layer_out[...] = (residual[...] + gather_sum_total(mine, layer_part, layer_near, layer_far)).astype(BF16)
+    for copy in far_copies:
+        copy.wait()
+    total = small_all[0]
+    for i in range(1, planes):
+        total = total + small_all[i]
+    small_out[...] = total
+    for copy in rows:
+        copy.wait()
+
+    @pl.when(here)
+    def _():
+        keep_rows.wait()
+
+    @pl.when(jnp.logical_not(here))
+    def _():
+        send_rows.wait()
+
+    row_fold.finish()
+    keep_feed.wait()
+    keep_qkv.wait()
+    fold.finish()
+
+
+def finish_kernel(qkv, feed, out_w, down, q_out, k_out, v_out, gate_out, up_out, out_w_out, down_out):
+    groups, _, three = qkv.shape
+    pair = three // 3
+    half = feed.shape[2] // 2
+    planes = half // TILE
+    for c in range(groups):
+        for i, out in enumerate((q_out, k_out, v_out)):
+            out[:, pair * c : pair * (c + 1)] = qkv[c, :, pair * i : pair * (i + 1)].astype(F32)
+        for i, out in enumerate((gate_out, up_out)):
+            for s in range(planes):
+                at = TILE * (groups * s + c)
+                out[:, at : at + TILE] = feed[c, :, half * i + TILE * s : half * i + TILE * (s + 1)].astype(F32)
+    out_w_out[...] = out_w[...].astype(F32)
+    down_out[...] = down[...].astype(F32)
+
+
+DMA = pltpu.SemaphoreType.DMA
+ANYWHERE = pl.BlockSpec(memory_space=pl.ANY)
+ON_CHIP = pl.BlockSpec(memory_space=pltpu.VMEM)
+
+
+def communicate(kernel, name, number, micros, outs, scratch, args, spec, specs=None, out_specs=None):
+    return pl.pallas_call(
+        kernel,
+        name=name,
+        out_shape=tuple(jax.ShapeDtypeStruct(shape, kind) for shape, kind in outs),
+        in_specs=specs or [spec] * len(args),
+        out_specs=out_specs or (spec,) * len(outs),
+        scratch_shapes=scratch,
+        compiler_params=pltpu.CompilerParams(
+            collective_id=number, has_side_effects=True, vmem_limit_bytes=48 << 20
+        ),
+        cost_estimate=pl.CostEstimate(flops=0, transcendentals=0, bytes_accessed=micros * 3500000),
+    )(*args)
+
+
+def sum_scratch(rows, width, count=1):
+    return [pltpu.VMEM((4, rows, width), BF16)] * (3 * count)
 
 
 PRECISE = lax.Precision.HIGHEST
@@ -853,12 +1400,6 @@
     )
 
 
-def shared_sum(values, groups):
-    moved = lax.all_to_all(values.astype(BF16), "ctx", 0, 0, tiled=True)
-    parts = moved.reshape(groups, -1, values.shape[1]).astype(F32)
-    return jnp.sum(parts, axis=0)
-
-
 def on_device(
     inputs,
     out_grad,
@@ -878,7 +1419,7 @@
 ):
     groups, planes = lax.axis_size("ctx"), lax.axis_size("seq")
     heads, width = score_kernel.shape[0], inputs.shape[3]
-    if heads != 2 * groups or (groups * inputs.shape[2]) % TILE:
+    if groups != 8 or heads != 2 * groups or (groups * inputs.shape[2]) % TILE:
         return general_device(
             inputs, out_grad, pair_index, norm_gain, query_weight, key_weight, value_weight,
             score_kernel, head_mixing, group_gain, output_weight, second_gain, gate_weight,
@@ -895,10 +1436,9 @@
     tokens_low = inputs.reshape(micro * local, width)
     grads_low = out_grad.reshape(micro * local, width)
 
-    gains = lax.all_gather(
-        jnp.stack([norm_gain, group_gain, second_gain]), ("seq", "ctx"), axis=1, tiled=True
-    ).astype(F32)
-    gain_first, gain_group, gain_second = gains[0], gains[1], gains[2]
+    packed = jnp.pad(
+        jnp.stack([norm_gain, group_gain, second_gain]).astype(F32), ((0, 5), (0, TILE - owned))
+    )
 
     def split_columns(weight):
         return jnp.transpose(weight.reshape(owned, groups, pair), (1, 0, 2))
@@ -908,23 +1448,33 @@
             groups, owned, planes * chunk
         )
 
-    all_tokens = lax.all_gather(tokens_low, "ctx", axis=0, tiled=True)
-    qkv_mine = lax.all_to_all(
-        jnp.concatenate(
-            [split_columns(query_weight), split_columns(key_weight), split_columns(value_weight)],
-            axis=2,
-        ),
-        "ctx", 0, 0, tiled=True,
-    ).reshape(groups * owned, 3 * pair)
-    qkv = lax.all_gather(qkv_mine, "seq", axis=0, tiled=True)
-    feed_mine = lax.all_to_all(
-        jnp.concatenate([split_hidden(gate_weight), split_hidden(up_weight)], axis=2),
-        "ctx", 0, 0, tiled=True,
-    ).reshape(groups * owned, 2 * planes * chunk)
-    out_full = lax.all_gather(output_weight, ("seq", "ctx"), axis=0, tiled=True)
-    feed = lax.all_gather(feed_mine, "seq", axis=0, tiled=True)
-    down = lax.all_gather(down_weight, "seq", axis=0, tiled=True)
-    all_grads = lax.all_gather(grads_low, "ctx", axis=0, tiled=True)
+    qkv_send = jnp.concatenate(
+        [split_columns(query_weight), split_columns(key_weight), split_columns(value_weight)], axis=2
+    )
+    feed_send = jnp.concatenate([split_hidden(gate_weight), split_hidden(up_weight)], axis=2)
+    rows_all = micro * local
+    feed_mine, qkv, out_rows, gains, all_tokens, all_grads = communicate(
+        functools.partial(enter_kernel, planes), "enter", 1, 60,
+        [
+            (feed_send.shape, BF16),
+            ((planes,) + qkv_send.shape, BF16),
+            ((4, owned, width), BF16),
+            ((planes, groups) + packed.shape, F32),
+            ((groups, rows_all, width), BF16),
+            ((groups, rows_all, width), BF16),
+        ],
+        [DMA((3, groups))] * 2 + [DMA, DMA((4,))] + [DMA((2, groups))] * 2
+        + [DMA((2, 2, planes))] * 2 + [DMA((2, 4))] * 2 + [DMA((6,))],
+        (feed_send, qkv_send, output_weight, packed, tokens_low, grads_low), ANYWHERE,
+    )
+    all_tokens, down_mine = lax.optimization_barrier((all_tokens.reshape(-1, width), down_weight))
+    all_grads = all_grads.reshape(-1, width)
+    down = lax.all_gather(down_mine, "seq", axis=0, tiled=True)
+    gains = jnp.transpose(gains.reshape((groups * planes,) + packed.shape)[:, :3, :owned], (1, 0, 2))
+    gains = gains.reshape(3, width)
+    gain_first, gain_group, gain_second = gains[0:1], gains[1:2], gains[2:3]
+    qkv = qkv.reshape(width, 3 * pair)
+    out_rows = out_rows.reshape(pair, width)
 
     slots = jnp.arange(blocks, dtype=jnp.int32)
     owner = jnp.repeat(pair_index, 2, axis=1)
@@ -939,24 +1489,28 @@
     ).astype(jnp.int32)
     ker = lax.dynamic_slice_in_dim(score_kernel, 2 * me, 2, 0)
     mix = jnp.repeat(lax.dynamic_slice_in_dim(head_mixing, 2 * me, 2, 0), pair // 2, axis=0).T
-    gain_pair = lax.dynamic_slice_in_dim(gain_group, pair * me, pair, 0)[None]
+    gain_pair = lax.dynamic_slice_in_dim(gain_group, pair * me, pair, 1)
     scale = (width // heads) ** (-0.5)
 
     normed_all, _ = normalize(all_tokens.astype(F32))
     hidden_all = (normed_all * gain_first).astype(BF16)
-    q, k, v = (
-        jnp.dot(hidden_all, qkv[:, pair * i : pair * (i + 1)], preferred_element_type=F32).astype(BF16)
-        for i in range(3)
-    )
-    mixed, y, prob = pair_forward(blk_table, ker, mix, gain_pair, q, k, v, micro, seq, blk, scale)
-    mixed_tok = jnp.transpose(
-        lax.all_to_all(mixed, "ctx", 0, 0, tiled=True).reshape(groups, -1, pair), (1, 0, 2)
-    ).reshape(-1, width)
-    tokens = tokens_low.astype(F32)
-    residual = tokens + jnp.dot(mixed_tok, out_full, preferred_element_type=F32)
-    normed_second, factor_second = normalize(residual)
-    second_low = (normed_second * gain_second).astype(BF16)
-    second_all = lax.all_gather(second_low, "ctx", axis=0, tiled=True)
+    heads_in = jnp.dot(hidden_all, qkv, preferred_element_type=F32).astype(BF16)
+    mixed, y, prob = pair_forward(blk_table, ker, mix, gain_pair, heads_in, micro, seq, blk, scale)
+    attended = jnp.dot(mixed, out_rows, preferred_element_type=F32).astype(BF16)
+    sum_spec = sum_scratch(rows_all, width) + [DMA((groups,))] * 4
+    residual, second_all, feed = communicate(
+        functools.partial(second_kernel, planes), "second", 2, 50,
+        [
+            ((rows_all, width), F32),
+            ((groups, rows_all, width), BF16),
+            ((planes,) + feed_send.shape, BF16),
+        ],
+        sum_spec + [DMA((1, 2, planes))] * 2 + [DMA],
+        (attended.reshape(groups, rows_all, width), tokens_low, gain_second, feed_mine),
+        None, [ON_CHIP] * 3 + [ANYWHERE], (ON_CHIP, ON_CHIP, ANYWHERE),
+    )
+    feed = feed.reshape(width, -1)
+    second_all = second_all.reshape(-1, width)
 
     half = planes * chunk
     both = jnp.dot(second_all, feed, preferred_element_type=F32)
@@ -968,91 +1522,103 @@
     gate_low = (hid_grad * up * sigmoid * (1.0 + gate * (1.0 - sigmoid))).astype(BF16)
     lows = jnp.concatenate([gate_low, up_low], axis=1)
     second_part = lax.dot_general(lows, feed, (((1,), (1,)), ((), ())), preferred_element_type=F32)
-    second_grad = shared_sum(second_part, groups)
     feed_grad = lax.dot_general(second_all, lows, (((0,), (0,)), ((), ())), preferred_element_type=F32)
     down_grad = lax.dot_general(active, all_grads, (((0,), (0,)), ((), ())), preferred_element_type=F32)
+    second_part, feed_grad, down_grad = lax.optimization_barrier(
+        (second_part.astype(BF16), feed_grad.astype(BF16), down_grad.astype(BF16))
+    )
     layer_part = jnp.dot(active, down, preferred_element_type=F32)
-    layer_out = (residual + shared_sum(layer_part, groups)).astype(BF16)
-
-    residual_part, gain_second_grad = normalize_back(
-        normed_second, factor_second, gain_second, second_grad
-    )
-    residual_grad = grads_low.astype(F32) + residual_part
-    attended_low = residual_grad.astype(BF16)
+    residual_grad, gain_second_grad, all_attended = communicate(
+        back_kernel, "back", 3, 45,
+        [((rows_all, width), F32), ((1, width), F32), ((groups, rows_all, width), BF16)],
+        sum_spec,
+        (second_part.reshape(groups, rows_all, width), residual, grads_low, gain_second),
+        ON_CHIP,
+    )
+    all_attended = all_attended.reshape(-1, width)
     mixed_grad = lax.dot_general(
-        attended_low, out_full, (((1,), (1,)), ((), ())), preferred_element_type=F32
+        all_attended, out_rows, (((1,), (1,)), ((), ())), preferred_element_type=F32
     ).astype(BF16)
-    mixed_grad = lax.all_to_all(
-        jnp.transpose(mixed_grad.reshape(-1, groups, pair), (1, 0, 2)), "ctx", 0, 0, tiled=True
-    ).reshape(-1, pair)
-    all_attended = lax.all_gather(attended_low, "ctx", axis=0, tiled=True)
-    mixed_rows = lax.all_to_all(
-        jnp.transpose(
-            mixed_tok.reshape(-1, planes, groups, owned), (2, 0, 1, 3)
-        ).reshape(groups, -1, planes * owned),
-        "ctx", 0, 0, tiled=True,
-    ).reshape(-1, planes * owned)
     out_w_grad = lax.dot_general(
-        mixed_rows, all_attended, (((0,), (0,)), ((), ())), preferred_element_type=F32
-    )
-    q_low, k_low, v_low, group_part, mix_part, ker_part = pair_backward(
-        blk_table, ker, mix, gain_pair, q, k, v, mixed_grad, y, prob, seq, blk, scale
-    )
-    qkv_low = jnp.concatenate([q_low, k_low, v_low], axis=1)
+        mixed, all_attended, (((0,), (0,)), ((), ())), preferred_element_type=F32
+    )
+    qkv_low, group_part, mix_part, ker_part = pair_backward(
+        blk_table, ker, mix, gain_pair, heads_in, mixed_grad, y, prob, seq, blk, scale
+    )
     hidden_part = lax.dot_general(qkv_low, qkv, (((1,), (1,)), ((), ())), preferred_element_type=F32)
-    hidden_grad = shared_sum(hidden_part, groups)
     qkv_grad = lax.dot_general(hidden_all, qkv_low, (((0,), (0,)), ((), ())), preferred_element_type=F32)
-    normed_first, factor_first = normalize(tokens)
-    token_part, gain_first_grad = normalize_back(normed_first, factor_first, gain_first, hidden_grad)
-    input_grad = (residual_grad + token_part).astype(BF16)
-
-    def over_planes(value):
-        return lax.psum_scatter(value.astype(BF16), "seq", scatter_dimension=0, tiled=True)
-
-    down_out = over_planes(down_grad).astype(F32)
-    out_w_out = over_planes(out_w_grad).astype(F32)
-    feed_back = lax.all_to_all(over_planes(feed_grad), "ctx", 0, 0, tiled=True)
-    feed_back = jnp.transpose(
-        feed_back.reshape(groups, owned, 2, planes, chunk), (2, 1, 3, 0, 4)
-    ).reshape(2, owned, hidden).astype(F32)
-    qkv_back = lax.all_to_all(over_planes(qkv_grad), "ctx", 0, 0, tiled=True)
-    qkv_back = jnp.transpose(qkv_back.reshape(groups, owned, 3, pair), (2, 1, 0, 3)).reshape(
-        3, owned, width
-    ).astype(F32)
-
     taps = score_kernel.shape[1] * score_kernel.shape[2]
     ker_mine = jnp.sum(ker_part, axis=2)[:, :taps]
     mix_mine = jnp.sum(mix_part.reshape(2, 2, pair // 2), axis=2).T
-    group_all = lax.dynamic_update_slice(jnp.zeros((width,), F32), group_part[0], (pair * me,))
-    ker_all = lax.dynamic_update_slice(jnp.zeros((heads, taps), F32), ker_mine, (2 * me, 0))
-    mix_all = lax.dynamic_update_slice(jnp.zeros((heads, 2), F32), mix_mine, (2 * me, 0))
-    sums = lax.psum(
-        jnp.concatenate(
-            [gain_first_grad, gain_second_grad, group_all, ker_all.reshape(-1), mix_all.reshape(-1)]
+    row = lax.dynamic_update_slice
+    group_all = row(jnp.zeros((1, width), F32), group_part, (0, pair * me))
+    ker_all = row(jnp.zeros((heads, taps), F32), ker_mine, (2 * me, 0)).reshape(1, -1)
+    mix_all = row(jnp.zeros((heads, 2), F32), mix_mine, (2 * me, 0)).reshape(1, -1)
+    tap_rows = -(-heads * taps // width)
+    taps_all = jnp.pad(ker_all, ((0, 0), (0, tap_rows * width - heads * taps))).reshape(-1, width)
+    mix_all = jnp.pad(mix_all, ((0, 0), (0, width - 2 * heads)))
+    small = jnp.concatenate(
+        [jnp.zeros((1, width), F32), gain_second_grad, group_all, mix_all, taps_all]
+    )
+    small = jnp.pad(small, ((0, -small.shape[0] % 8), (0, 0)))
+    down_sum = lax.psum_scatter(down_grad, "seq", scatter_dimension=0, tiled=True)
+    feed_sum = lax.psum_scatter(feed_grad, "seq", scatter_dimension=0, tiled=True)
+    input_grad, layer_out, sums, qkv_back, feed_back, out_w_back = communicate(
+        functools.partial(leave_kernel, planes), "leave", 4, 60,
+        [
+            ((rows_all, width), BF16),
+            ((rows_all, width), BF16),
+            (small.shape, F32),
+            (qkv_send.shape, BF16),
+            (feed_send.shape, BF16),
+            (output_weight.shape, BF16),
+        ],
+        sum_scratch(rows_all, width, 2)
+        + [pltpu.VMEM((groups,) + small.shape, F32), pltpu.VMEM((planes,) + small.shape, F32)]
+        + [pltpu.VMEM((2, planes, groups * owned, 3 * pair), BF16)] * 2
+        + [pltpu.VMEM(qkv_send.shape, BF16)]
+        + [pltpu.VMEM((2, planes, owned, width), BF16)] * 2
+        + [pltpu.VMEM((1, owned, width), BF16)]
+        + [DMA((2, groups))] * 4
+        + [DMA((2, planes))] * 4
+        + [DMA((2, groups))] * 2
+        + [DMA, DMA, DMA((3,))],
+        (
+            hidden_part.astype(BF16).reshape(groups, rows_all, width),
+            layer_part.astype(BF16).reshape(groups, rows_all, width),
+            residual, residual_grad, tokens_low, gain_first, small,
+            qkv_grad.astype(BF16).reshape(planes, groups * owned, 3 * pair),
+            feed_sum.reshape(feed_send.shape), out_w_grad.astype(BF16).reshape(planes, owned, width),
         ),
-        ("seq", "ctx"),
-    )
+        None, [ON_CHIP] * 8 + [ANYWHERE, ON_CHIP], (ON_CHIP,) * 3 + (ANYWHERE,) * 3,
+    )
+    plain = [(owned, width)] * 3 + [(owned, hidden)] * 2 + [(owned, width), (chunk, width)]
+    q_back, k_back, v_back, gate_back, up_back, out_w_out, down_out = pl.pallas_call(
+        finish_kernel,
+        name="finish",
+        out_shape=tuple(jax.ShapeDtypeStruct(shape, F32) for shape in plain),
+        compiler_params=pltpu.CompilerParams(vmem_limit_bytes=32 << 20),
+    )(qkv_back, feed_back, out_w_back, down_sum)
+
     at = (lax.axis_index("seq") * groups + me) * owned
-    gain_outs = [
-        lax.dynamic_slice_in_dim(sums[width * i : width * (i + 1)], at, owned, 0) for i in range(3)
-    ]
-    ker_out = sums[3 * width : 3 * width + heads * taps].reshape(score_kernel.shape)
-    mix_out = sums[3 * width + heads * taps :].reshape(heads, 2)
+    gain_outs = [lax.dynamic_slice_in_dim(sums[i], at, owned, 0) for i in range(3)]
+    ker_out = sums[4 : 4 + tap_rows].reshape(-1)[: heads * taps].reshape(score_kernel.shape)
+    mix_out = sums[3, : 2 * heads].reshape(heads, 2)
     shape = inputs.shape
     return (
         layer_out.reshape(shape),
         input_grad.reshape(shape),
         gain_outs[0],
-        qkv_back[0],
-        qkv_back[1],
-        qkv_back[2],
+        q_back,
+        k_back,
+        v_back,
         ker_out,
         mix_out,
         gain_outs[2],
         out_w_out,
         gain_outs[1],
-        feed_back[0],
-        feed_back[1],
+        gate_back,
+        up_back,
         down_out,
     )
 

time: 616 us -> 443 us (0.72)
  Pallas kernels: 38.4 us -> 327 us
  waiting for transfers between devices: 235 us -> 0.05 us
  blocking collectives: 153 us -> 0 us
  starting transfers between devices: 46.1 us -> 0.12 us
  other arithmetic: 21.3 us -> 3.81 us
  matrix products: 66.8 us -> 57.8 us
    pallas_call x0 -> x5, Pallas kernels: none -> 288 us  [the longest x4 286 us: communicate(): pl.pallas_call(kernel, name=name, out_shape=tuple((jax.ShapeDtypeStruct(s...]
    all_gather x8 -> x1, waiting for transfers between devices: 199 us -> 0.01 us  [on_device(): down = lax.all_gather(down_mine, 'seq', axis=0, tiled=True)]
    all_to_all x3 -> x0, blocking collectives: 67.4 us -> none  [the longest x1 39.3 us: shared_sum(): moved = lax.all_to_all(values.astype(BF16), 'ctx', 0, 0, tiled=True)]
    all_gather x1 -> x0, blocking collectives: 45.4 us -> none  [on_device(): lax.all_gather(jnp.stack([norm_gain, group_gain, second_gain]), ('seq', '...]
    all_to_all x7 -> x0, starting transfers between devices: 44.8 us -> none  [the longest x2 14.9 us: shared_sum(): moved = lax.all_to_all(values.astype(BF16), 'ctx', 0, 0, tiled=True)]
    psum x1 -> x0, blocking collectives: 40.2 us -> none  [on_device(): lax.psum(jnp.concatenate([gain_first_grad, gain_second_grad, group_all, k...]
    all_to_all x7 -> x0, waiting for transfers between devices: 33.4 us -> none  [the longest x2 29.5 us: shared_sum(): moved = lax.all_to_all(values.astype(BF16), 'ctx', 0, 0, tiled=True)]
    unnamed x66 -> x80, local copies, waits for them, and re-layouts: 7.89 us -> 20 us
  transfers between devices with their start and end apart: 19 -> 3, of which waited for: 10 -> 0; matrix products, arithmetic and copies ran while one was open for 18% -> 11% of each run, Pallas kernels for 6% -> 58%
where the time goes in v2:
time: 443 us; the launch traced here: 438 us
  Pallas kernels  327 us (74%)
  matrix products  57.8 us (13%)
  local copies, waits for them, and re-layouts  33.9 us (8%)
  between operations  14.5 us (3%)
    pallas_call x4, Pallas kernels, communicate(): pl.pallas_call(kernel, name=name, out_shape=tuple((jax.ShapeDtypeStruct(s...  286 us
    pallas_call x1, Pallas kernels, pair_backward(): pl.pallas_call(functools.partial(backward_kernel, seq, blk, rows_tap, key...  24.9 us
    unnamed x80, local copies, waits for them, and re-layouts  20 us
    pallas_call x1, Pallas kernels, pair_forward(): pl.pallas_call(functools.partial(forward_kernel, seq, blk, rows_tap, keys...  14.3 us
  transfers between devices with their start and end apart: 3, of which 0 were waited for; matrix products, arithmetic and copies ran while one was open for 11% of the time, Pallas kernels for 58%

profile of v2, /device:TPU:9, one launch (start us, length us, event | category | flops | bytes accessed | tf_op | source)
XLA Modules:
  0.0 437.7 jit_solution(12929637789705538146)
XLA Ops:
  7.3 1.2 reshape.232
  8.4 1.1 reshape.233
  9.5 1.1 reshape.231
  10.7 1.1 copy.102
  13.1 73.3 %enter.1 = (bf16[8,48,1024]{2,1,0:T(8,128)(2,1)S(1)}, bf16[4,8,48,576]{3,2,1,0:T(8,128)(2,1)S(1)}, bf16[4,48,1536]{2,1,0:T(8,128)(2,1)S(1)}, f32[4,8,8,128]{3,2,...) custom-call(bf16[8,48,1024]{2,1,0:T(8,128)(2,1)S(1)} %pad_maximum_fusion.3.feed, ...), custom_call_target="tpu_custom_call" | custom-call | bytes 210000000 | tf_op jit(solution)/shard_map/enter/pallas_call | solution.py:873
  86.5 1.3 copy-done.16
  88.0 2.6 fusion
  90.8 0.7 copy.100.ker_ref
  91.6 0.7 reshape.226
  92.5 0.6 constant_dynamic-slice_fusion.2.gain_ref
  93.3 0.7 select_reduce_fusion.blk_ref
  93.9 6.2 %convolution_convert_fusion.8.qkv_ref = bf16[1024,576]{1,0:T(8,128)(2,1)} fusion(bf16[1536,576]{1,0:T(8,128)(2,1)} %bitcast.94, bf16[1024,1536]{1,0:T(8,128)(2,1)} %bitcast.99, f32[1536]{0:T(1024)S(1)} %mul.84, f32[1024]{0:T(1024)S(1)} %add_rsqrt_fusion), kind=kOutput, calls=%fused_computation.18 | convolution fusion | flops 1818820608 | bytes 6105088 | tf_op jit(solution)/shard_map/dot_general | solution.py:1497
  100.2 14.3 %pair_forward.1 = (bf16[1024,192]{1,0:T(8,128)(2,1)}, f32[2,2,512,192]{3,2,1,0:T(8,128)}, bf16[2,2,512,512]{3,2,1,0:T(8,128)(2,1)}) custom-call(s32[2,16]{1,0:T(2,128)} %select_reduce_fusion.blk_ref, f32[2,6,11]{2,1,0:T(8,128)} %copy.100.ker_ref, f32[2,192]{1,0:T(2,128)} %bitcast.113, f32[1,192]{1,0:T(1,128)} %constant_dynamic-slice_fusion.2.gain_ref, ...), custom_call_target="tpu_custom_call" | custom-call | flops 20000000000 | bytes 8388608 | tf_op jit(solution)/shard_map/pair_forward/pallas_call | solution.py:273
  114.5 3.7 convolution_convert_fusion.1
  118.2 73.3 %second.1 = (f32[128,1536]{1,0:T(8,128)S(1)}, bf16[8,128,1536]{2,1,0:T(8,128)(2,1)S(1)}, bf16[4,8,48,1024]{3,2,1,0:T(8,128)(2,1)}) custom-call(bf16[8,128,1536]{2,1,0:T(8,128)(2,1)} %bitcast.96, bf16[128,1536]{1,0:T(8,128)(2,1)S(1)} %bitcast.79, f32[1,1536]{1,0:T(1,128)S(1)} %slice.53.gain, bf16[8,48,1024]{2,1,0:T(8,128)(2,1)S(1)} %get-tuple-element.59.feed), custom_call_target="tpu_custom_call" | custom-call | bytes 175000000 | tf_op jit(solution)/shard_map/second/pallas_call | solution.py:873
  191.6 1.7 copy-done.14
  193.3 7.0 %fusion.23 = f32[1024,1024]{0,1:T(8,128)} fusion(bf16[1024,1536]{1,0:T(8,128)(2,1)S(1)} %bitcast.92, bf16[1536,1024]{1,0:T(8,128)(2,1)} %bitcast.120), kind=kOutput, calls=%fused_computation.70 | convolution fusion | flops 3221225472 | bytes 10485760 | tf_op jit(solution)/shard_map/dot_general | solution.py:1516
  200.3 7.3 %multiply_convert_fusion.2 = (bf16[1024,512]{0,1:T(8,128)(2,1)S(1)}, bf16[1024,512]{0,1:T(8,128)(2,1)S(1)}, bf16[1024,512]{0,1:T(8,128)(2,1)}) fusion(f32[1024,1024]{0,1:T(8,128)} %fusion.23, bf16[1024,1536]{1,0:T(8,128)(2,1)} %bitcast.118, bf16[512,1536]{1,0:T(8,128)(2,1)} %all-gather.2.cloned.1.call-done), kind=kOutput, calls=%fused_computation.16 | convolution fusion | flops 1619001344 | bytes 12058624 | tf_op jit(solution)/shard_map/dot_general | solution.py:1518
  207.5 1.0 copy-done.34
  208.8 6.1 %convolution_convert_fusion.3 = bf16[1536,1024]{1,0:T(8,128)(2,1)} fusion(bf16[1024,1536]{1,0:T(8,128)(2,1)S(1)} %bitcast.93, bf16[1024,512]{0,1:T(8,128)(2,1)S(1)} %get-tuple-element.159, bf16[1024,512]{0,1:T(8,128)(2,1)S(1)} %get-tuple-element.158), kind=kOutput, calls=%fused_computation.8 | convolution fusion | flops 3226992640 | bytes 8388608 | tf_op jit(solution)/shard_map/dot_general | solution.py:1525
  214.9 7.9 %convolution_convert_fusion.4 = bf16[1024,1536]{1,0:T(8,128)(2,1)} fusion(bf16[1536,1024]{1,0:T(8,128)(2,1)} %bitcast.121, bf16[1024,512]{0,1:T(8,128)(2,1)} %copy-done.35, bf16[1024,512]{0,1:T(8,128)(2,1)} %copy-done.34), kind=kOutput, calls=%fused_computation.9 | convolution fusion | flops 3226992640 | bytes 8388608 | tf_op jit(solution)/shard_map/dot_general | solution.py:1524
  222.8 3.0 convolution_convert_fusion.6
  226.0 46.7 %back.1 = (f32[128,1536]{1,0:T(8,128)S(1)}, f32[1,1536]{1,0:T(1,128)S(1)}, bf16[8,128,1536]{2,1,0:T(8,128)(2,1)S(1)}) custom-call(bf16[8,128,1536]{2,1,0:T(8,128)(2,1)} %bitcast.101, f32[128,1536]{1,0:T(8,128)S(1)} %get-tuple-element.63.residual, bf16[128,1536]{1,0:T(8,128)(2,1)S(1)} %bitcast.85, f32[1,1536]{1,0:T(1,128)S(1)} %slice.53.gain), custom_call_target="tpu_custom_call" | custom-call | bytes 157500000 | tf_op jit(solution)/shard_map/back/pallas_call | solution.py:873
  272.7 1.7 copy-done.3
  274.4 1.2 convolution_convert_fusion.9
  275.6 1.0 copy.92.zg_ref
  276.6 24.9 %pair_backward.1 = (bf16[1024,576]{1,0:T(8,128)(2,1)}, f32[1,192]{1,0:T(1,128)}, f32[2,192]{1,0:T(2,128)}, f32[2,72,128]{2,1,0:T(8,128)}) custom-call(s32[2,16]{1,0:T(2,128)} %select_reduce_fusion.blk_ref, f32[2,6,11]{2,1,0:T(8,128)} %copy.100.ker_ref, f32[2,192]{1,0:T(2,128)} %bitcast.114, f32[1,192]{1,0:T(1,128)} %constant_dynamic-slice_fusion.2.gain_ref, ...), custom_call_target="tpu_custom_call" | custom-call | flops 30000001024 | bytes 12582912 | tf_op jit(solution)/shard_map/pair_backward/pallas_call | solution.py:309
  301.5 4.9 %convolution_convert_fusion.5 = bf16[1536,576]{0,1:T(8,128)(2,1)} fusion(bf16[1024,576]{1,0:T(8,128)(2,1)} %get-tuple-element.67, bf16[1024,1536]{1,0:T(8,128)(2,1)S(1)} %bitcast.100, f32[1536]{0:T(1024)S(1)} %mul.84, f32[1024]{0:T(1024)S(1)} %add_rsqrt_fusion), kind=kOutput, calls=%fused_computation.10 | convolution fusion | flops 1819115520 | bytes 6105088 | tf_op jit(solution)/shard_map/dot_general | solution.py:1549
  306.4 4.0 copy.94
  311.5 2.9 convolution_convert_fusion.7
  314.4 3.6 convolution_convert_fusion.2
  317.9 4.1 convolution_convert_fusion
  322.1 1.1 copy-done.5
  323.2 92.9 %leave.1 = (bf16[128,1536]{1,0:T(8,128)(2,1)S(1)}, bf16[128,1536]{1,0:T(8,128)(2,1)S(1)}, f32[8,1536]{1,0:T(8,128)S(1)}, bf16[8,48,576]{2,1,0:T(8,128)(2,1)S(1)}...) custom-call(bf16[8,128,1536]{2,1,0:T(8,128)(2,1)} %bitcast.103, bf16[8,128,1536]{2,1,0:T(8,128)(2,1)} %bitcast.102, ...), custom_call_target="tpu_custom_call" | custom-call | bytes 210000000 | tf_op jit(solution)/shard_map/leave/pallas_call | solution.py:873
  416.1 0.8 copy-done.6
  416.9 0.7 copy-done.9
  417.6 0.7 copy-done.10
  418.4 0.7 copy-done.12
  419.2 0.8 copy.97
  420.1 0.6 copy.98
  420.7 0.6 fusion.16
  421.3 0.6 fusion.17
  422.5 1.0 copy-done.7
  423.5 1.0 copy-done.8
  424.5 0.9 copy-done.13
  425.4 2.0 finish.1
  427.4 1.8 copy.124
  429.2 1.8 copy.125
  (120 shorter events, 4.5 us)
Async XLA Ops:
  7.2 83.5 %copy-start = (f32[16,6,11]{0,1,2:T(8,128)S(1)}, f32[16,6,11]{0,1,2:T(8,128)}, u32[]{:S(2)}) copy-start(f32[16,6,11]{0,1,2:T(8,128)} %param.22) | copy-start | bytes 12676
  7.2 5.0 %copy-start.20 = (bf16[48,4096]{1,0:T(8,128)(2,1)S(1)}, bf16[48,4096]{1,0:T(8,128)(2,1)}, u32[]{:S(2)}) copy-start(bf16[48,4096]{1,0:T(8,128)(2,1)} %param.28) | copy-start | bytes 1179652
  7.2 193.0 %all-gather.2.cloned.1.call-start = ((), (), s32[]{:S(2)}) async-start(), calls=%async_computation.2 | async-start | bytes 1966080 | tf_op jit(solution)/shard_map/all_gather | solution.py:1472
  11.9 1.0 copy-start.26
  11.9 1.0 copy-start.27
  11.9 1.0 copy-start.28
  12.0 1.0 copy-start.2
  12.0 1.1 copy-start.4
  12.0 1.1 copy-start.11
  13.1 78.4 %copy-start.25 = (f32[16,2]{0,1:T(2,128)S(1)}, f32[16,2]{0,1:T(2,128)}, u32[]{:S(2)}) copy-start(f32[16,2]{0,1:T(2,128)} %param.23) | copy-start | bytes 388
  13.1 79.2 %copy-start.23 = (s32[2,8]{1,0:T(2,128)S(1)}, s32[2,8]{1,0:T(2,128)}, u32[]{:S(2)}) copy-start(s32[2,8]{1,0:T(2,128)} %param.17) | copy-start | bytes 196
  86.5 1.3 copy-start.16
  87.8 234.3 %reduce-scatter.3.cloned.1.call-start = ((), (), s32[]{:S(2)}) async-start(), calls=%async_computation.3 | async-start | bytes 3932160 | tf_op jit(solution)/shard_map/reduce_scatter | solution.py:1565
  191.6 1.7 copy-start.14
  200.3 8.6 %copy-start.15 = (bf16[8,128,1536]{2,1,0:T(8,128)(2,1)S(1)}, bf16[8,128,1536]{2,1,0:T(8,128)(2,1)}, u32[]{:S(2)}) copy-start(bf16[8,128,1536]{2,1,0:T(8,128)(2,1)} %copy-done.14) | copy-start | bytes 9437188
  207.5 1.0 copy-start.34
  207.5 1.3 copy-start.35
  214.9 7.9 %copy-start.29 = (bf16[8,128,1536]{2,1,0:T(8,128)(2,1)S(1)}, bf16[8,128,1536]{2,1,0:T(8,128)(2,1)}, u32[]{:S(2)}) copy-start(bf16[8,128,1536]{2,1,0:T(8,128)(2,1)} %get-tuple-element.55) | copy-start | bytes 9437188
  214.9 7.9 %copy-start.31 = (bf16[1024,512]{0,1:T(8,128)(2,1)S(1)}, bf16[1024,512]{0,1:T(8,128)(2,1)}, u32[]{:S(2)}) copy-start(bf16[1024,512]{0,1:T(8,128)(2,1)} %get-tuple-element.160) | copy-start | bytes 3145732
  225.8 196.7 %reduce-scatter.5.cloned.1.call-start = ((), (), s32[]{:S(2)}) async-start(), calls=%async_computation.4 | async-start | bytes 1966080 | tf_op jit(solution)/shard_map/reduce_scatter | solution.py:1564
  272.7 1.7 copy-start.3
  276.6 24.9 %copy-start.19 = (bf16[8,128,1536]{2,1,0:T(8,128)(2,1)S(1)}, bf16[8,128,1536]{2,1,0:T(8,128)(2,1)}, u32[]{:S(2)}) copy-start(bf16[8,128,1536]{2,1,0:T(8,128)(2,1)} %get-tuple-element.52) | copy-start | bytes 9437188
  306.4 4.0 copy-start.21
  306.4 4.2 copy-start.22
  306.4 4.6 %copy-start.24 = (f32[1,192]{1,0:T(1,128)S(1)}, f32[1,192]{1,0:T(1,128)}, u32[]{:S(2)}) copy-start(f32[1,192]{1,0:T(1,128)} %get-tuple-element.70) | copy-start | bytes 2308
  306.4 5.0 %copy-start.18 = (bf16[1024,192]{1,0:T(8,128)(2,1)S(1)}, bf16[1024,192]{1,0:T(8,128)(2,1)}, u32[]{:S(2)}) copy-start(bf16[1024,192]{1,0:T(8,128)(2,1)} %get-tuple-element.57) | copy-start | bytes 1179652
  311.4 2.9 copy-start.30
  311.4 2.9 copy-start.32
  314.3 3.6 copy-start.17
  314.4 3.6 copy-start.33
  322.1 1.1 copy-start.5
  323.2 107.7 %copy-start.1 = (f32[16,6,11]{0,1,2:T(8,128)S(1)}, f32[16,6,11]{0,1,2:T(8,128)}, u32[]{:S(2)}) copy-start(f32[16,6,11]{0,1,2:T(8,128)} %param.22) | copy-start | bytes 12676
  416.1 0.8 copy-start.6
  416.9 0.7 copy-start.9
  417.6 0.7 copy-start.10
  418.4 0.7 copy-start.12
  422.5 1.0 copy-start.7
  423.5 1.0 copy-start.8
  424.5 0.9 copy-start.13
Sparse Core Ops, SparseCore 0:
  87.9 44.4 all-gather.1
  225.9 60.1 reduce-scatter.2
  288.4 33.8 reduce-scatter.4

commit v3 on v2

--- a/solution.py
+++ b/solution.py
@@ -125,7 +125,7 @@
             y_ref[0, h, rows, :] = nn(lowered, vn[0:wide, :])
     out = mix_ref[0:1, :] * y_ref[0, 0] + mix_ref[1:2, :] * y_ref[0, 1]
     normed = out * head_factor(out, first, width // 2)
-    final = (normed * gain_ref[...]).astype(BF16)
+    final = (normed * gain_ref[1:2, :]).astype(BF16)
     for b, row in enumerate(natural_rows(blk_ref, m, blk, seq)):
         z_ref[pl.ds(row, blk), :] = final[blk * b : blk * (b + 1), :]
 
@@ -174,7 +174,7 @@
     normed = out * factor
     upstream = zn[...]
     gg_ref[...] += jnp.sum(upstream * normed, axis=0, keepdims=True)
-    scaled = upstream * gain_ref[...]
+    scaled = upstream * gain_ref[1:2, :]
     both = scaled * normed
     own = jnp.sum(jnp.where(first, both, 0.0), axis=1, keepdims=True) / dim
     other = jnp.sum(jnp.where(first, 0.0, both), axis=1, keepdims=True) / dim
@@ -341,7 +341,6 @@
 
 
 MESH = pl.DeviceIdType.MESH
-CHIPS = (6, 2, 4)
 
 
 def peer(offset):
@@ -376,72 +375,116 @@
     return copies
 
 
-def spread_start(plane, mine, source, target, sends, receives):
-    copies = {
-        d: remote(source, target.at[mine], sends.at[d], receives.at[d], (plane, peer(d)))
-        for d in CHIPS + (1,)
-    }
-    for copy in copies.values():
+class Spread:
+    def __init__(self, source, target, sends, receives):
+        self.plane, self.mine = lax.axis_index("seq"), lax.axis_index("ctx")
+        self.source, self.target, self.sends, self.receives = source, target, sends, receives
+        self.copies = {}
+        half = target.shape[1] // 2
+        self.first, self.second = pl.ds(0, half), pl.ds(half, half)
+
+    def send(self, key, source, target, offset):
+        copy = remote(source, target, self.sends.at[key], self.receives.at[key], (self.plane, peer(offset)))
         copy.start()
-    return copies
-
-
-def spread_pass(plane, copies, d, target, sends, receives):
-    copies[d].wait_recv()
-    block = peer(d)
-    copy = remote(target.at[block], target.at[block], sends.at[d + 1], receives.at[d + 1], (plane, peer(1)))
-    copy.start()
-    copies[d + 1] = copy
-
-
-def spread_finish(copies):
-    for d in (1, 3, 5, 7):
-        copies[d].wait_recv()
-    for copy in copies.values():
-        copy.wait_send()
-
-
-def spread(plane, mine, target, sends, receives):
-    copies = spread_start(plane, mine, target.at[mine], target, sends, receives)
-    for d in (2, 4, 6):
-        spread_pass(plane, copies, d, target, sends, receives)
-    spread_finish(copies)
-
-
-def gather_sum_start(plane, part, near, sends, receives):
-    copies = {}
-    for d in CHIPS + (0,):
-        copies[d] = remote(
-            part.at[peer(d + 1)], near.at[d // 2], sends.at[d], receives.at[d], (plane, peer(1))
-        )
-        copies[d].start()
-    return copies
-
-
-def gather_sum_pass(plane, copies, part, near, stage, far, sends, receives):
-    for d in CHIPS:
-        copies[d].wait_recv()
-        stage[d // 2] = (part[peer(d)].astype(F32) + near[d // 2].astype(F32)).astype(BF16)
-        copy = remote(
-            stage.at[d // 2], far.at[d // 2], sends.at[d + 1], receives.at[d + 1], (plane, peer(d))
-        )
+        self.copies[key] = copy
+
+    def hand_on(self, key, block, offset, rows=None):
+        piece = self.target.at[block] if rows is None else self.target.at[block, rows]
+        self.send(key, piece, piece, offset)
+
+    def start(self):
+        for d in (2, 4, 1):
+            self.send(d, self.source, self.target.at[self.mine], d)
+
+    def near(self):
+        self.copies[2].wait_recv()
+        self.hand_on(6, peer(2), 4, self.first)
+        self.hand_on(3, peer(2), 1)
+        self.copies[4].wait_recv()
+        self.hand_on(0, peer(4), 2, self.second)
+        self.hand_on(5, peer(4), 1)
+
+    def across(self):
+        self.copies[6].wait_recv()
+        self.hand_on(7, peer(6), 1, self.first)
+        self.copies[0].wait_recv()
+        self.hand_on(8, peer(6), 1, self.second)
+
+    def finish(self):
+        for key in (1, 3, 5, 7, 8):
+            self.copies[key].wait_recv()
+        for copy in self.copies.values():
+            copy.wait_send()
+
+
+class PlaneSum:
+    def __init__(self, terms, part, own, near, stage, far, hop, sends, receives):
+        self.plane, self.mine = lax.axis_index("seq"), lax.axis_index("ctx")
+        self.terms, self.part, self.own = terms, part, own
+        self.near, self.stage, self.far, self.hop = near, stage, far, hop
+        self.sends, self.receives = sends, receives
+        self.copies = {}
+        half = part.shape[1] // 2
+        self.first, self.second = pl.ds(0, half), pl.ds(half, half)
+
+    def send(self, key, source, target, offset):
+        copy = remote(source, target, self.sends.at[key], self.receives.at[key], (self.plane, peer(offset)))
         copy.start()
-        copies[d + 1] = copy
-    copies[0].wait_recv()
-
-
-def gather_sum_finish(copies):
-    for d in (3, 5, 7):
-        copies[d].wait_recv()
-    for copy in copies.values():
-        copy.wait_send()
-
-
-def gather_sum_total(mine, part, near, far):
-    total = part[mine].astype(F32) + near[0].astype(F32)
-    for i in (1, 2, 3):
-        total = total + far[i].astype(F32)
-    return total
+        self.copies[key] = copy
+
+    def start(self):
+        self.part[...] = self.terms(1 - self.mine % 2).astype(BF16)
+        for d in (6, 2, 4, 0):
+            self.send(d, self.part.at[peer(d) // 2], self.near.at[d // 2], 1)
+
+    def prepare(self):
+        self.own[...] = self.terms(self.mine % 2)
+
+    def chip_sum(self, d):
+        self.copies[d].wait_recv()
+        self.stage[d // 2] = (self.own[peer(d) // 2] + self.near[d // 2].astype(F32)).astype(BF16)
+
+    def add_hop(self, slot, rows, hop):
+        self.stage[slot, rows, :] = (
+            self.stage[slot, rows, :].astype(F32) + self.hop[hop].astype(F32)
+        ).astype(BF16)
+
+    def run(self):
+        first, second = self.first, self.second
+        self.chip_sum(6)
+        self.send(1, self.stage.at[3, first], self.hop.at[0], 2)
+        self.send(3, self.stage.at[3, second], self.hop.at[1], 4)
+        self.chip_sum(2)
+        self.send(5, self.stage.at[1, first], self.far.at[0, first], 2)
+        self.chip_sum(4)
+        self.send(7, self.stage.at[2, second], self.far.at[1, second], 4)
+        self.copies[1].wait_recv()
+        self.add_hop(2, first, 0)
+        self.send(8, self.stage.at[2, first], self.far.at[1, first], 4)
+        self.copies[3].wait_recv()
+        self.add_hop(1, second, 1)
+        self.send(9, self.stage.at[1, second], self.far.at[0, second], 2)
+
+    def total(self):
+        self.copies[0].wait_recv()
+        value = self.own[self.mine // 2] + self.near[0].astype(F32)
+        for key in (5, 7, 8, 9):
+            self.copies[key].wait_recv()
+        return value + self.far[0].astype(F32) + self.far[1].astype(F32)
+
+    def finish(self):
+        for copy in self.copies.values():
+            copy.wait_send()
+
+
+def terms_of(values, product):
+    chips, _, rows, width = values.shape
+
+    def terms(core):
+        left = values[:, core].reshape(chips * rows, width)
+        return product(left).reshape(chips, rows, -1)
+
+    return terms
 
 
 class Line:
@@ -499,136 +542,178 @@
     return [((plane + d) % planes, mine) for d in range(1, planes)]
 
 
-class Relay:
-    def __init__(self, target, planes, sends, receives):
-        self.target, self.planes, self.sends, self.receives = target, planes, sends, receives
+class RowDeal:
+    def __init__(self, gathered, dealt, sends, receives, local):
         self.plane, self.mine = lax.axis_index("seq"), lax.axis_index("ctx")
-        origin = self.mine // 2
-        self.source = self.plane == origin
-        self.above, self.below = self.plane > origin, self.plane < origin
-        self.up = (self.source | self.above) & (self.plane + 1 < planes)
-        self.down = (self.source | self.below) & (self.plane > 0)
-
-    def copy(self, i, up):
-        place = jnp.clip(self.plane + 1 if up else self.plane - 1, 0, self.planes - 1)
-        at = (int(up), i)
-        block = self.target.at[i]
-        return remote(block, block, self.sends.at[at], self.receives.at[at], (place, self.mine))
-
-    def start(self, i):
-        for up, go in ((True, self.up), (False, self.down)):
-            @pl.when(self.source & go)
+        self.gathered, self.dealt, self.sends, self.receives, self.local = gathered, dealt, sends, receives, local
+
+    def out(self, s, back):
+        if back:
+            target = 4 * (self.mine % 2) + s
+            source, place = self.dealt.at[s], self.gathered.at[self.mine // 2]
+        else:
+            target = 2 * s + self.mine // 4
+            source, place = self.gathered.at[s], self.dealt.at[self.mine % 4]
+        slot = self.mine // 2 if back else self.mine % 4
+        copy = remote(source, place, self.sends.at[s], self.receives.at[slot], (self.plane, target))
+        keep = pltpu.make_async_copy(source, place, self.local)
+        return target == self.mine, copy, keep
+
+    def into(self, r, back):
+        if back:
+            origin = 2 * r + self.mine // 4
+            place = self.gathered.at[r]
+        else:
+            origin = 4 * (self.mine % 2) + r
+            place = self.dealt.at[r]
+        return origin == self.mine, remote(place, place, self.sends.at[r], self.receives.at[r], (self.plane, origin))
+
+    def start(self, back):
+        for s in range(4):
+            here, copy, keep = self.out(s, back)
+
+            @pl.when(here)
             def _():
-                self.copy(i, up).start()
-
-    def hand_on(self, i):
-        for up, got, go in ((True, self.above, self.up), (False, self.below, self.down)):
-            @pl.when(got)
+                keep.start()
+
+            @pl.when(jnp.logical_not(here))
             def _():
-                self.copy(i, up).wait_recv()
-
-            @pl.when(got & go)
+                copy.start()
+
+    def wait(self, back):
+        for s in range(4):
+            here, copy, keep = self.out(s, back)
+
+            @pl.when(here)
             def _():
-                self.copy(i, up).start()
-
-    def finish(self, i):
-        for up, go in ((True, self.up), (False, self.down)):
-            @pl.when(go)
+                keep.wait()
+
+            @pl.when(jnp.logical_not(here))
             def _():
-                self.copy(i, up).wait_send()
+                copy.wait_send()
+
+        for r in range(4):
+            here, copy = self.into(r, back)
+
+            @pl.when(jnp.logical_not(here))
+            def _():
+                copy.wait_recv()
 
 
 def enter_kernel(
-    planes, feed, qkv, out_w, gains, tokens, grads,
-    feed_out, qkv_out, out_w_out, gains_out, tokens_out, grads_out,
-    deal_sends, deal_receives, row_sends, row_receives, sends, receives,
-    line_sends, line_receives, relay_sends, relay_receives, local,
+    planes, q, k, v, gate, up, gains, tokens, out_w,
+    feed_out, qkv_out, gains_out, tokens_out, out_w_out,
+    q_near, k_near, v_near, gate_near, up_near, gains_near, packed, qkv, feed,
+    deal_sends, deal_receives, sends, receives, row_sends, row_receives, line_sends, line_receives, local,
 ):
     plane, mine = lax.axis_index("seq"), lax.axis_index("ctx")
+    loads = [
+        pltpu.make_async_copy(source, place, local.at[5 + i])
+        for i, (source, place) in enumerate(
+            ((gains, gains_near), (q, q_near), (k, k_near), (v, v_near), (gate, gate_near), (up, up_near))
+        )
+    ]
     keep = [
         pltpu.make_async_copy(qkv.at[mine], qkv_out.at[plane, mine], local.at[0]),
-        pltpu.make_async_copy(gains, gains_out.at[plane, mine], local.at[1]),
+        pltpu.make_async_copy(packed, gains_out.at[plane, mine], local.at[1]),
         pltpu.make_async_copy(feed.at[mine], feed_out.at[mine], local.at[2]),
         pltpu.make_async_copy(tokens, tokens_out.at[mine], local.at[3]),
-        pltpu.make_async_copy(grads, grads_out.at[mine], local.at[4]),
+        pltpu.make_async_copy(out_w, out_w_out.at[plane], local.at[4]),
     ]
-    for copy in keep:
+    for copy in loads + keep[3:]:
+        copy.start()
+    groups, _, three = qkv.shape
+    pair = three // 3
+    half = feed.shape[2] // 2
+    for copy in loads[:4]:
+        copy.wait()
+    packed[...] = jnp.zeros(packed.shape, F32)
+    packed[0:3, 0 : gains.shape[1]] = gains_near[...].astype(F32)
+    for c in range(groups):
+        for i, weight in enumerate((q_near, k_near, v_near)):
+            qkv[c, :, pair * i : pair * (i + 1)] = weight[:, pair * c : pair * (c + 1)]
+    for copy in keep[:2]:
         copy.start()
     greet(plane_peers(plane, range(1, 8)) + other_planes(plane, mine, planes))
-    qkv_copies = exchange_start(plane, mine, qkv, qkv_out.at[plane], deal_sends.at[0], deal_receives.at[0])
-    gain_copies = [
-        remote(gains, gains_out.at[plane, mine], deal_sends.at[1, d], deal_receives.at[1, d], (plane, peer(d)))
-        for d in (6, 7, 2, 3, 4, 5, 1)
-    ]
-    for copy in gain_copies:
+    first = exchange_start(plane, mine, qkv, qkv_out.at[plane], deal_sends.at[0], deal_receives.at[0])
+    for d in (6, 7, 2, 3, 4, 5, 1):
+        copy = remote(packed, gains_out.at[plane, mine], deal_sends.at[1, d], deal_receives.at[1, d], (plane, peer(d)))
         copy.start()
-    owner = 2 * plane + mine // 4
-    here = owner == mine
-    slot = mine % 4
-    send_rows = remote(out_w, out_w_out.at[slot], row_sends, row_receives.at[slot], (plane, owner))
-    keep_rows = pltpu.make_async_copy(out_w, out_w_out.at[slot], local.at[5])
-
-    @pl.when(here)
-    def _():
-        keep_rows.start()
-
-    @pl.when(jnp.logical_not(here))
-    def _():
-        send_rows.start()
-
-    copies = spread_start(plane, mine, tokens, tokens_out, sends.at[0], receives.at[0])
+        first.append(copy)
+    rows = Line([out_w], [out_w_out], planes, row_sends, row_receives)
+    rows.step(0)
+    for copy in loads[4:]:
+        copy.wait()
+    for c in range(groups):
+        for i, weight in enumerate((gate_near, up_near)):
+            for s in range(half // TILE):
+                at = TILE * (groups * s + c)
+                feed[c, :, half * i + TILE * s : half * i + TILE * (s + 1)] = weight[:, at : at + TILE]
+    keep[2].start()
     keep[0].wait()
-    for copy in qkv_copies:
-        copy.wait_recv()
     keep[1].wait()
-    for copy in gain_copies:
+    for copy in first:
         copy.wait_recv()
     line = Line(
         [qkv_out.at[plane], gains_out.at[plane]], [qkv_out, gains_out], planes, line_sends, line_receives
     )
     line.step(0)
-    relay = Relay(out_w_out, planes, relay_sends, relay_receives)
-
-    @pl.when(here)
-    def _():
-        keep_rows.wait()
-
-    for r in range(4):
-        @pl.when(relay.source & (4 * (mine % 2) + r != mine))
-        def _():
-            remote(out_w, out_w_out.at[r], row_sends, row_receives.at[r], (plane, owner)).wait_recv()
-
-        relay.start(r)
-    for d in (2, 4, 6):
-        spread_pass(plane, copies, d, tokens_out, sends.at[0], receives.at[0])
-    more = spread_start(plane, mine, grads, grads_out, sends.at[1], receives.at[1])
+    spread = Spread(tokens, tokens_out, sends, receives)
+    spread.start()
+    rows.step(1)
     line.step(1)
+    spread.near()
     deals = exchange_start(plane, mine, feed, feed_out, deal_sends.at[2], deal_receives.at[2])
-    spread_pass(plane, more, 2, grads_out, sends.at[1], receives.at[1])
-    spread_pass(plane, more, 4, grads_out, sends.at[1], receives.at[1])
-    for step in range(2, planes):
+    rows.step(2)
+    line.step(2)
+    spread.across()
+    for step in range(3, planes):
+        rows.step(step)
         line.step(step)
-        if step == 2:
-            relay.hand_on(0)
-            spread_pass(plane, more, 6, grads_out, sends.at[1], receives.at[1])
-    for i in range(1, 4):
-        relay.hand_on(i)
-    for i in range(4):
-        relay.finish(i)
-    spread_finish(copies)
-    spread_finish(more)
-    for copy in qkv_copies + gain_copies:
+    spread.finish()
+    for copy in first:
         copy.wait_send()
     for copy in deals:
         copy.wait()
-
-    @pl.when(jnp.logical_not(here))
-    def _():
-        send_rows.wait_send()
-
     for copy in keep[2:]:
         copy.wait()
     line.finish()
+    rows.finish()
+
+
+def heads_kernel(
+    planes, tokens, qkv, gains, out_w, grads, hidden, heads, gains_out, pair_gain, out_w_out, grads_out,
+    row_sends, row_receives, sends, receives, local,
+):
+    plane, mine = lax.axis_index("seq"), lax.axis_index("ctx")
+    keep = pltpu.make_async_copy(grads, grads_out.at[mine], local.at[1])
+    keep.start()
+    greet(plane_peers(plane, range(1, 8)))
+    spread = Spread(grads, grads_out, sends, receives)
+    spread.start()
+    deal = RowDeal(out_w, out_w_out, row_sends, row_receives, local.at[0])
+    deal.start(False)
+    groups = tokens.shape[0]
+    owned = out_w.shape[1]
+    for s in range(planes):
+        for c in range(groups):
+            at = owned * (groups * s + c)
+            gains_out[:, at : at + owned] = gains[s, c, :, 0:owned]
+    for r in range(4):
+        pair_gain[:, owned * r : owned * (r + 1)] = gains[mine // 2, 4 * (mine % 2) + r, :, 0:owned]
+    gain = gains_out[0:1, :]
+    for i in range(groups):
+        value = tokens[i].astype(F32)
+        low = (value * inverse_root(value) * gain).astype(BF16)
+        rows = pl.ds(value.shape[0] * i, value.shape[0])
+        hidden[:, rows] = low.T
+        heads[rows, :] = nn(low, qkv[...]).astype(BF16)
+        if i == groups // 2:
+            spread.near()
+    deal.wait(False)
+    spread.across()
+    spread.finish()
+    keep.wait()
 
 
 def inverse_root(values):
@@ -636,27 +721,27 @@
 
 
 def second_kernel(
-    planes, part, tokens, gain, feed, residual, spread_out, feed_out,
-    near, stage, far, rs_sends, rs_receives, sends, receives, line_sends, line_receives, local,
+    mixed, out_w, tokens, gains, residual, spread_out,
+    part, own, near, stage, far, hop, sum_sends, sum_receives, sends, receives,
 ):
     plane, mine = lax.axis_index("seq"), lax.axis_index("ctx")
-    keep = pltpu.make_async_copy(feed, feed_out.at[plane], local)
-    keep.start()
-    greet(plane_peers(plane, (1, 2, 4, 6)) + other_planes(plane, mine, planes))
-    copies = gather_sum_start(plane, part, near, rs_sends, rs_receives)
-    line = Line([feed], [feed_out], planes, line_sends, line_receives)
-    line.step(0)
-    gather_sum_pass(plane, copies, part, near, stage, far, rs_sends, rs_receives)
-    gather_sum_finish(copies)
-    line.step(1)
-    value = tokens[...].astype(F32) + gather_sum_total(mine, part, near, far)
+    greet(plane_peers(plane, (1, 2, 4)))
+    rows = PlaneSum(
+        terms_of(mixed, lambda left: nn(left, out_w[...])), part, own, near, stage, far, hop,
+        sum_sends, sum_receives,
+    )
+    rows.start()
+    rows.prepare()
+    rows.run()
+    value = tokens[...].astype(F32) + rows.total()
+    spread_out[mine] = (value * inverse_root(value) * gains[2:3, :]).astype(BF16)
+    spread = Spread(spread_out.at[mine], spread_out, sends, receives)
+    spread.start()
     residual[...] = value
-    spread_out[mine] = (value * inverse_root(value) * gain[...]).astype(BF16)
-    spread(plane, mine, spread_out, sends, receives)
-    for step in range(2, planes):
-        line.step(step)
-    keep.wait()
-    line.finish()
+    rows.finish()
+    spread.near()
+    spread.across()
+    spread.finish()
 
 
 def back_through_norm(upstream, values, gain):
@@ -667,18 +752,30 @@
     return grad, jnp.sum(upstream * normed, axis=0, keepdims=True)
 
 
-def back_kernel(part, residual, grads, gain, residual_grad, gain_grad, spread_out, near, stage, far, rs_sends, rs_receives, sends, receives):
+def back_kernel(
+    lows, feed, residual, grads, gains, residual_grad, gain_grad, spread_out,
+    part, own, near, stage, far, hop, sum_sends, sum_receives, sends, receives,
+):
     plane, mine = lax.axis_index("seq"), lax.axis_index("ctx")
-    greet(plane_peers(plane, (1, 2, 4, 6)))
-    copies = gather_sum_start(plane, part, near, rs_sends, rs_receives)
-    gather_sum_pass(plane, copies, part, near, stage, far, rs_sends, rs_receives)
-    gather_sum_finish(copies)
-    grad, gain_part = back_through_norm(gather_sum_total(mine, part, near, far), residual[...], gain[...])
+    greet(plane_peers(plane, (1, 2, 4)))
+    rows = PlaneSum(
+        terms_of(lows, lambda left: nt(left, feed[...])), part, own, near, stage, far, hop,
+        sum_sends, sum_receives,
+    )
+    rows.start()
+    rows.prepare()
+    rows.run()
+    grad, gain_part = back_through_norm(rows.total(), residual[...], gains[2:3, :])
     grad = grad + grads[...].astype(F32)
+    spread_out[mine] = grad.astype(BF16)
+    spread = Spread(spread_out.at[mine], spread_out, sends, receives)
+    spread.start()
     gain_grad[...] = gain_part
     residual_grad[...] = grad
-    spread_out[mine] = grad.astype(BF16)
-    spread(plane, mine, spread_out, sends, receives)
+    rows.finish()
+    spread.near()
+    spread.across()
+    spread.finish()
 
 
 class Fold:
@@ -739,51 +836,61 @@
 
 
 def leave_kernel(
-    planes, part, layer_part, residual, residual_grad, tokens, gain, small, qkv_grad, feed_grad, out_w_grad,
+    planes, qkv_low, qkv, hidden, active, down, residual, residual_grad, tokens, gains, small, feed_grad, out_w_grad,
     input_grad, layer_out, small_out, qkv_out, feed_out, out_w_out,
-    near, stage, far, layer_near, layer_stage, layer_far, small_plane, small_all,
-    fold_stage, fold_landed, qkv_sum, row_stage, row_landed, row_sum,
-    rs_sends, rs_receives, small_sends, small_receives, fold_sends, fold_receives, row_fold_sends, row_fold_receives,
-    deal_sends, deal_receives, row_sends, row_receives, local,
+    part, own, near, stage, far, hop, layer_part, layer_own, layer_near, layer_stage, layer_far, layer_hop, small_plane, small_all,
+    qkv_grad, fold_stage, fold_landed, qkv_sum, row_grad, row_stage, row_landed,
+    sum_sends, sum_receives, layer_sends, layer_receives, small_sends, small_receives,
+    fold_sends, fold_receives, row_fold_sends, row_fold_receives, deal_sends, deal_receives,
+    row_sends, row_receives, local,
 ):
     plane, mine = lax.axis_index("seq"), lax.axis_index("ctx")
     keep_feed = pltpu.make_async_copy(feed_grad.at[mine], feed_out.at[mine], local.at[0])
     keep_feed.start()
-    greet([((plane + dz) % planes, peer(d)) for dz in range(planes) for d in range(8) if dz or d])
+    greet(plane_peers(plane, range(1, 8)) + other_planes(plane, mine, planes))
+    row_deal = RowDeal(row_grad, out_w_grad, row_sends, row_receives, local.at[1])
+    row_deal.start(True)
+    rows = PlaneSum(
+        terms_of(qkv_low, lambda left: nt(left, qkv[...])), part, own, near, stage, far, hop,
+        sum_sends, sum_receives,
+    )
+    layer = PlaneSum(
+        terms_of(active, lambda left: nn(left, down[...])), layer_part, layer_own, layer_near, layer_stage, layer_far, layer_hop,
+        layer_sends, layer_receives,
+    )
     fold = Fold(qkv_grad, fold_stage, fold_landed, planes, fold_sends, fold_receives)
-    row_fold = Fold(out_w_grad, row_stage, row_landed, planes, row_fold_sends, row_fold_receives)
-    copies = gather_sum_start(plane, part, near, rs_sends.at[0], rs_receives.at[0])
-
+    row_fold = Fold(row_grad, row_stage, row_landed, planes, row_fold_sends, row_fold_receives)
     ends = (plane == 0) | (plane == planes - 1)
-
-    @pl.when(ends)
-    def _():
-        for i in range(planes - 1):
-            fold.round(i)
-            row_fold.round(i)
-
-    layer_copies = gather_sum_start(plane, layer_part, layer_near, rs_sends.at[1], rs_receives.at[1])
-    gather_sum_pass(plane, copies, part, near, stage, far, rs_sends.at[0], rs_receives.at[0])
-
-    @pl.when(jnp.logical_not(ends))
-    def _():
-        for i in range(2):
-            fold.round(i)
-            row_fold.round(i)
-
-    rows = exchange_start(plane, mine, feed_grad, feed_out, deal_sends.at[0], deal_receives.at[0])
-    gather_sum_pass(plane, layer_copies, layer_part, layer_near, layer_stage, layer_far, rs_sends.at[1], rs_receives.at[1])
-
-    @pl.when(jnp.logical_not(ends))
-    def _():
-        for i in range(2, planes - 1):
-            fold.round(i)
-            row_fold.round(i)
-
-    gather_sum_finish(copies)
-    grad, gain_part = back_through_norm(
-        gather_sum_total(mine, part, near, far), tokens[...].astype(F32), gain[...]
-    )
+    lows = qkv_low[...].reshape(hidden.shape[1], qkv_low.shape[3])
+    block = qkv_grad.shape[1]
+
+    def project(i):
+        j = jnp.where(plane < planes // 2, planes - 1 - i, i)
+        columns = hidden[pl.ds(pl.multiple_of(block * j, block), block), :]
+        qkv_grad[j] = nn(columns, lows).astype(BF16)
+
+    def rounds(which, outer, inner):
+        for here, i in ((ends, outer), (jnp.logical_not(ends), inner)):
+            if 0 <= i < planes - 1:
+                @pl.when(here)
+                def _():
+                    which.round(i)
+
+    rows.start()
+    project(0)
+    rounds(fold, 0, -1)
+    rows.prepare()
+    for i in range(1, planes):
+        project(i)
+    rounds(fold, 1, -1)
+    row_deal.wait(True)
+    rows.run()
+    deals = exchange_start(plane, mine, feed_grad, feed_out, deal_sends.at[0], deal_receives.at[0])
+    rounds(fold, 2, 0)
+    layer.start()
+    layer.prepare()
+    rounds(row_fold, 0, -1)
+    grad, gain_part = back_through_norm(rows.total(), tokens[...].astype(F32), gains[0:1, :])
     small_plane[mine] = small[...]
     small_plane[mine, 0:1, :] = gain_part
     near_copies = [
@@ -793,6 +900,10 @@
     for copy in near_copies:
         copy.start()
     input_grad[...] = (residual_grad[...] + grad).astype(BF16)
+    rounds(fold, -1, 1)
+    rounds(row_fold, 1, 0)
+    layer.run()
+    rounds(row_fold, 2, -1)
     for copy in near_copies:
         copy.wait()
     total = small_plane[0]
@@ -805,63 +916,69 @@
     ]
     for copy in far_copies:
         copy.start()
-    row_fold.total(row_sum)
-    owner_plane, owner = mine // 2, 4 * (mine % 2) + plane
-    here = (owner_plane == plane) & (owner == mine)
-    send_rows = remote(row_sum.at[0], out_w_out, row_sends, row_receives, (owner_plane, owner))
-    keep_rows = pltpu.make_async_copy(row_sum.at[0], out_w_out, local.at[1])
-
-    @pl.when(here)
-    def _():
-        keep_rows.start()
-
-    @pl.when(jnp.logical_not(here))
-    def _():
-        send_rows.start()
-
+    rounds(fold, -1, 2)
+    rounds(row_fold, -1, 1)
     fold.total(qkv_sum)
     keep_qkv = pltpu.make_async_copy(qkv_sum.at[mine], qkv_out.at[mine], local.at[2])
     keep_qkv.start()
-    rows += exchange_start(plane, mine, qkv_sum, qkv_out, deal_sends.at[1], deal_receives.at[1])
-    gather_sum_finish(layer_copies)
-    layer_out[...] = (residual[...] + gather_sum_total(mine, layer_part, layer_near, layer_far)).astype(BF16)
+    deals += exchange_start(plane, mine, qkv_sum, qkv_out, deal_sends.at[1], deal_receives.at[1])
+    rounds(row_fold, -1, 2)
+    row_fold.total(out_w_out)
+    layer_out[...] = (residual[...] + layer.total()).astype(BF16)
+    rows.finish()
+    layer.finish()
     for copy in far_copies:
         copy.wait()
     total = small_all[0]
     for i in range(1, planes):
         total = total + small_all[i]
     small_out[...] = total
-    for copy in rows:
+    for copy in deals:
         copy.wait()
-
-    @pl.when(here)
-    def _():
-        keep_rows.wait()
-
-    @pl.when(jnp.logical_not(here))
-    def _():
-        send_rows.wait()
-
     row_fold.finish()
     keep_feed.wait()
     keep_qkv.wait()
     fold.finish()
 
 
-def finish_kernel(qkv, feed, out_w, down, q_out, k_out, v_out, gate_out, up_out, out_w_out, down_out):
+def finish_kernel(count, *refs):
+    ins, outs = refs[:6], refs[6 : 6 + count]
+    near, made = refs[6 + count : 12 + count], refs[12 + count : 12 + 2 * count - 2]
+    loads, stores = refs[-2:]
+    moves = [pltpu.make_async_copy(ins[i], near[i], loads.at[i]) for i in range(6)]
+    for move in moves:
+        move.start()
+    qkv, feed, out_w, down, grad, layer = near
     groups, _, three = qkv.shape
     pair = three // 3
     half = feed.shape[2] // 2
-    planes = half // TILE
-    for c in range(groups):
-        for i, out in enumerate((q_out, k_out, v_out)):
-            out[:, pair * c : pair * (c + 1)] = qkv[c, :, pair * i : pair * (i + 1)].astype(F32)
-        for i, out in enumerate((gate_out, up_out)):
-            for s in range(planes):
+    results = list(made) + [grad, layer]
+    out = [pltpu.make_async_copy(results[i], outs[i], stores.at[i]) for i in range(count)]
+    moves[3].wait()
+    made[6][...] = down[...].astype(F32)
+    out[6].start()
+    moves[2].wait()
+    made[5][...] = out_w[0].astype(F32)
+    out[5].start()
+    for i in (4, 5):
+        moves[i].wait()
+        out[i + 3].start()
+    moves[1].wait()
+    for i in range(2):
+        for c in range(groups):
+            for s in range(half // TILE):
                 at = TILE * (groups * s + c)
-                out[:, at : at + TILE] = feed[c, :, half * i + TILE * s : half * i + TILE * (s + 1)].astype(F32)
-    out_w_out[...] = out_w[...].astype(F32)
-    down_out[...] = down[...].astype(F32)
+                made[3 + i][:, at : at + TILE] = feed[
+                    c, :, half * i + TILE * s : half * i + TILE * (s + 1)
+                ].astype(F32)
+        out[3 + i].start()
+    moves[0].wait()
+    for i in range(3):
+        for c in range(groups):
+            made[i][:, pair * c : pair * (c + 1)] = qkv[c, :, pair * i : pair * (i + 1)].astype(F32)
+        out[i].start()
+    for copy in out:
+        copy.wait()
 
 
 DMA = pltpu.SemaphoreType.DMA
@@ -878,14 +995,23 @@
         out_specs=out_specs or (spec,) * len(outs),
         scratch_shapes=scratch,
         compiler_params=pltpu.CompilerParams(
-            collective_id=number, has_side_effects=True, vmem_limit_bytes=48 << 20
+            collective_id=number, has_side_effects=True, vmem_limit_bytes=56 << 20
         ),
         cost_estimate=pl.CostEstimate(flops=0, transcendentals=0, bytes_accessed=micros * 3500000),
     )(*args)
 
 
-def sum_scratch(rows, width, count=1):
-    return [pltpu.VMEM((4, rows, width), BF16)] * (3 * count)
+def sum_scratch(rows, width):
+    return [
+        pltpu.VMEM((4, rows, width), BF16),
+        pltpu.VMEM((4, rows, width), F32),
+        pltpu.VMEM((4, rows, width), BF16),
+        pltpu.VMEM((4, rows, width), BF16),
+        pltpu.VMEM((2, rows, width), BF16),
+        pltpu.VMEM((2, rows // 2, width), BF16),
+        DMA((10,)),
+        DMA((10,)),
+    ]
 
 
 PRECISE = lax.Precision.HIGHEST
@@ -1436,44 +1562,50 @@
     tokens_low = inputs.reshape(micro * local, width)
     grads_low = out_grad.reshape(micro * local, width)
 
-    packed = jnp.pad(
-        jnp.stack([norm_gain, group_gain, second_gain]).astype(F32), ((0, 5), (0, TILE - owned))
-    )
-
-    def split_columns(weight):
-        return jnp.transpose(weight.reshape(owned, groups, pair), (1, 0, 2))
-
-    def split_hidden(weight):
-        return jnp.transpose(weight.reshape(owned, planes, groups, chunk), (2, 0, 1, 3)).reshape(
-            groups, owned, planes * chunk
-        )
-
-    qkv_send = jnp.concatenate(
-        [split_columns(query_weight), split_columns(key_weight), split_columns(value_weight)], axis=2
-    )
-    feed_send = jnp.concatenate([split_hidden(gate_weight), split_hidden(up_weight)], axis=2)
     rows_all = micro * local
-    feed_mine, qkv, out_rows, gains, all_tokens, all_grads = communicate(
-        functools.partial(enter_kernel, planes), "enter", 1, 60,
+    qkv_shape = (groups, owned, 3 * pair)
+    feed_shape = (groups, owned, 2 * planes * chunk)
+    gain_rows = jnp.stack([norm_gain, group_gain, second_gain])
+    spread_sems = [DMA((9,))] * 2
+    feed_mine, qkv, gains, all_tokens, out_rows = communicate(
+        functools.partial(enter_kernel, planes), "enter", 1, 50,
         [
-            (feed_send.shape, BF16),
-            ((planes,) + qkv_send.shape, BF16),
+            (feed_shape, BF16),
+            ((planes,) + qkv_shape, BF16),
+            ((planes, groups, 8, TILE), F32),
+            ((groups, rows_all, width), BF16),
+            ((planes, owned, width), BF16),
+        ],
+        [pltpu.VMEM((owned, width), BF16)] * 3 + [pltpu.VMEM((owned, hidden), BF16)] * 2
+        + [pltpu.VMEM((3, owned), BF16), pltpu.VMEM((8, TILE), F32)]
+        + [pltpu.VMEM(qkv_shape, BF16), pltpu.VMEM(feed_shape, BF16)]
+        + [DMA((3, groups))] * 2 + spread_sems + [DMA((1, 2, planes))] * 2
+        + [DMA((2, 2, planes))] * 2 + [DMA((11,))],
+        (
+            query_weight, key_weight, value_weight, gate_weight, up_weight, gain_rows, tokens_low,
+            output_weight,
+        ),
+        ANYWHERE,
+    )
+    all_tokens, down_mine = lax.optimization_barrier((all_tokens, down_weight))
+    feed = lax.all_gather(feed_mine.reshape(groups * owned, -1), "seq", axis=0, tiled=True)
+    down = lax.all_gather(down_mine, "seq", axis=0, tiled=True)
+    qkv = qkv.reshape(width, 3 * pair)
+    hidden_all, heads_in, gains, gain_pair, out_rows, all_grads = communicate(
+        functools.partial(heads_kernel, planes), "heads", 2, 20,
+        [
+            ((width, groups * rows_all), BF16),
+            ((groups * rows_all, 3 * pair), BF16),
+            ((8, width), F32),
+            ((8, pair), F32),
             ((4, owned, width), BF16),
-            ((planes, groups) + packed.shape, F32),
-            ((groups, rows_all, width), BF16),
             ((groups, rows_all, width), BF16),
         ],
-        [DMA((3, groups))] * 2 + [DMA, DMA((4,))] + [DMA((2, groups))] * 2
-        + [DMA((2, 2, planes))] * 2 + [DMA((2, 4))] * 2 + [DMA((6,))],
-        (feed_send, qkv_send, output_weight, packed, tokens_low, grads_low), ANYWHERE,
-    )
-    all_tokens, down_mine = lax.optimization_barrier((all_tokens.reshape(-1, width), down_weight))
+        [DMA((4,))] * 2 + spread_sems + [DMA((2,))],
+        (all_tokens, qkv, gains, out_rows, grads_low),
+        None, [ON_CHIP] * 3 + [ANYWHERE] * 2, (ON_CHIP,) * 4 + (ANYWHERE,) * 2,
+    )
     all_grads = all_grads.reshape(-1, width)
-    down = lax.all_gather(down_mine, "seq", axis=0, tiled=True)
-    gains = jnp.transpose(gains.reshape((groups * planes,) + packed.shape)[:, :3, :owned], (1, 0, 2))
-    gains = gains.reshape(3, width)
-    gain_first, gain_group, gain_second = gains[0:1], gains[1:2], gains[2:3]
-    qkv = qkv.reshape(width, 3 * pair)
     out_rows = out_rows.reshape(pair, width)
 
     slots = jnp.arange(blocks, dtype=jnp.int32)
@@ -1489,50 +1621,39 @@
     ).astype(jnp.int32)
     ker = lax.dynamic_slice_in_dim(score_kernel, 2 * me, 2, 0)
     mix = jnp.repeat(lax.dynamic_slice_in_dim(head_mixing, 2 * me, 2, 0), pair // 2, axis=0).T
-    gain_pair = lax.dynamic_slice_in_dim(gain_group, pair * me, pair, 1)
     scale = (width // heads) ** (-0.5)
 
-    normed_all, _ = normalize(all_tokens.astype(F32))
-    hidden_all = (normed_all * gain_first).astype(BF16)
-    heads_in = jnp.dot(hidden_all, qkv, preferred_element_type=F32).astype(BF16)
     mixed, y, prob = pair_forward(blk_table, ker, mix, gain_pair, heads_in, micro, seq, blk, scale)
-    attended = jnp.dot(mixed, out_rows, preferred_element_type=F32).astype(BF16)
-    sum_spec = sum_scratch(rows_all, width) + [DMA((groups,))] * 4
-    residual, second_all, feed = communicate(
-        functools.partial(second_kernel, planes), "second", 2, 50,
-        [
-            ((rows_all, width), F32),
-            ((groups, rows_all, width), BF16),
-            ((planes,) + feed_send.shape, BF16),
-        ],
-        sum_spec + [DMA((1, 2, planes))] * 2 + [DMA],
-        (attended.reshape(groups, rows_all, width), tokens_low, gain_second, feed_mine),
-        None, [ON_CHIP] * 3 + [ANYWHERE], (ON_CHIP, ON_CHIP, ANYWHERE),
-    )
-    feed = feed.reshape(width, -1)
+    by_core = (groups // 2, 2, rows_all)
+    sum_spec = sum_scratch(rows_all, width)
+    residual, second_all = communicate(
+        second_kernel, "second", 3, 40,
+        [((rows_all, width), F32), ((groups, rows_all, width), BF16)],
+        sum_spec + spread_sems,
+        (mixed.reshape(by_core + (pair,)), out_rows, tokens_low, gains), ON_CHIP,
+    )
     second_all = second_all.reshape(-1, width)
 
     half = planes * chunk
     both = jnp.dot(second_all, feed, preferred_element_type=F32)
     gate, up = both[:, :half], both[:, half:]
-    hid_grad = lax.dot_general(all_grads, down, (((1,), (1,)), ((), ())), preferred_element_type=F32)
     sigmoid = jax.nn.sigmoid(gate)
     active = (gate * sigmoid * up).astype(BF16)
+    down_grad = lax.dot_general(active, all_grads, (((0,), (0,)), ((), ())), preferred_element_type=F32)
+    all_grads, down_grad = lax.optimization_barrier((all_grads, down_grad.astype(BF16)))
+    hid_grad = lax.dot_general(all_grads, down, (((1,), (1,)), ((), ())), preferred_element_type=F32)
     up_low = (hid_grad * gate * sigmoid).astype(BF16)
     gate_low = (hid_grad * up * sigmoid * (1.0 + gate * (1.0 - sigmoid))).astype(BF16)
     lows = jnp.concatenate([gate_low, up_low], axis=1)
-    second_part = lax.dot_general(lows, feed, (((1,), (1,)), ((), ())), preferred_element_type=F32)
     feed_grad = lax.dot_general(second_all, lows, (((0,), (0,)), ((), ())), preferred_element_type=F32)
-    down_grad = lax.dot_general(active, all_grads, (((0,), (0,)), ((), ())), preferred_element_type=F32)
-    second_part, feed_grad, down_grad = lax.optimization_barrier(
-        (second_part.astype(BF16), feed_grad.astype(BF16), down_grad.astype(BF16))
-    )
-    layer_part = jnp.dot(active, down, preferred_element_type=F32)
+    lows, feed_grad = lax.optimization_barrier((lows, feed_grad.astype(BF16)))
+    feed_sum = lax.psum_scatter(feed_grad, "seq", scatter_dimension=0, tiled=True)
+    down_sum = lax.psum_scatter(down_grad, "seq", scatter_dimension=0, tiled=True)
     residual_grad, gain_second_grad, all_attended = communicate(
-        back_kernel, "back", 3, 45,
+        back_kernel, "back", 4, 40,
         [((rows_all, width), F32), ((1, width), F32), ((groups, rows_all, width), BF16)],
-        sum_spec,
-        (second_part.reshape(groups, rows_all, width), residual, grads_low, gain_second),
+        sum_spec + spread_sems,
+        (lows.reshape(by_core + (2 * half,)), feed, residual, grads_low, gains),
         ON_CHIP,
     )
     all_attended = all_attended.reshape(-1, width)
@@ -1542,11 +1663,10 @@
     out_w_grad = lax.dot_general(
         mixed, all_attended, (((0,), (0,)), ((), ())), preferred_element_type=F32
     )
+    mixed_grad, down_sum = lax.optimization_barrier((mixed_grad, down_sum))
     qkv_low, group_part, mix_part, ker_part = pair_backward(
         blk_table, ker, mix, gain_pair, heads_in, mixed_grad, y, prob, seq, blk, scale
     )
-    hidden_part = lax.dot_general(qkv_low, qkv, (((1,), (1,)), ((), ())), preferred_element_type=F32)
-    qkv_grad = lax.dot_general(hidden_all, qkv_low, (((0,), (0,)), ((), ())), preferred_element_type=F32)
     taps = score_kernel.shape[1] * score_kernel.shape[2]
     ker_mine = jnp.sum(ker_part, axis=2)[:, :taps]
     mix_mine = jnp.sum(mix_part.reshape(2, 2, pair // 2), axis=2).T
@@ -1561,44 +1681,52 @@
         [jnp.zeros((1, width), F32), gain_second_grad, group_all, mix_all, taps_all]
     )
     small = jnp.pad(small, ((0, -small.shape[0] % 8), (0, 0)))
-    down_sum = lax.psum_scatter(down_grad, "seq", scatter_dimension=0, tiled=True)
-    feed_sum = lax.psum_scatter(feed_grad, "seq", scatter_dimension=0, tiled=True)
     input_grad, layer_out, sums, qkv_back, feed_back, out_w_back = communicate(
-        functools.partial(leave_kernel, planes), "leave", 4, 60,
+        functools.partial(leave_kernel, planes), "leave", 5, 55,
         [
             ((rows_all, width), BF16),
             ((rows_all, width), BF16),
             (small.shape, F32),
-            (qkv_send.shape, BF16),
-            (feed_send.shape, BF16),
-            (output_weight.shape, BF16),
+            (qkv_shape, BF16),
+            (feed_shape, BF16),
+            ((1, owned, width), BF16),
         ],
-        sum_scratch(rows_all, width, 2)
+        sum_spec[:6] * 2
         + [pltpu.VMEM((groups,) + small.shape, F32), pltpu.VMEM((planes,) + small.shape, F32)]
+        + [pltpu.VMEM((planes, groups * owned, 3 * pair), BF16)]
         + [pltpu.VMEM((2, planes, groups * owned, 3 * pair), BF16)] * 2
-        + [pltpu.VMEM(qkv_send.shape, BF16)]
+        + [pltpu.VMEM(qkv_shape, BF16)]
+        + [pltpu.VMEM((planes, owned, width), BF16)]
         + [pltpu.VMEM((2, planes, owned, width), BF16)] * 2
-        + [pltpu.VMEM((1, owned, width), BF16)]
-        + [DMA((2, groups))] * 4
+        + sum_spec[6:] * 2
+        + [DMA((2, groups))] * 2
         + [DMA((2, planes))] * 4
         + [DMA((2, groups))] * 2
-        + [DMA, DMA, DMA((3,))],
+        + [DMA((4,))] * 2 + [DMA((3,))],
         (
-            hidden_part.astype(BF16).reshape(groups, rows_all, width),
-            layer_part.astype(BF16).reshape(groups, rows_all, width),
-            residual, residual_grad, tokens_low, gain_first, small,
-            qkv_grad.astype(BF16).reshape(planes, groups * owned, 3 * pair),
-            feed_sum.reshape(feed_send.shape), out_w_grad.astype(BF16).reshape(planes, owned, width),
+            qkv_low.reshape(by_core + (3 * pair,)), qkv, hidden_all,
+            active.reshape(by_core + (half,)), down,
+            residual, residual_grad, tokens_low, gains, small,
+            feed_sum.reshape(feed_shape),
+            out_w_grad.astype(BF16).reshape(4, owned, width),
         ),
-        None, [ON_CHIP] * 8 + [ANYWHERE, ON_CHIP], (ON_CHIP,) * 3 + (ANYWHERE,) * 3,
+        None, [ON_CHIP] * 10 + [ANYWHERE] * 2, (ON_CHIP,) * 3 + (ANYWHERE,) * 2 + (ON_CHIP,),
     )
     plain = [(owned, width)] * 3 + [(owned, hidden)] * 2 + [(owned, width), (chunk, width)]
-    q_back, k_back, v_back, gate_back, up_back, out_w_out, down_out = pl.pallas_call(
-        finish_kernel,
+    landed = (qkv_back, feed_back, out_w_back, down_sum, input_grad, layer_out)
+    out_shapes = [jax.ShapeDtypeStruct(shape, F32) for shape in plain]
+    out_shapes += [jax.ShapeDtypeStruct((rows_all, width), BF16)] * 2
+    q_back, k_back, v_back, gate_back, up_back, out_w_out, down_out, input_grad, layer_out = pl.pallas_call(
+        functools.partial(finish_kernel, len(out_shapes)),
         name="finish",
-        out_shape=tuple(jax.ShapeDtypeStruct(shape, F32) for shape in plain),
+        out_shape=tuple(out_shapes),
+        in_specs=[ANYWHERE] * 6,
+        out_specs=(ANYWHERE,) * len(out_shapes),
+        scratch_shapes=[pltpu.VMEM(value.shape, BF16) for value in landed]
+        + [pltpu.VMEM(shape, F32) for shape in plain]
+        + [DMA((6,)), DMA((len(out_shapes),))],
         compiler_params=pltpu.CompilerParams(vmem_limit_bytes=32 << 20),
-    )(qkv_back, feed_back, out_w_back, down_sum)
+    )(*landed)
 
     at = (lax.axis_index("seq") * groups + me) * owned
     gain_outs = [lax.dynamic_slice_in_dim(sums[i], at, owned, 0) for i in range(3)]

time: 443 us -> 379 us (0.86)
  matrix products: 57.8 us -> 25.9 us
  Pallas kernels: 327 us -> 297 us
  local copies, waits for them, and re-layouts: 33.9 us -> 19.6 us
  waiting for transfers between devices: 0.05 us -> 10.1 us
    pallas_call x4 -> x5, Pallas kernels: 286 us -> 255 us  [communicate(): pl.pallas_call(kernel, name=name, out_shape=tuple((jax.ShapeDtypeStruct(s...]
    dot_general x6 -> x0, matrix products: 30.5 us -> none  [the longest x1 7.91 us: on_device(): lax.dot_general(lows, feed, (((1,), (1,)), ((), ())), preferred_element_t...]
    unnamed x80 -> x37, local copies, waits for them, and re-layouts: 20 us -> 11.3 us
    reduce_scatter x1, waiting for transfers between devices: 0.01 us -> 8.44 us  [on_device(): lax.psum_scatter(feed_grad, 'seq', scatter_dimension=0, tiled=True)]
    convert_element_type x2 -> x0, local copies, waits for them, and re-layouts: 4.99 us -> none  [the longest x1 3.99 us: on_device(): qkv_grad.astype(BF16).reshape(planes, groups * owned, 3 * pair)]
  transfers between devices with their start and end apart: 3 -> 4, of which waited for: 0 -> 2; matrix products, arithmetic and copies ran while one was open for 11% -> 9% of each run, Pallas kernels for 58% -> 40%
where the time goes in v3:
time: 379 us; the launch traced here: 373 us
  Pallas kernels  297 us (78%)
  matrix products  25.9 us (7%)
  local copies, waits for them, and re-layouts  19.6 us (5%)
  between operations  14.5 us (4%)
  waiting for transfers between devices  10.1 us (3%)
  other arithmetic  5.49 us (1%)
    pallas_call x5, Pallas kernels, communicate(): pl.pallas_call(kernel, name=name, out_shape=tuple((jax.ShapeDtypeStruct(s...  255 us
    pallas_call x1, Pallas kernels, pair_backward(): pl.pallas_call(functools.partial(backward_kernel, seq, blk, rows_tap, key...  24.1 us
    pallas_call x1, Pallas kernels, pair_forward(): pl.pallas_call(functools.partial(forward_kernel, seq, blk, rows_tap, keys...  14.6 us
    unnamed x37, local copies, waits for them, and re-layouts  11.3 us
    reduce_scatter x1, waiting for transfers between devices, on_device(): lax.psum_scatter(feed_grad, 'seq', scatter_dimension=0, tiled=True)  8.44 us
  transfers between devices with their start and end apart: 4, of which 2 were waited for; matrix products, arithmetic and copies ran while one was open for 9% of the time, Pallas kernels for 40%

profile of v3, /device:TPU:9, one launch (start us, length us, event | category | flops | bytes accessed | tf_op | source)
XLA Modules:
  0.0 373.4 jit_solution(13938223624487932827)
XLA Ops:
  7.3 1.3 pad_maximum_fusion.1.gains
  8.5 54.1 %enter.1 = (bf16[8,48,1024]{2,1,0:T(8,128)(2,1)}, bf16[4,8,48,576]{3,2,1,0:T(8,128)(2,1)}, f32[4,8,8,128]{3,2,1,0:T(8,128)}, bf16[8,128,1536]{2,1,0:T(8,128)(2,1)}, bf16[4,48,1536]{2,1,0:T(8,128)(2,1)}) custom-call(bf16[48,1536]{1,0:T(8,128)(2,1)} %q.1, bf16[48,1536]{1,0:T(8,128)(2,1)} %k.1, bf16[48,1536]{1,0:T(8,128)(2,1)} %v.1, bf16[48,4096]{1,0:T(8,128)(2,1)} %gate.1, ...), custom_call_target="tpu_custom_call" | custom-call | bytes 175000000 | tf_op jit(solution)/shard_map/enter/pallas_call | solution.py:990
  62.7 0.7 all-gather.5.cloned.1.call-update
  63.6 0.7 copy.65.ker_ref
  64.5 0.7 reshape.183
  65.4 0.7 select_reduce_fusion.blk_ref
  66.0 29.6 %heads.1 = (bf16[1536,1024]{1,0:T(8,128)(2,1)}, bf16[1024,576]{1,0:T(8,128)(2,1)}, f32[8,1536]{1,0:T(8,128)}, f32[8,192]{1,0:T(8,128)}, bf16[4,48,1536]{2,1,0:T(8,128)(2,1)}, /*index=5*/bf16[8,128,1536]{2,1,0:T(8,128)(2,1)}) custom-call(bf16[8,128,1536]{2,1,0:T(8,128)(2,1)} %get-tuple-element.61.tokens, bf16[1536,576]{1,0:T(8,128)(2,1)} %bitcast.45, ...), custom_call_target="tpu_custom_call" | custom-call | bytes 70000000 | tf_op jit(solution)/shard_map/heads/pallas_call | solution.py:990
  95.7 14.6 %pair_forward.1 = (bf16[1024,192]{1,0:T(8,128)(2,1)}, f32[2,2,512,192]{3,2,1,0:T(8,128)}, bf16[2,2,512,512]{3,2,1,0:T(8,128)(2,1)}) custom-call(s32[2,16]{1,0:T(2,128)} %select_reduce_fusion.blk_ref, f32[2,6,11]{2,1,0:T(8,128)} %copy.65.ker_ref, f32[2,192]{1,0:T(2,128)} %bitcast.63, f32[8,192]{1,0:T(8,128)} %get-tuple-element.65.gain_ref, ...), custom_call_target="tpu_custom_call" | custom-call | flops 20000000000 | bytes 8388608 | tf_op jit(solution)/shard_map/pair_forward/pallas_call | solution.py:273
  110.3 38.7 %second.1 = (f32[128,1536]{1,0:T(8,128)}, bf16[8,128,1536]{2,1,0:T(8,128)(2,1)}) custom-call(bf16[4,2,128,192]{3,2,1,0:T(8,128)(2,1)} %bitcast.54, bf16[192,1536]{1,0:T(8,128)(2,1)} %bitcast.60, bf16[128,1536]{1,0:T(8,128)(2,1)} %bitcast.49, f32[8,1536]{1,0:T(8,128)} %get-tuple-element.70.gains), custom_call_target="tpu_custom_call" | custom-call | bytes 140000000 | tf_op jit(solution)/shard_map/second/pallas_call | solution.py:990
  149.1 6.3 %fusion.5 = f32[1024,1024]{1,0:T(8,128)S(1)} fusion(bf16[1024,1536]{1,0:T(8,128)(2,1)} %bitcast.70, bf16[1536,1024]{1,0:T(8,128)(2,1)} %all-gather.3.cloned.1.call-done.feed), kind=kOutput, calls=%fused_computation.35 | convolution fusion | flops 3221225472 | bytes 10485760 | tf_op jit(solution)/shard_map/dot_general | solution.py:1638
  155.4 0.7 multiply_convert_fusion.2
  156.1 1.4 copy-done.8
  157.5 1.7 copy-done.15
  159.1 3.0 convolution_convert_fusion.1
  162.1 0.2 reduce-scatter.5.cloned.1.call-start
  162.4 0.9 all-gather.5.cloned.1.call-done.down
  163.2 6.1 %multiply_convert_fusion.1 = (bf16[1024,512]{1,0:T(8,128)(2,1)S(1)}, bf16[1024,512]{1,0:T(8,128)(2,1)S(1)}) fusion(f32[1024,1024]{1,0:T(8,128)} %copy-done.8, bf16[1024,1536]{1,0:T(8,128)(2,1)} %bitcast.68, bf16[512,1536]{1,0:T(8,128)(2,1)} %all-gather.5.cloned.1.call-done.down), kind=kOutput, calls=%fused_computation.5 | convolution fusion | flops 1617428480 | bytes 11010048 | tf_op jit(solution)/shard_map/dot_general | solution.py:1644
  169.3 1.7 pad_maximum_fusion
  171.0 1.0 copy-done.16
  172.0 5.1 %convolution_convert_fusion = bf16[1536,1024]{1,0:T(8,128)(2,1)} fusion(bf16[1024,1536]{1,0:T(8,128)(2,1)S(1)} %bitcast.71, bf16[1024,512]{1,0:T(8,128)(2,1)S(1)} %get-tuple-element.163, bf16[1024,512]{1,0:T(8,128)(2,1)S(1)} %get-tuple-element.162), kind=kOutput, calls=%fused_computation | convolution fusion | flops 3226992640 | bytes 8388608 | tf_op jit(solution)/shard_map/dot_general | solution.py:1648
  177.1 42.7 %back.1 = (f32[128,1536]{1,0:T(8,128)}, f32[1,1536]{1,0:T(1,128)}, bf16[8,128,1536]{2,1,0:T(8,128)(2,1)}) custom-call(bf16[4,2,128,1024]{3,2,1,0:T(8,128)(2,1)} %bitcast.44, bf16[1536,1024]{1,0:T(8,128)(2,1)} %all-gather.3.cloned.1.call-done.feed, f32[128,1536]{1,0:T(8,128)} %get-tuple-element.76.residual, bf16[128,1536]{1,0:T(8,128)(2,1)} %bitcast.56, ...), custom_call_target="tpu_custom_call" | custom-call | bytes 140000000 | tf_op jit(solution)/shard_map/back/pallas_call | solution.py:990
  219.9 3.7 convolution_convert_fusion.2
  223.5 1.8 convolution_convert_fusion.3.zg_ref
  225.3 24.1 %pair_backward.1 = (bf16[1024,576]{1,0:T(8,128)(2,1)}, f32[1,192]{1,0:T(1,128)}, f32[2,192]{1,0:T(2,128)}, f32[2,72,128]{2,1,0:T(8,128)}) custom-call(s32[2,16]{1,0:T(2,128)} %select_reduce_fusion.blk_ref, f32[2,6,11]{2,1,0:T(8,128)} %copy.65.ker_ref, f32[2,192]{1,0:T(2,128)} %bitcast.64, f32[8,192]{1,0:T(8,128)} %get-tuple-element.65.gain_ref, ...), custom_call_target="tpu_custom_call" | custom-call | flops 30000001024 | bytes 12582912 | tf_op jit(solution)/shard_map/pair_backward/pallas_call | solution.py:309
  249.4 1.0 reduce_sum.29
  250.4 0.1 reshape.198
  250.5 0.8 reshape.196
  251.3 0.1 reduce_sum.28
  251.4 0.1 copy.58
  251.6 1.1 dynamic_update_slice.9
  252.8 0.6 pad.14.small
  253.5 8.4 %reduce-scatter.5.cloned.1.call-done = bf16[384,1024]{1,0:T(8,128)(2,1)} async-done(((bf16[1536,1024]{1,0:T(8,128)(2,1)}), bf16[384,1024]{1,0:T(8,128)(2,1)}) %reduce-scatter.5.cloned.1.call-update) | async-done | bytes 786448 | tf_op jit(solution)/shard_map/reduce_scatter | solution.py:1650
  261.9 90.3 %leave.1 = (bf16[128,1536]{1,0:T(8,128)(2,1)}, bf16[128,1536]{1,0:T(8,128)(2,1)}, f32[8,1536]{1,0:T(8,128)}, bf16[8,48,576]{2,1,0:T(8,128)(2,1)}, bf16[8,48,1024...) custom-call(bf16[4,2,128,576]{3,2,1,0:T(8,128)(2,1)} %bitcast.57, bf16[1536,576]{1,0:T(8,128)(2,1)} %bitcast.46, ...), custom_call_target="tpu_custom_call" | custom-call | bytes 192500000 | tf_op jit(solution)/shard_map/leave/pallas_call | solution.py:990
  352.2 0.8 slice_reduce_fusion
  353.0 0.9 fusion.4
  353.9 0.7 slice_reduce_fusion.1
  354.6 0.2 reshape.203
  354.8 0.8 copy.61
  355.5 0.6 fusion
  356.1 0.6 fusion.1
  356.7 0.6 fusion.2
  357.4 0.6 copy.62
  358.0 1.1 copy-done.1
  359.1 1.0 copy-done.2
  360.2 1.0 copy-done.4
  361.2 1.0 copy-done.5
  362.2 0.9 copy-done.6
  363.1 3.3 finish.1
  (55 shorter events, 1.0 us)
Async XLA Ops:
  7.2 56.3 %copy-start = (f32[16,6,11]{0,1,2:T(8,128)S(1)}, f32[16,6,11]{0,1,2:T(8,128)}, u32[]{:S(2)}) copy-start(f32[16,6,11]{0,1,2:T(8,128)} %param.22) | copy-start | bytes 12676
  7.2 57.1 %copy-start.14 = (f32[16,2]{0,1:T(2,128)S(1)}, f32[16,2]{0,1:T(2,128)}, u32[]{:S(2)}) copy-start(f32[16,2]{0,1:T(2,128)} %param.23) | copy-start | bytes 388
  7.2 57.9 %copy-start.13 = (s32[2,8]{1,0:T(2,128)S(1)}, s32[2,8]{1,0:T(2,128)}, u32[]{:S(2)}) copy-start(s32[2,8]{1,0:T(2,128)} %param.17) | copy-start | bytes 196
  7.2 141.8 %all-gather.3.cloned.1.call-start = ((), (), s32[]{:S(2)}) async-start(), calls=%async_computation.2 | async-start | bytes 3932160 | tf_op jit(solution)/shard_map/all_gather | solution.py:1591
  62.6 100.6 %all-gather.5.cloned.1.call-start = ((), (), s32[]{:S(2)}) async-start(), calls=%async_computation.3 | async-start | bytes 1966080 | tf_op jit(solution)/shard_map/all_gather | solution.py:1592
  63.4 161.9 %reduce-scatter.3.cloned.1.call-start = ((), (), s32[]{:S(2)}) async-start(), calls=%async_computation.4 | async-start | bytes 1966080 | tf_op jit(solution)/shard_map/reduce_scatter | solution.py:1651
  155.3 2.1 copy-start.8
  155.3 3.8 %copy-start.15 = (bf16[8,128,1536]{2,1,0:T(8,128)(2,1)S(1)}, bf16[8,128,1536]{2,1,0:T(8,128)(2,1)}, u32[]{:S(2)}) copy-start(bf16[8,128,1536]{2,1,0:T(8,128)(2,1)} %get-tuple-element.67) | copy-start | bytes 9437188
  157.5 4.6 %copy-start.7 = (bf16[1024,512]{1,0:T(8,128)(2,1)}, bf16[1024,512]{1,0:T(8,128)(2,1)S(1)}, u32[]{:S(2)}) copy-start(bf16[1024,512]{1,0:T(8,128)(2,1)S(1)} %multiply_convert_fusion.2) | copy-start | bytes 3145732
  162.1 99.8 %reduce-scatter.5.cloned.1.call-start = ((), (), s32[]{:S(2)}) async-start(), calls=%async_computation.5 | async-start | bytes 3932160 | tf_op jit(solution)/shard_map/reduce_scatter | solution.py:1650
  169.3 2.6 copy-start.16
  177.1 42.7 %copy-start.10 = (bf16[1024,192]{1,0:T(8,128)(2,1)S(1)}, bf16[1024,192]{1,0:T(8,128)(2,1)}, u32[]{:S(2)}) copy-start(bf16[1024,192]{1,0:T(8,128)(2,1)} %get-tuple-element.68) | copy-start | bytes 1179652
  219.8 3.7 copy-start.9
  219.8 3.7 copy-start.11
  225.3 27.5 %copy-start.12 = (f32[1,1536]{1,0:T(1,128)S(1)}, f32[1,1536]{1,0:T(1,128)}, u32[]{:S(2)}) copy-start(f32[1,1536]{1,0:T(1,128)} %get-tuple-element.85) | copy-start | bytes 18436
  261.9 96.1 %copy-start.3 = (bf16[128,1536]{1,0:T(8,128)(2,1)S(1)}, bf16[128,1536]{1,0:T(8,128)(2,1)}, u32[]{:S(2)}) copy-start(bf16[128,1536]{1,0:T(8,128)(2,1)} %reduce-scatter.3.cloned.1.call-done.refs_3_) | copy-start | bytes 1179652
  358.0 1.1 copy-start.1
  359.1 1.0 copy-start.2
  360.2 1.0 copy-start.4
  361.2 1.0 copy-start.5
  362.2 0.9 copy-start.6
Sparse Core Ops, SparseCore 0:
  62.8 61.8 all-gather.2
  126.2 36.9 all-gather.4
  165.5 33.4 reduce-scatter.2
  201.2 60.6 reduce-scatter.4
